TPU v7x, 32 devices: a whole 2x2x4 slice. The times are simulated.
32 devices in a mesh: shard: 4 (over y, x), replica: 8 (over z, core).
Axes of the slice: x: 2, y: 2, z: 4, core: 2. Of those that a mesh axis runs over, the one named last changes fastest.
Arguments:
- tokens: bfloat16 [4096, 896], P(('shard', 'replica')), may hold values from -6 to 6
- seg_ids: int32 [32, 128], P(('shard', 'replica')), may hold values from 0 to 7, never falling along the last dimension, each value on 1 to 64 neighbouring positions
- norm1_gain: bfloat16 [896], P('shard'), may hold values from 0.25 to 1.75
- w_qkv: bfloat16 [896, 1152], P('shard'), may hold values from -0.1875 to 0.1875
- b_qkv: bfloat16 [1152], P('shard'), may hold values from -3 to 3
- w_out: bfloat16 [896, 896], P('shard'), may hold values from -0.75 to 0.75
- norm2_gain: bfloat16 [896], P('shard'), may hold values from 0.25 to 1.75
- w_gate: bfloat16 [896, 4864], P('shard'), may hold values from -0.1875 to 0.1875
- w_up: bfloat16 [896, 4864], P('shard'), may hold values from -0.1875 to 0.1875
- w_down: bfloat16 [4864, 896], P('shard'), may hold values from -0.15625 to 0.15625
- cotangent: bfloat16 [4096, 896], P(('shard', 'replica')), may hold values from -6 to 6
Outputs:
- layer_out: bfloat16 [4096, 896], P(('shard', 'replica'))
- grad_tokens: float32 [4096, 896], P(('shard', 'replica'))
- grad_norm1: float32 [896], P('shard')
- grad_qkv: float32 [896, 1152], P('shard')
- grad_bias: float32 [1152], P('shard')
- grad_out: float32 [896, 896], P('shard')
- grad_norm2: float32 [896], P('shard')
- grad_gate: float32 [896, 4864], P('shard')
- grad_up: float32 [896, 4864], P('shard')
- grad_down: float32 [4864, 896], P('shard')
Inputs may be any that keep to these rules, and one draw needn't show every extreme that they name: `seg_ids`: within a row, ids never fall; each document has 1 to 64 tokens and one has exactly 64.
All inputs are finite; a program needn't handle non-finite values.
Results may differ from a plain program's by a relative error of at most 0.01.
Values may be sent and summed in bfloat16 or wider, within the bound.
No kernel may reach another device: no remote copies, remote signals or barrier semaphores. Data moves between devices by JAX's collectives and lax.ppermute only.
A program may use at most 256 MiB of HBM per device.

v0:
```python
import functools
import math
import jax
import jax.numpy as jnp
from jax import lax
from jax.experimental import pallas as pl
from jax.experimental.pallas import tpu as pltpu
from jax.sharding import PartitionSpec as P


QUERY_HEADS = 14
KEY_VALUE_HEADS = 2
HEAD_SIZE = 64
HALF = HEAD_SIZE // 2
GROUP = QUERY_HEADS // KEY_VALUE_HEADS
PAIRS = QUERY_HEADS // 2
LANES = 128

EPS = 1e-06
THETA = 1000000.0
SCALE = HEAD_SIZE ** (-0.5)
BF = jnp.bfloat16
F32 = jnp.float32


def swap_core(x):
    n = lax.axis_size("replica")
    return lax.ppermute(x, "replica", [(i, i ^ 1) for i in range(n)])


def shard_swap(x, k):
    n = lax.axis_size("shard")
    return lax.ppermute(x, "shard", [(i, i ^ k) for i in range(n)])


def pair_swap(x):
    n = lax.axis_size("replica")
    return lax.ppermute(x, "replica", [(i, i ^ 2) for i in range(n)])


def spread(x):
    return [x] + [shard_swap(x, k) for k in range(1, lax.axis_size("shard"))]


def line_sum(where, x):
    line = lax.axis_size("replica") // 2
    half = line // 2

    def hop(value, chips):
        links = [(2 * a + k, 2 * b + k) for a, b in chips for k in range(2)]
        return lax.ppermute(value, "replica", links)

    total = x
    for i in range(half - 1):
        arrived = hop(total, [(i, i + 1), (line - 1 - i, line - 2 - i)])
        total = total + arrived
    arrived = hop(total, [(half - 1, half), (half, half - 1)])
    total = total + arrived
    for i in reversed(range(half - 1)):
        arrived = hop(total, [(i + 1, i), (line - 2 - i, line - 1 - i)])
        total = pick(where, total, arrived, i, line - 1 - i)
    return total


def dot(a, b):
    return jnp.dot(a, b, preferred_element_type=F32)


def dot_t(a, b):
    return lax.dot_general(a, b, (((1,), (1,)), ((), ())), preferred_element_type=F32)


def t_dot(a, b):
    return lax.dot_general(a, b, (((0,), (0,)), ((), ())), preferred_element_type=F32)


GRANTS = {'pack': 12, 'attend': 3, 'mix': 4, 'down_back': 5, 'feed': 9, 'narrow': 4, 'back': 18, 'wide': 8, 'merge': 5, 'finish': 4, 'lay': 18, 'close': 6, 'ydown': 4, 'yout': 4, 'pick': 4, 'stack': 8}


def call(kernel, name, outs, where, args, scratch=(), flops=0, space=pltpu.VMEM):
    grant = GRANTS[name]
    total = sum(a.size * a.dtype.itemsize for a in args)
    total += sum(o.size * jnp.dtype(o.dtype).itemsize for o in outs)
    vmem = pl.BlockSpec(memory_space=pltpu.VMEM)
    return pl.pallas_call(
        kernel,
        out_shape=outs,
        in_specs=[pl.BlockSpec(memory_space=pltpu.SMEM)] + [pl.BlockSpec(memory_space=space)] * len(args),
        out_specs=[vmem] * len(outs),
        scratch_shapes=list(scratch),
        cost_estimate=pl.CostEstimate(flops=flops, bytes_accessed=total, transcendentals=0),
        compiler_params=pltpu.CompilerParams(vmem_limit_bytes=grant << 20),
    )(where, *args)


def shape(dims, dtype=BF):
    return jax.ShapeDtypeStruct(dims, dtype)


def rows_at(start, size):
    return pl.ds(pl.multiple_of(start, 8 if size % 16 else 16), size)


def pack_kernel(shards, where, gate, up, *rest):
    outs, (stage, gate_buf, up_buf, sems) = rest[:shards], rest[shards:]
    rows, slab = gate.shape[0], stage.shape[3]
    step = rows // 2
    s, c = where[0], where[1]
    copies = []
    for i in range(2):
        at = pl.ds(i * step, step)
        for m, (src, dst) in enumerate(((gate, gate_buf), (up, up_buf))):
            copy = pltpu.make_async_copy(src.at[at], dst.at[at], sems.at[i, m])
            copy.start()
            copies.append(copy)
    for i in range(2):
        for m, buf in enumerate((gate_buf, up_buf)):
            copies[2 * i + m].wait()
            for j in range(2 * shards):

                @pl.when(c == j % 2)
                def _(i=i, j=j, m=m, buf=buf):
                    at = slice(i * step, (i + 1) * step)
                    stage[(j // 2) ^ s, m, at] = buf[at, j * slab : (j + 1) * slab]

    outs[0][:rows] = stage[0, 0]
    outs[0][rows:] = stage[0, 1]
    for k in range(1, shards):
        outs[k][...] = stage[k, where[2] & 1]


def pack(where, gate, up, shards):
    rows, ff = gate.shape
    slab = ff // (2 * shards)
    outs = [shape((2 * rows, slab))] + [shape((rows, slab))] * (shards - 1)
    return call(
        functools.partial(pack_kernel, shards), "pack", outs, where, [gate, up],
        [
            pltpu.VMEM((shards, 2, rows, slab), BF), pltpu.VMEM((rows, ff), BF),
            pltpu.VMEM((rows, ff), BF), pltpu.SemaphoreType.DMA((2, 2)),
        ],
        space=pltpu.HBM,
    )


def place_rows(dst, s, c, own, mine, other):
    rows = own.shape[0]
    half = rows // 2
    dst[rows_at(s * rows, rows)] = own[...]
    for k in range(1, len(mine) + 1):
        base = (s ^ k) * rows
        dst[rows_at(base + c * half, half)] = mine[k - 1][:half]
        dst[rows_at(base + (1 - c) * half, half)] = other[k - 1][:half]


def lane_kinds(x):
    lane = lax.broadcasted_iota(jnp.int32, x.shape, 1)
    low = lane < HEAD_SIZE
    zero = jnp.zeros_like(x)
    turned = pltpu.roll(x, HEAD_SIZE, 1)
    return [
        [jnp.where(low, x, zero), jnp.where(low, zero, turned)],
        [jnp.where(low, turned, zero), jnp.where(low, zero, x)],
    ]


def swap_halves(x):
    lane = lax.broadcasted_iota(jnp.int32, x.shape, 1)
    first = (lane % HEAD_SIZE) < HALF
    return jnp.where(first, pltpu.roll(x, LANES - HALF, 1), pltpu.roll(x, HALF, 1))


def attend_kernel(shards, where, x, seg, own, extra, *rest):
    n = shards - 1
    vectors, mine, other = rest[:n], rest[n : 2 * n], rest[2 * n : 3 * n]
    n1_ref, q_ref, k_ref, v_ref, p_ref, o_ref, w_ref, vec_ref, cos_ref, sin_ref = rest[3 * n :]
    s, c = where[0], where[1]
    width, joined_width = x.shape[1], own.shape[1]
    place_rows(w_ref, s, c, own, mine, other)
    is_gain = lax.broadcasted_iota(jnp.int32, extra.shape, 0) < 2
    vec = jnp.zeros(extra.shape, F32)
    for k, piece in enumerate((extra,) + tuple(vectors)):
        value = piece[...].astype(F32)
        gains = pltpu.roll(value, (s ^ k) * (width // shards), 1)
        biases = pltpu.roll(value, (s ^ k) * (joined_width // shards), 1)
        vec = vec + jnp.where(is_gain, gains, biases)
    vec_ref[...] = vec
    xf = x[...].astype(F32)
    root = lax.rsqrt(jnp.mean(xf * xf, axis=1, keepdims=True) + EPS)
    n1 = (xf * root * vec[0:1, :width]).astype(BF)
    n1_ref[...] = n1
    joined = dot(n1, w_ref[...]) + vec[2:3]
    tokens = x.shape[0]
    square = (tokens, LANES)
    down = lax.broadcasted_iota(jnp.int32, square, 0)
    along = lax.broadcasted_iota(jnp.int32, square, 1)
    of_key = jnp.broadcast_to(seg[...], square).astype(F32)
    of_query = of_key.T
    allowed = (along <= down) & (of_key == of_query)
    before = jnp.where(of_key < of_query, 1.0, 0.0)
    position = down.astype(F32) - jnp.sum(before, axis=1, keepdims=True)
    power = (along % HALF).astype(F32) * (2.0 / HEAD_SIZE)
    angle = position * jnp.exp(power * -math.log(THETA))
    cosine = jnp.cos(angle)
    sine = jnp.sin(angle)
    sine = jnp.where((along % HEAD_SIZE) < HALF, -sine, sine)
    cos_ref[...] = cosine
    sin_ref[...] = sine

    def turn(v):
        return v * cosine + swap_halves(v) * sine

    keys = turn(joined[:, width : width + LANES])
    values = joined[:, width + LANES : width + 2 * LANES]
    keys_low = keys.astype(BF)
    values_low = values.astype(BF)
    k_ref[...] = keys_low
    v_ref[...] = values_low
    key_kinds = lane_kinds(keys_low.astype(F32))
    value_kinds = lane_kinds(values_low.astype(F32))
    key_kinds = [[k.astype(BF) for k in ks] for ks in key_kinds]
    value_kinds = [[v.astype(BF) for v in vs] for vs in value_kinds]
    for i in range(PAIRS):
        q = turn(joined[:, i * LANES : (i + 1) * LANES]).astype(BF)
        q_ref[:, i * LANES : (i + 1) * LANES] = q
        mixed = jnp.zeros(q.shape, F32)
        for side in range(2):
            h = 2 * i + side
            g = h // GROUP
            scores = dot_t(q, key_kinds[g][side]) * SCALE
            scores = jnp.where(allowed, scores, -1e30)
            top = jnp.max(scores, axis=-1, keepdims=True)
            e = jnp.exp(scores - top)
            p = e / jnp.sum(e, axis=-1, keepdims=True)
            p_ref[h] = p
            mixed = mixed + dot(p.astype(BF), value_kinds[g][side])
        o_ref[:, i * LANES : (i + 1) * LANES] = mixed.astype(BF)


def attend(where, x, seg, own, vectors, mine, other, shards):
    tokens, width = x.shape
    joined = own.shape[1]
    outs = [
        shape((tokens, width)), shape((tokens, width)), shape((tokens, LANES)),
        shape((tokens, LANES)), shape((QUERY_HEADS, tokens, tokens), F32),
        shape((tokens, width)), shape((width, joined)), shape(vectors[0].shape, F32),
        shape((tokens, LANES), F32), shape((tokens, LANES), F32),
    ]
    return call(
        functools.partial(attend_kernel, shards), "attend", outs, where,
        [x, seg, own, *vectors, *mine, *other],
        flops=2 * tokens * width * joined + 8 * QUERY_HEADS * tokens * tokens * LANES,
    )


def mix_kernel(shards, where, x, o, vec, own, *rest):
    n = shards - 1
    mine, other = rest[:n], rest[n : 2 * n]
    h_ref, n2_ref, w_ref = rest[2 * n :]
    place_rows(w_ref, where[0], where[1], own, mine, other)
    width = x.shape[1]
    h = x[...].astype(F32) + dot(o[...], w_ref[...])
    h_ref[...] = h
    root = lax.rsqrt(jnp.mean(h * h, axis=1, keepdims=True) + EPS)
    n2_ref[...] = (h * root * vec[1:2, :width]).astype(BF)


def mix(where, x, o, vec, own, mine, other, shards):
    tokens, width = x.shape
    outs = [shape(x.shape, F32), shape(x.shape), shape((width, width))]
    return call(
        functools.partial(mix_kernel, shards), "mix", outs, where,
        [x, o, vec, own, *mine, *other], flops=2 * tokens * width * width,
    )


def down_back_kernel(pieces, where, down, *rest):
    parts, (dact_ref, dy_ref) = rest[:pieces], rest[pieces:]
    tokens = parts[0].shape[0]
    for i in range(pieces):
        dy_ref[i * tokens : (i + 1) * tokens] = parts[i][...]
    slab = dact_ref.shape[1]
    w = down[rows_at(where[1] * slab, slab)]
    step = 2 * tokens

    @pl.loop(0, pieces // 2)
    def _(i):
        at = pl.ds(pl.multiple_of(i * step, step), step)
        dact_ref[at] = dot_t(dy_ref[at], w)


def down_back(where, down, parts, slab):
    tokens, width = parts[0].shape
    total = tokens * len(parts)
    outs = [shape((total, slab), F32), shape((total, width))]
    return call(
        functools.partial(down_back_kernel, len(parts)), "down_back", outs, where,
        [down, *parts], flops=2 * total * width * slab,
    )


def feed_kernel(shards, where, dact, dy, *rest):
    pieces = 2 * shards
    parts, rest = rest[:pieces], rest[pieces:]
    own, direct, passed = rest[0], rest[1:shards], rest[shards : 2 * shards - 1]
    rest = rest[2 * shards - 1 :]
    d1_ref, d2_ref, act_ref, dgate_ref, dup_ref, n_ref, wg_ref, wu_ref = rest
    s = where[0]
    tokens = parts[0].shape[0]
    rows = own.shape[0] // 2
    wg_ref[rows_at(s * rows, rows)] = own[:rows]
    wu_ref[rows_at(s * rows, rows)] = own[rows:]
    for parity, (first, second) in enumerate(((wg_ref, wu_ref), (wu_ref, wg_ref))):

        @pl.when((where[2] & 1) == parity)
        def _(first=first, second=second):
            for k in range(1, shards):
                at = rows_at((s ^ k) * rows, rows)
                first[at] = direct[k - 1][...]
                second[at] = passed[k - 1][...]

    for i in range(pieces):
        n_ref[i * tokens : (i + 1) * tokens] = parts[i][...]
    step = 2 * tokens

    @pl.loop(0, pieces // 2)
    def _(i):
        at = pl.ds(pl.multiple_of(i * step, step), step)
        block = n_ref[at]
        gate = dot(block, wg_ref[...])
        up = dot(block, wu_ref[...])
        sigma = jax.nn.sigmoid(gate)
        swish = gate * sigma
        act_ref[at] = (swish * up).astype(BF)
        da = dact[at]
        dgate_ref[at] = (da * up * sigma * (1.0 + gate * (1.0 - sigma))).astype(BF)
        dup_ref[at] = (da * swish).astype(BF)

    cut = d1_ref.shape[0]
    grad = t_dot(act_ref[...], dy[...])
    d1_ref[...] = grad[:cut].astype(BF)
    d2_ref[...] = grad[cut:].astype(BF)


def feed(where, dact, dy, parts, weights, shards):
    total, slab = dact.shape
    width = dy.shape[1]
    cut = slab // 32 * 16
    outs = [
        shape((cut, width)), shape((slab - cut, width)), shape((total, slab)),
        shape((total, slab)), shape((total, slab)), shape((total, width)),
        shape((width, slab)), shape((width, slab)),
    ]
    return call(
        functools.partial(feed_kernel, shards), "feed", outs, where,
        [dact, dy, *parts, *weights], flops=6 * total * width * slab,
    )


def wide_kernel(shards, where, n, dgate, dup, *rest):
    outs, acc = rest[:shards], rest[shards]
    rows = outs[0].shape[0] // 2
    s = where[0]
    acc[...] = t_dot(n[...], dgate[...])
    for k in range(shards):
        outs[k][:rows] = acc[rows_at((s ^ k) * rows, rows)].astype(BF)
    acc[...] = t_dot(n[...], dup[...])
    for k in range(shards):
        outs[k][rows:] = acc[rows_at((s ^ k) * rows, rows)].astype(BF)


def wide(where, n, dgate, dup, shards):
    total, width = n.shape
    slab = dgate.shape[1]
    outs = [shape((2 * width // shards, slab))] * shards
    return call(
        functools.partial(wide_kernel, shards), "wide", outs, where, [n, dgate, dup],
        [pltpu.VMEM((width, slab), F32)], flops=4 * total * width * slab,
    )


def lay_kernel(shards, where, *rest):
    mine, other = rest[:shards], rest[shards : 2 * shards]
    gate_ref, up_ref, stage = rest[2 * shards :]
    rows, slab = gate_ref.shape[0], stage.shape[2]
    s, c = where[0], where[1]
    for k in range(shards):
        stage[k] = mine[k][...]
        stage[shards + k] = other[k][...]
    for j in range(2 * shards):
        at = ((j // 2) ^ s) + jnp.where(c == j % 2, 0, shards)
        gate_ref[:, j * slab : (j + 1) * slab] = stage[at, :rows].astype(F32)
        up_ref[:, j * slab : (j + 1) * slab] = stage[at, rows:].astype(F32)


def lay(where, mine, other):
    shards = len(mine)
    rows, slab = mine[0].shape[0] // 2, mine[0].shape[1]
    outs = [shape((rows, 2 * shards * slab), F32)] * 2
    return call(
        functools.partial(lay_kernel, shards), "lay", outs, where, [*mine, *other],
        [pltpu.VMEM((2 * shards, 2 * rows, slab), BF)],
    )


def narrow_kernel(where, dgate, dup, wg, wu, keep, give):
    count = keep.shape[0]
    step = count // 2

    def block(i):
        at = pl.ds(pl.multiple_of(i * step, step), step)
        return dot_t(dgate[at], wg[...]) + dot_t(dup[at], wu[...])

    @pl.loop(0, 2)
    def _(i):
        give[pl.ds(pl.multiple_of(i * step, step), step)] = block(i + 2).astype(BF)

    @pl.loop(0, 2)
    def _(i):
        keep[pl.ds(pl.multiple_of(i * step, step), step)] = block(i)


def narrow(where, dgate, dup, wg, wu):
    total, slab = dgate.shape
    width = wg.shape[0]
    outs = [shape((total // 2, width), F32), shape((total // 2, width))]
    return call(
        narrow_kernel, "narrow", outs, where, [dgate, dup, wg, wu],
        flops=4 * total * width * slab,
    )


def back_kernel(shards, tall, where, *rest):
    dn, rest = rest[:shards], rest[shards:]
    hidden, ct, x, vec, wout, wqkv, mixed, n1, query, keys, values, probs, cos, sin = rest[:14]
    gt_ref, keep, give, da_ref, acc_q, acc_o, dob_ref = rest[14:]
    s, c = where[0], where[1]
    tokens, width = x.shape
    joined = wqkv.shape[1]
    rows = width // shards
    half = rows // 2
    cosine, sine = cos[...], sin[...]
    gain1, gain2 = vec[0:1, :width], vec[1:2, :width]

    dn2 = dn[0][...]
    for k in range(1, shards):
        dn2 = dn2 + dn[k][...].astype(F32)
    h = hidden[...]
    root = lax.rsqrt(jnp.mean(h * h, axis=1, keepdims=True) + EPS)
    g_norm2 = jnp.sum(dn2 * h * root, axis=0, keepdims=True)
    e = dn2 * gain2
    mean = jnp.mean(e * h, axis=1, keepdims=True)
    dh = ct[...].astype(F32) + root * e - h * (root * root * root * mean)
    dab = dh.astype(BF)
    gt_ref[...] = dh
    acc_o[...] = t_dot(mixed[...], dab)
    dob_ref[...] = dot_t(dab, wout[...]).astype(BF)

    key_kinds = [[k.astype(BF) for k in ks] for ks in lane_kinds(keys[...].astype(F32))]
    value_kinds = [[v.astype(BF) for v in vs] for vs in lane_kinds(values[...].astype(F32))]
    zero = jnp.zeros((tokens, LANES), F32)
    d_key = [[zero, zero], [zero, zero]]
    d_value = [[zero, zero], [zero, zero]]

    def turn_back(v):
        return v * cosine - swap_halves(v) * sine

    for i in range(PAIRS):
        q = query[:, i * LANES : (i + 1) * LANES]
        do = dob_ref[:, i * LANES : (i + 1) * LANES]
        dq = zero
        for side in range(2):
            head = 2 * i + side
            g = head // GROUP
            p = probs[head]
            dp = dot_t(do, value_kinds[g][side])
            d_value[g][side] = d_value[g][side] + t_dot(p.astype(BF), do)
            ds = (p * (dp - jnp.sum(p * dp, axis=-1, keepdims=True))).astype(BF)
            dq = dq + dot(ds, key_kinds[g][side])
            d_key[g][side] = d_key[g][side] + t_dot(ds, q)
        da_ref[:, i * LANES : (i + 1) * LANES] = turn_back(dq * SCALE).astype(BF)

    low = lax.broadcasted_iota(jnp.int32, (tokens, LANES), 1) < HEAD_SIZE

    def collect(parts):
        first = jnp.where(low, parts[0][0], parts[1][1])
        second = jnp.where(low, parts[1][0], parts[0][1])
        return first + pltpu.roll(second, HEAD_SIZE, 1)

    da_ref[:, width : width + LANES] = turn_back(collect(d_key) * SCALE).astype(BF)
    da_ref[:, width + LANES :] = collect(d_value).astype(BF)
    da = da_ref[...]
    acc_q[...] = t_dot(n1[...], da)
    g_bias = jnp.sum(da.astype(F32), axis=0, keepdims=True)
    dn1 = dot_t(da, wqkv[...])
    xf = x[...].astype(F32)
    root = lax.rsqrt(jnp.mean(xf * xf, axis=1, keepdims=True) + EPS)
    g_norm1 = jnp.sum(dn1 * xf * root, axis=0, keepdims=True)
    e = dn1 * gain1
    mean = jnp.mean(e * xf, axis=1, keepdims=True)
    gt_ref[...] = gt_ref[...] + root * e - xf * (root * root * root * mean)

    blank = jnp.zeros((5, LANES), F32)
    for target, side in ((keep, c), (give, 1 - c)):
        for k in range(shards):
            at = rows_at((s ^ k) * rows + side * half, half)
            for b in range(joined // LANES):
                lanes = slice(b * LANES, (b + 1) * LANES)
                base = b * (half + 8)
                target[k, base : base + half] = acc_q[at, lanes].astype(target.dtype)
                if (b + 1) * LANES <= width:
                    head = [g_norm1[:, lanes], g_norm2[:, lanes]]
                else:
                    head = [blank[:2]]
                tail = jnp.concatenate(head + [g_bias[:, lanes], blank], axis=0)
                target[k, base + half : base + half + 8] = tail.astype(target.dtype)
            for b in range(width // LANES):
                lanes = slice(b * LANES, (b + 1) * LANES)
                base = tall + b * half
                target[k, base : base + half] = acc_o[at, lanes].astype(target.dtype)


def layout_of(width, joined, rows):
    half = rows // 2
    tall = joined // LANES * (half + 8)
    return tall, tall + width // LANES * half


def down_kernel(where, act, down, keep, give):
    count = keep.shape[0]
    step = count // 2
    slab = act.shape[1]
    w = down[rows_at(where[1] * slab, slab)]

    @pl.loop(0, 2)
    def _(i):
        at = pl.multiple_of(i * step, step)
        give[pl.ds(at, step)] = dot(act[pl.ds(at + count, step)], w).astype(BF)
        keep[pl.ds(at, step)] = dot(act[pl.ds(at, step)], w)


def down_project(where, act, down):
    total, slab = act.shape
    width = down.shape[1]
    outs = [shape((total // 2, width), F32), shape((total // 2, width))]
    return call(
        down_kernel, "ydown", outs, where, [act, down], flops=2 * total * width * slab
    )


def pick_kernel(low, high, where, total, arrived, out):
    inside = (where[2] > low) & (where[2] < high)

    @pl.when(inside)
    def _():
        out[...] = total[...]

    @pl.when(jnp.logical_not(inside))
    def _():
        out[...] = arrived[...]


def pick(where, total, arrived, low, high):
    return call(
        functools.partial(pick_kernel, low, high), "pick", [shape(total.shape)], where,
        [total, arrived],
    )[0]


def stack_kernel(where, *rest):
    mine, other, out = rest[: len(rest) // 2], rest[len(rest) // 2 : -1], rest[-1]
    slab = out.shape[0] // 2
    for parts, side in ((mine, where[1]), (other, 1 - where[1])):
        start = side * slab
        for part in parts:
            out[rows_at(start, part.shape[0])] = part[...].astype(F32)
            start = start + part.shape[0]


def stack(where, mine, other):
    rows = 2 * sum(p.shape[0] for p in mine)
    outs = [shape((rows, mine[0].shape[1]), F32)]
    return call(stack_kernel, "stack", outs, where, [*mine, *other])[0]


def back(where, dn, hidden, ct, x, vec, wout, wqkv, mixed, n1, query, keys, values, probs, cos, sin):
    shards = len(dn)
    tokens, width = x.shape
    joined = wqkv.shape[1]
    tall, whole = layout_of(width, joined, width // shards)
    outs = [
        shape(x.shape, F32), shape((shards, whole, LANES), F32), shape((shards, whole, LANES)),
    ]
    return call(
        functools.partial(back_kernel, shards, tall), "back", outs, where,
        [*dn, hidden, ct, x, vec, wout, wqkv, mixed, n1, query, keys, values, probs, cos, sin],
        [
            pltpu.VMEM((tokens, joined), BF), pltpu.VMEM((width, joined), F32),
            pltpu.VMEM((width, width), F32), pltpu.VMEM((tokens, width), BF),
        ],
        flops=4 * tokens * width * (joined + width),
    )


def merge_kernel(shards, where, keep, arrived, *outs):
    for k in range(shards):
        total = keep[k] + arrived[k].astype(F32)
        outs[k][...] = total.astype(outs[k].dtype)


def merge(where, keep, arrived):
    shards = keep.shape[0]
    outs = [shape(keep.shape[1:], F32)] + [shape(keep.shape[1:])] * (shards - 1)
    return call(functools.partial(merge_kernel, shards), "merge", outs, where, [keep, arrived])


def finish_kernel(where, own, *rest):
    value = own[...]
    for piece in rest[:-1]:
        value = value + piece[...].astype(F32)
    rest[-1][...] = value.astype(BF)


def finish(where, parts):
    return call(finish_kernel, "finish", [shape(parts[0].shape)], where, parts)[0]


def close_kernel(tall, where, mine, other, qkv_ref, out_ref, vec_ref):
    c = where[1]
    half = qkv_ref.shape[0] // 2
    for source, side in ((mine, c), (other, 1 - c)):
        at = pl.ds(pl.multiple_of(side * half, 8), half)
        for b in range(qkv_ref.shape[1] // LANES):
            base = b * (half + 8)
            qkv_ref[at, b * LANES : (b + 1) * LANES] = source[base : base + half].astype(F32)
        for b in range(out_ref.shape[1] // LANES):
            base = tall + b * half
            out_ref[at, b * LANES : (b + 1) * LANES] = source[base : base + half].astype(F32)
    for b in range(qkv_ref.shape[1] // LANES):
        base = b * (half + 8) + half
        vec_ref[:, b * LANES : (b + 1) * LANES] = mine[base : base + 8].astype(F32)


def close(where, mine, other, rows, width, joined, tall):
    outs = [shape((rows, joined), F32), shape((rows, width), F32), shape((8, joined), F32)]
    return call(functools.partial(close_kernel, tall), "close", outs, where, [mine, other])


def body(
    tokens, seg_ids, norm1_gain, w_qkv, b_qkv, w_out, norm2_gain, w_gate, w_up, w_down, cotangent
):
    shards = lax.axis_size("shard")
    shard = lax.axis_index("shard")
    replica = lax.axis_index("replica")
    core = replica & 1
    where = jnp.stack([shard, core, replica >> 1]).astype(jnp.int32)
    count, width = tokens.shape
    rows = norm1_gain.shape[0]
    half_rows = rows // 2
    joined = w_qkv.shape[1]
    bias_rows = b_qkv.shape[0]
    slab = w_gate.shape[1] // (2 * shards)
    half = lax.dynamic_slice_in_dim(w_qkv, core * half_rows, half_rows, 0)
    qkv_mine = spread(half)[1:]
    vectors = [
        jnp.pad(v[None], ((0, 0), (0, joined - v.shape[0])))
        for v in (norm1_gain, norm2_gain, b_qkv)
    ]
    vectors = jnp.concatenate(vectors + [jnp.zeros((5, joined), BF)], axis=0)
    vectors = spread(vectors)
    qkv_other = [swap_core(p) for p in qkv_mine]
    out_mine = spread(lax.dynamic_slice_in_dim(w_out, core * half_rows, half_rows, 0))[1:]
    out_other = [swap_core(p) for p in out_mine]

    packed = pack(where, w_gate, w_up, shards)
    direct = [shard_swap(packed[k], k) for k in range(1, shards)]
    passed = [pair_swap(w) for w in direct]
    dy = spread(cotangent)
    dy = dy + [swap_core(p) for p in dy]

    n_one, query, keys, values, probs, mixed, wqkv, vec, cosine, sine = attend(
        where, tokens, seg_ids,
        w_qkv, vectors, qkv_mine, qkv_other, shards,
    )
    hidden, n_two, wout = mix(where, tokens, mixed, vec, w_out, out_mine, out_other, shards)
    n_parts = spread(n_two)
    n_parts = n_parts + [swap_core(p) for p in n_parts]

    dact, dy_all = down_back(where, w_down, dy, slab)
    down_one, down_two, act, d_gate, d_up, n_all, wgate, wup = feed(
        where, dact, dy_all, n_parts, [packed[0], *direct, *passed], shards
    )
    down_one, down_two = line_sum(where, down_one), line_sum(where, down_two)

    def plane_sum(keep, give):
        arrived = swap_core(give)
        total = keep + arrived.astype(F32)
        parts = [total[:count]]
        for k in range(1, shards):
            send = total[k * count : (k + 1) * count].astype(BF)
            parts.append(shard_swap(send, k))
        return parts

    dn = plane_sum(*narrow(where, d_gate, d_up, wgate, wup))

    grads = wide(where, n_all, d_gate, d_up, shards)
    grads = [grads[0]] + [shard_swap(grads[k], k) for k in range(1, shards)]
    grads = [line_sum(where, g) for g in grads]
    gate_part, up_part = lay(where, grads, [swap_core(g) for g in grads])

    down_part = stack(where, [down_one, down_two], [swap_core(down_one), swap_core(down_two)])
    y = plane_sum(*down_project(where, act, w_down))
    layer_out = call(finish_kernel, "yout", [shape(hidden.shape)], where, [hidden, *y])[0]

    grad_tokens, keep, give = back(
        where, dn, hidden, cotangent, tokens, vec, wout, wqkv, mixed, n_one, query, keys, values,
        probs, cosine, sine,
    )
    parts = merge(where, keep, swap_core(give))
    parts = [parts[0]] + [shard_swap(parts[k], k) for k in range(1, shards)]
    tall, _ = layout_of(width, joined, rows)
    item = line_sum(where, finish(where, parts))
    qkv_part, out_part, vec_grads = close(where, item, swap_core(item), rows, width, joined, tall)
    one_part = lax.dynamic_slice(vec_grads[0], (shard * rows,), (rows,))
    two_part = lax.dynamic_slice(vec_grads[1], (shard * rows,), (rows,))
    bias_part = lax.dynamic_slice(vec_grads[2], (shard * bias_rows,), (bias_rows,))
    return (
        layer_out,
        grad_tokens,
        one_part,
        qkv_part,
        bias_part,
        out_part,
        two_part,
        gate_part,
        up_part,
        down_part,
    )


def solution(mesh):
    split = P(("shard", "replica"), None)
    matrix = P("shard", None)
    vector = P("shard")
    in_specs = (
        split, split, vector, matrix, vector, matrix, vector, matrix, matrix, matrix, split,
    )
    out_specs = (split, split, vector, matrix, vector, matrix, vector, matrix, matrix, matrix)
    return jax.shard_map(body, mesh=mesh, in_specs=in_specs, out_specs=out_specs, check_vma=False)
```

profile of v0, /device:TPU:0, one launch (start us, length us, event | category | flops | bytes accessed | tf_op | source)
XLA Modules:
  0.0 308.5 jit_solution(6282036751736325287)
XLA Ops:
  1.6 3.0 collective-permute-start.9
  8.9 2.9 collective-permute-start.2
  14.1 1.6 collective-permute-start.16
  18.2 2.7 collective-permute-done.11.rest_2_
  21.4 3.4 %collective-permute-done.15.rest_1_ = bf16[128,896]{1,0:T(8,128)(2,1)S(1)} collective-permute-done((bf16[128,896]{1,0:T(8,128)(2,1)}, bf16[128,896]{1,0:T(8,128)(2,1)S(1)}, u32[]{:S(2)}, u32[]{:S(2)}) %collective-permute-start.15) | collective-permute-done | bytes 229408 | tf_op jit(solution)/shard_map/ppermute | solution.py:33
  27.7 1.7 collective-permute-start.5
  29.5 1.6 copy-done
  31.1 1.6 copy-done.1
  32.7 2.2 shard_map.189
  36.8 1.7 collective-permute-start.31
  38.9 2.8 collective-permute-done.5.rest_5_
  41.7 5.2 %collective-permute-done.29.rest_9_ = bf16[224,608]{1,0:T(8,128)(2,1)S(1)} collective-permute-done((bf16[224,608]{1,0:T(8,128)(2,1)S(1)}, bf16[224,608]{1,0:T(8,128)(2,1)S(1)}, u32[]{:S(2)}, u32[]{:S(2)}) %collective-permute-start.29) | collective-permute-done | bytes 272416 | tf_op jit(solution)/shard_map/ppermute | solution.py:33
  47.9 3.6 %collective-permute-done.31.rest_11_ = bf16[224,608]{1,0:T(8,128)(2,1)S(1)} collective-permute-done((bf16[224,608]{1,0:T(8,128)(2,1)S(1)}, bf16[224,608]{1,0:T(8,128)(2,1)S(1)}, u32[]{:S(2)}, u32[]{:S(2)}) %collective-permute-start.31) | collective-permute-done | bytes 272416 | tf_op jit(solution)/shard_map/ppermute | solution.py:33
  53.0 1.6 collective-permute-start.32
  55.0 4.3 %shard_map.186 = (bf16[128,896]{1,0:T(8,128)(2,1)S(1)}, bf16[128,896]{1,0:T(8,128)(2,1)S(1)}, bf16[128,128]{1,0:T(8,128)(2,1)S(1)}, bf16[128,128]{1,0:T(8,128)(2...) custom-call(s32[3]{0:T(128)S(1)} %pad_add_fusion.where, ...), custom_call_target="tpu_custom_call" | custom-call | flops 499122176 | bytes 6271488 | tf_op jit(solution)/shard_map/pallas_call | solution.py:85
  65.8 3.1 collective-permute-done.33.rest_13_
  69.4 4.2 %collective-permute-done.23.rest_2_ = bf16[128,896]{1,0:T(8,128)(2,1)S(1)} collective-permute-done((bf16[128,896]{1,0:T(8,128)(2,1)S(1)}, bf16[128,896]{1,0:T(8,128)(2,1)S(1)}, u32[]{:S(2)}, u32[]{:S(2)}) %collective-permute-start.23) | collective-permute-done | bytes 229408 | tf_op jit(solution)/shard_map/ppermute | solution.py:33
  74.1 3.3 %shard_map.188 = (f32[1024,608]{1,0:T(8,128)S(1)}, bf16[1024,896]{1,0:T(8,128)(2,1)S(1)}) custom-call(s32[3]{0:T(128)S(1)} %pad_add_fusion.where, bf16[1216,896]{1,0:T(8,128)(2,1)S(1)} %copy-done.19, bf16[128,896]{1,0:T(8,128)(2,1)S(1)} %copy-done.11, bf16[128,896]{1,0:T(8,128)(2,1)S(1)} %collective-permute-done.15.rest_1_, ...), custom_call_target="tpu_custom_call" | custom-call | flops 1115684864 | bytes 8339456 | tf_op jit(solution)/shard_map/pallas_call | solution.py:85
  77.4 7.0 %shard_map.190 = (bf16[304,896]{1,0:T(8,128)(2,1)S(1)}, bf16[304,896]{1,0:T(8,128)(2,1)S(1)}, bf16[1024,608]{1,0:T(8,128)(2,1)S(1)}, bf16[1024,608]{1,0:T(8,128)...) custom-call(s32[3]{0:T(128)S(1)} %pad_add_fusion.where, ...), custom_call_target="tpu_custom_call" | custom-call | flops 3347054592 | bytes 17178624 | tf_op jit(solution)/shard_map/pallas_call | solution.py:85
  84.4 4.6 %shard_map.193 = (f32[512,896]{1,0:T(8,128)S(1)}, bf16[512,896]{1,0:T(8,128)(2,1)S(1)}) custom-call(s32[3]{0:T(128)S(1)} %pad_add_fusion.where, bf16[1024,608]{1,0:T(8,128)(2,1)S(1)} %get-tuple-element.70.dgate, bf16[1024,608]{1,0:T(8,128)(2,1)S(1)} %get-tuple-element.71.dup, bf16[896,608]{1,0:T(8,128)(2,1)S(1)} %get-tuple-element.72.wg, ...), custom_call_target="tpu_custom_call" | custom-call | flops 2231369728 | bytes 7421952 | tf_op jit(solution)/shard_map/pallas_call | solution.py:85
  89.1 2.5 collective-permute-done.39
  95.5 5.0 %collective-permute-done.40.rest_1_ = bf16[128,896]{1,0:T(8,128)(2,1)S(1)} collective-permute-done((bf16[128,896]{1,0:T(8,128)(2,1)S(1)}, bf16[128,896]{1,0:T(8,128)(2,1)S(1)}, u32[]{:S(2)}, u32[]{:S(2)}) %collective-permute-start.40) | collective-permute-done | bytes 229408 | tf_op jit(solution)/shard_map/ppermute | solution.py:33
  100.4 4.9 %collective-permute-done.41.rest_2_ = bf16[128,896]{1,0:T(8,128)(2,1)S(1)} collective-permute-done((bf16[128,896]{1,0:T(8,128)(2,1)S(1)}, bf16[128,896]{1,0:T(8,128)(2,1)S(1)}, u32[]{:S(2)}, u32[]{:S(2)}) %collective-permute-start.41) | collective-permute-done | bytes 229408 | tf_op jit(solution)/shard_map/ppermute | solution.py:33
  105.3 7.1 %shard_map.194 = (f32[128,896]{1,0:T(8,128)}, f32[4,1864,128]{2,1,0:T(8,128)S(1)}, bf16[4,1864,128]{2,1,0:T(8,128)(2,1)S(1)}) custom-call(s32[3]{0:T(128)S(1)} %pad_add_fusion.where, f32[128,896]{1,0:T(8,128)S(1)} %slice.54.rest_0_, bf16[128,896]{1,0:T(8,128)(2,1)S(1)} %collective-permute-done.40.rest_1_, ...), custom_call_target="tpu_custom_call" | custom-call | flops 939524096 | bytes 13758464 | tf_op jit(solution)/shard_map/pallas_call | solution.py:85
  112.4 3.8 %shard_map.199 = (bf16[448,608]{1,0:T(8,128)(2,1)S(1)}, bf16[448,608]{1,0:T(8,128)(2,1)S(1)}, bf16[448,608]{1,0:T(8,128)(2,1)S(1)}, bf16[448,608]{1,0:T(8,128)(2,1)S(1)}) custom-call(s32[3]{0:T(128)S(1)} %pad_add_fusion.where, bf16[1024,896]{1,0:T(8,128)(2,1)S(1)} %get-tuple-element.95.n, bf16[1024,608]{1,0:T(8,128)(2,1)S(1)} %get-tuple-element.70.dgate, ...), custom_call_target="tpu_custom_call" | custom-call | flops 2231369728 | bytes 6504448 | tf_op jit(solution)/shard_map/pallas_call | solution.py:85
  116.2 3.3 %collective-permute-start.51 = (bf16[448,608]{1,0:T(8,128)(2,1)S(1)}, bf16[448,608]{1,0:T(8,128)(2,1)S(1)}, u32[]{:S(2)}, u32[]{:S(2)}) collective-permute-start(bf16[448,608]{1,0:T(8,128)(2,1)S(1)} %get-tuple-element.96), channel_id=1, source_target_pairs={{0,2},{1,3},{6,4},{7,5},{8,10},{9,11},{14,12},{15,13},{16,18},{17,... | collective-permute-start | bytes 1634312 | tf_op jit(solution)/shard_map/ppermute | solution.py:51
  123.1 9.3 %collective-permute-done.51 = bf16[448,608]{1,0:T(8,128)(2,1)S(1)} collective-permute-done((bf16[448,608]{1,0:T(8,128)(2,1)S(1)}, bf16[448,608]{1,0:T(8,128)(2,1)S(1)}, u32[]{:S(2)}, u32[]{:S(2)}) %collective-permute-start.51) | collective-permute-done | bytes 544800 | tf_op jit(solution)/shard_map/ppermute | solution.py:51
  132.4 4.4 %collective-permute-start.70 = (bf16[304,896]{1,0:T(8,128)(2,1)S(1)}, bf16[304,896]{1,0:T(8,128)(2,1)S(1)}, u32[]{:S(2)}, u32[]{:S(2)}) collective-permute-start(bf16[304,896]{1,0:T(8,128)(2,1)S(1)} %get-tuple-element.102), channel_id=1, source_target_pairs={{0,2},{1,3},{6,4},{7,5},{8,10},{9,11},{14,12},{15,13},{16,18},{17,... | collective-permute-start | bytes 1634312 | tf_op jit(solution)/shard_map/ppermute | solution.py:51
  136.8 2.6 shard_map.191
  139.5 8.2 %collective-permute-done.58 = bf16[448,608]{1,0:T(8,128)(2,1)S(1)} collective-permute-done((bf16[448,608]{1,0:T(8,128)(2,1)S(1)}, bf16[448,608]{1,0:T(8,128)(2,1)S(1)}, u32[]{:S(2)}, u32[]{:S(2)}) %collective-permute-start.58) | collective-permute-done | bytes 544800 | tf_op jit(solution)/shard_map/ppermute | solution.py:33
  147.7 1.8 collective-permute-start.73
  150.3 4.3 %collective-permute-start.55 = (bf16[448,608]{1,0:T(8,128)(2,1)S(1)}, bf16[448,608]{1,0:T(8,128)(2,1)S(1)}, u32[]{:S(2)}, u32[]{:S(2)}) collective-permute-start(bf16[448,608]{1,0:T(8,128)(2,1)S(1)} %collective-permute-done.54), channel_id=1, source_target_pairs={{0,2},{1,3},{6,4},{7,5},{8,10},{9,11},{14,12},{15,13},{16,18},{17,... | collective-permute-start | bytes 1634312 | tf_op jit(solution)/shard_map/ppermute | solution.py:51
  156.9 5.0 %collective-permute-done.73 = bf16[304,896]{1,0:T(8,128)(2,1)S(1)} collective-permute-done((bf16[304,896]{1,0:T(8,128)(2,1)S(1)}, bf16[304,896]{1,0:T(8,128)(2,1)S(1)}, u32[]{:S(2)}, u32[]{:S(2)}) %collective-permute-start.73) | collective-permute-done | bytes 544800 | tf_op jit(solution)/shard_map/ppermute | solution.py:51
  163.2 4.4 %collective-permute-start.63 = (bf16[448,608]{1,0:T(8,128)(2,1)S(1)}, bf16[448,608]{1,0:T(8,128)(2,1)S(1)}, u32[]{:S(2)}, u32[]{:S(2)}) collective-permute-start(bf16[448,608]{1,0:T(8,128)(2,1)S(1)} %collective-permute-done.62), channel_id=1, source_target_pairs={{0,2},{1,3},{6,4},{7,5},{8,10},{9,11},{14,12},{15,13},{16,18},{17,... | collective-permute-start | bytes 1634312 | tf_op jit(solution)/shard_map/ppermute | solution.py:51
  168.3 5.9 %collective-permute-done.55 = bf16[448,608]{1,0:T(8,128)(2,1)S(1)} collective-permute-done((bf16[448,608]{1,0:T(8,128)(2,1)S(1)}, bf16[448,608]{1,0:T(8,128)(2,1)S(1)}, u32[]{:S(2)}, u32[]{:S(2)}) %collective-permute-start.55) | collective-permute-done | bytes 544800 | tf_op jit(solution)/shard_map/ppermute | solution.py:51
  175.3 11.2 %collective-permute-done.59 = bf16[448,608]{1,0:T(8,128)(2,1)S(1)} collective-permute-done((bf16[448,608]{1,0:T(8,128)(2,1)S(1)}, bf16[448,608]{1,0:T(8,128)(2,1)S(1)}, u32[]{:S(2)}, u32[]{:S(2)}) %collective-permute-start.59) | collective-permute-done | bytes 544800 | tf_op jit(solution)/shard_map/ppermute | solution.py:51
  192.0 4.2 %collective-permute-done.46.rest_2_ = bf16[1864,128]{1,0:T(8,128)(2,1)S(1)} collective-permute-done((bf16[1864,128]{1,0:T(8,128)(2,1)S(1)}, bf16[1864,128]{1,0:T(8,128)(2,1)S(1)}, u32[]{:S(2)}, u32[]{:S(2)}) %collective-permute-start.46) | collective-permute-done | bytes 477216 | tf_op jit(solution)/shard_map/ppermute | solution.py:33
  196.9 4.4 %collective-permute-start.47 = (bf16[1864,128]{1,0:T(8,128)(2,1)S(1)}, bf16[1864,128]{1,0:T(8,128)(2,1)S(1)}, u32[]{:S(2)}, u32[]{:S(2)}) collective-permute-start(bf16[1864,128]{1,0:T(8,128)(2,1)S(1)} %shard_map.196), channel_id=1, source_target_pairs={{0,2},{1,3},{6,4},{7,5},{8,10},{9,11},{14,12},{15,13},{16,18},{17,... | collective-permute-start | bytes 1431560 | tf_op jit(solution)/shard_map/ppermute | solution.py:51
  204.1 4.9 %collective-permute-done.36.rest_1_ = bf16[128,896]{1,0:T(8,128)(2,1)S(1)} collective-permute-done((bf16[128,896]{1,0:T(8,128)(2,1)S(1)}, bf16[128,896]{1,0:T(8,128)(2,1)S(1)}, u32[]{:S(2)}, u32[]{:S(2)}) %collective-permute-start.36) | collective-permute-done | bytes 229408 | tf_op jit(solution)/shard_map/ppermute | solution.py:33
  216.5 14.6 %collective-permute-done.72.arrived = bf16[304,896]{1,0:T(8,128)(2,1)S(1)} collective-permute-done((bf16[304,896]{1,0:T(8,128)(2,1)S(1)}, bf16[304,896]{1,0:T(8,128)(2,1)S(1)}, u32[]{:S(2)}, u32[]{:S(2)}) %collective-permute-start.72) | collective-permute-done | bytes 544800 | tf_op jit(solution)/shard_map/ppermute | solution.py:51
  233.2 9.6 %collective-permute-done.75.arrived = bf16[304,896]{1,0:T(8,128)(2,1)S(1)} collective-permute-done((bf16[304,896]{1,0:T(8,128)(2,1)S(1)}, bf16[304,896]{1,0:T(8,128)(2,1)S(1)}, u32[]{:S(2)}, u32[]{:S(2)}) %collective-permute-start.75) | collective-permute-done | bytes 544800 | tf_op jit(solution)/shard_map/ppermute | solution.py:51
  244.6 10.4 %collective-permute-done.57.arrived = bf16[448,608]{1,0:T(8,128)(2,1)S(1)} collective-permute-done((bf16[448,608]{1,0:T(8,128)(2,1)S(1)}, bf16[448,608]{1,0:T(8,128)(2,1)S(1)}, u32[]{:S(2)}, u32[]{:S(2)}) %collective-permute-start.57) | collective-permute-done | bytes 544800 | tf_op jit(solution)/shard_map/ppermute | solution.py:51
  255.0 12.3 %collective-permute-done.61.arrived = bf16[448,608]{1,0:T(8,128)(2,1)S(1)} collective-permute-done((bf16[448,608]{1,0:T(8,128)(2,1)S(1)}, bf16[448,608]{1,0:T(8,128)(2,1)S(1)}, u32[]{:S(2)}, u32[]{:S(2)}) %collective-permute-start.61) | collective-permute-done | bytes 544800 | tf_op jit(solution)/shard_map/ppermute | solution.py:51
  268.3 10.5 %collective-permute-done.65.arrived = bf16[448,608]{1,0:T(8,128)(2,1)S(1)} collective-permute-done((bf16[448,608]{1,0:T(8,128)(2,1)S(1)}, bf16[448,608]{1,0:T(8,128)(2,1)S(1)}, u32[]{:S(2)}, u32[]{:S(2)}) %collective-permute-start.65) | collective-permute-done | bytes 544800 | tf_op jit(solution)/shard_map/ppermute | solution.py:51
  282.8 2.9 collective-permute-done.38.rest_3_
  295.3 2.9 shard_map.207
  298.2 6.4 %shard_map.204 = (f32[224,4864]{1,0:T(8,128)}, f32[224,4864]{1,0:T(8,128)}) custom-call(s32[3]{0:T(128)S(1)} %pad_add_fusion.where, bf16[448,608]{1,0:T(8,128)(2,1)S(1)} %shard_map.200.rest_0_, bf16[448,608]{1,0:T(8,128)(2,1)S(1)} %shard_map.201.rest_1_, bf16[448,608]{1,0:T(8,128)(2,1)S(1)} %shard_map.202.rest_2_, bf16[448,608]{1,0:T(8,128)(2,1)S(1)} %shard_map.203.rest_3_, ...), custom_call_target="tpu_custom_call" | custom-call | bytes 13074432 | tf_op jit(solution)/shard_map/pallas_call | solution.py:85
  304.6 2.5 shard_map.198
  (202 shorter events, 75.7 us)
Async XLA Ops:
  1.6 14.1 %collective-permute-start.9 = (bf16[112,896]{1,0:T(8,128)(2,1)S(1)}, bf16[112,896]{1,0:T(8,128)(2,1)S(1)}, u32[]{:S(2)}, u32[]{:S(2)}) collective-permute-start(bf16[112,896]{1,0:T(8,128)(2,1)S(1)} %constant_dynamic-slice_fusion.2), channel_id=1, source_target_pairs={{0,8},{8,0},{16,24},{24,16},{1,9},{9,1},{17,25},{25,17},{2,10},{10... | collective-permute-start | bytes 602120 | tf_op jit(solution)/shard_map/ppermute | solution.py:33
  4.6 12.5 %collective-permute-start.10 = (bf16[112,896]{1,0:T(8,128)(2,1)S(1)}, bf16[112,896]{1,0:T(8,128)(2,1)S(1)}, u32[]{:S(2)}, u32[]{:S(2)}) collective-permute-start(bf16[112,896]{1,0:T(8,128)(2,1)S(1)} %constant_dynamic-slice_fusion.2), channel_id=1, source_target_pairs={{0,16},{8,24},{16,0},{24,8},{1,17},{9,25},{17,1},{25,9},{2,18},{10... | collective-permute-start | bytes 602120 | tf_op jit(solution)/shard_map/ppermute | solution.py:33
  12.7 12.1 %collective-permute-start.15 = (bf16[128,896]{1,0:T(8,128)(2,1)}, bf16[128,896]{1,0:T(8,128)(2,1)S(1)}, u32[]{:S(2)}, u32[]{:S(2)}) collective-permute-start(bf16[128,896]{1,0:T(8,128)(2,1)} %rest_5_.1), channel_id=1, source_target_pairs={{0,8},{8,0},{16,24},{24,16},{1,9},{9,1},{17,25},{25,17},{2,10},{10... | collective-permute-start | bytes 688136 | tf_op jit(solution)/shard_map/ppermute | solution.py:33
  14.1 13.6 %collective-permute-start.16 = (bf16[128,896]{1,0:T(8,128)(2,1)}, bf16[128,896]{1,0:T(8,128)(2,1)S(1)}, u32[]{:S(2)}, u32[]{:S(2)}) collective-permute-start(bf16[128,896]{1,0:T(8,128)(2,1)} %rest_5_.1), channel_id=1, source_target_pairs={{0,16},{8,24},{16,0},{24,8},{1,17},{9,25},{17,1},{25,9},{2,18},{10... | collective-permute-start | bytes 688136 | tf_op jit(solution)/shard_map/ppermute | solution.py:33
  15.7 19.2 %collective-permute-start.17 = (bf16[128,896]{1,0:T(8,128)(2,1)}, bf16[128,896]{1,0:T(8,128)(2,1)S(1)}, u32[]{:S(2)}, u32[]{:S(2)}) collective-permute-start(bf16[128,896]{1,0:T(8,128)(2,1)} %rest_5_.1), channel_id=1, source_target_pairs={{0,24},{8,16},{16,8},{24,0},{1,25},{9,17},{17,9},{25,1},{2,26},{10... | collective-permute-start | bytes 688136 | tf_op jit(solution)/shard_map/ppermute | solution.py:33
  17.2 19.1 %collective-permute-start.18 = (bf16[128,896]{1,0:T(8,128)(2,1)}, bf16[128,896]{1,0:T(8,128)(2,1)S(1)}, u32[]{:S(2)}, u32[]{:S(2)}) collective-permute-start(bf16[128,896]{1,0:T(8,128)(2,1)} %rest_5_.1), channel_id=1, source_target_pairs={{0,1},{1,0},{2,3},{3,2},{4,5},{5,4},{6,7},{7,6},{8,9},{9,8},{10,11... | collective-permute-start | bytes 688136 | tf_op jit(solution)/shard_map/ppermute | solution.py:28
  20.8 16.0 %collective-permute-start.3 = (bf16[112,1152]{1,0:T(8,128)(2,1)S(1)}, bf16[112,1152]{1,0:T(8,128)(2,1)S(1)}, u32[]{:S(2)}, u32[]{:S(2)}) collective-permute-start(bf16[112,1152]{1,0:T(8,128)(2,1)S(1)} %constant_dynamic-slice_fusion.3), channel_id=1, source_target_pairs={{0,8},{8,0},{16,24},{24,16},{1,9},{9,1},{17,25},{25,17},{2,10},{10... | collective-permute-start | bytes 774152 | tf_op jit(solution)/shard_map/ppermute | solution.py:33
  24.8 14.1 %collective-permute-start.4 = (bf16[112,1152]{1,0:T(8,128)(2,1)S(1)}, bf16[112,1152]{1,0:T(8,128)(2,1)S(1)}, u32[]{:S(2)}, u32[]{:S(2)}) collective-permute-start(bf16[112,1152]{1,0:T(8,128)(2,1)S(1)} %constant_dynamic-slice_fusion.3), channel_id=1, source_target_pairs={{0,16},{8,24},{16,0},{24,8},{1,17},{9,25},{17,1},{25,9},{2,18},{10... | collective-permute-start | bytes 774152 | tf_op jit(solution)/shard_map/ppermute | solution.py:33
  27.7 14.0 %collective-permute-start.5 = (bf16[112,1152]{1,0:T(8,128)(2,1)S(1)}, bf16[112,1152]{1,0:T(8,128)(2,1)S(1)}, u32[]{:S(2)}, u32[]{:S(2)}) collective-permute-start(bf16[112,1152]{1,0:T(8,128)(2,1)S(1)} %constant_dynamic-slice_fusion.3), channel_id=1, source_target_pairs={{0,24},{8,16},{16,8},{24,0},{1,25},{9,17},{17,9},{25,1},{2,26},{10... | collective-permute-start | bytes 774152 | tf_op jit(solution)/shard_map/ppermute | solution.py:33
  34.9 12.0 %collective-permute-start.29 = (bf16[224,608]{1,0:T(8,128)(2,1)S(1)}, bf16[224,608]{1,0:T(8,128)(2,1)S(1)}, u32[]{:S(2)}, u32[]{:S(2)}) collective-permute-start(bf16[224,608]{1,0:T(8,128)(2,1)S(1)} %get-tuple-element.64), channel_id=1, source_target_pairs={{0,8},{8,0},{16,24},{24,16},{1,9},{9,1},{17,25},{25,17},{2,10},{10... | collective-permute-start | bytes 817160 | tf_op jit(solution)/shard_map/ppermute | solution.py:33
  36.8 14.7 %collective-permute-start.31 = (bf16[224,608]{1,0:T(8,128)(2,1)S(1)}, bf16[224,608]{1,0:T(8,128)(2,1)S(1)}, u32[]{:S(2)}, u32[]{:S(2)}) collective-permute-start(bf16[224,608]{1,0:T(8,128)(2,1)S(1)} %get-tuple-element.66), channel_id=1, source_target_pairs={{0,24},{8,16},{16,8},{24,0},{1,25},{9,17},{17,9},{25,1},{2,26},{10... | collective-permute-start | bytes 817160 | tf_op jit(solution)/shard_map/ppermute | solution.py:33
  38.9 12.6 %collective-permute-start.12 = (bf16[112,896]{1,0:T(8,128)(2,1)S(1)}, bf16[112,896]{1,0:T(8,128)(2,1)S(1)}, u32[]{:S(2)}, u32[]{:S(2)}) collective-permute-start(bf16[112,896]{1,0:T(8,128)(2,1)S(1)} %collective-permute-done.9.rest_0_), channel_id=1, source_target_pairs={{0,1},{1,0},{2,3},{3,2},{4,5},{5,4},{6,7},{7,6},{8,9},{9,8},{10,11... | collective-permute-start | bytes 602120 | tf_op jit(solution)/shard_map/ppermute | solution.py:28
  54.6 14.2 %collective-permute-start.33 = (bf16[224,608]{1,0:T(8,128)(2,1)S(1)}, bf16[224,608]{1,0:T(8,128)(2,1)S(1)}, u32[]{:S(2)}, u32[]{:S(2)}) collective-permute-start(bf16[224,608]{1,0:T(8,128)(2,1)S(1)} %collective-permute-done.30.rest_10_), channel_id=1, source_target_pairs={{0,2},{1,3},{2,0},{3,1},{4,6},{5,7},{6,4},{7,5},{8,10},{9,11},{10,... | collective-permute-start | bytes 817160 | tf_op jit(solution)/shard_map/ppermute | solution.py:38
  61.6 11.9 %collective-permute-start.23 = (bf16[128,896]{1,0:T(8,128)(2,1)S(1)}, bf16[128,896]{1,0:T(8,128)(2,1)S(1)}, u32[]{:S(2)}, u32[]{:S(2)}) collective-permute-start(bf16[128,896]{1,0:T(8,128)(2,1)S(1)} %get-tuple-element.62.rest_0_), channel_id=1, source_target_pairs={{0,16},{8,24},{16,0},{24,8},{1,17},{9,25},{17,1},{25,9},{2,18},{10... | collective-permute-start | bytes 688136 | tf_op jit(solution)/shard_map/ppermute | solution.py:33
  64.2 13.2 %collective-permute-start.34 = (bf16[224,608]{1,0:T(8,128)(2,1)S(1)}, bf16[224,608]{1,0:T(8,128)(2,1)S(1)}, u32[]{:S(2)}, u32[]{:S(2)}) collective-permute-start(bf16[224,608]{1,0:T(8,128)(2,1)S(1)} %collective-permute-done.31.rest_11_), channel_id=1, source_target_pairs={{0,2},{1,3},{2,0},{3,1},{4,6},{5,7},{6,4},{7,5},{8,10},{9,11},{10,... | collective-permute-start | bytes 817160 | tf_op jit(solution)/shard_map/ppermute | solution.py:38
  93.0 12.3 %collective-permute-start.41 = (bf16[128,896]{1,0:T(8,128)(2,1)S(1)}, bf16[128,896]{1,0:T(8,128)(2,1)S(1)}, u32[]{:S(2)}, u32[]{:S(2)}) collective-permute-start(bf16[128,896]{1,0:T(8,128)(2,1)S(1)} %get-tuple-element.109), channel_id=1, source_target_pairs={{0,16},{8,24},{16,0},{24,8},{1,17},{9,25},{17,1},{25,9},{2,18},{10... | collective-permute-start | bytes 688136 | tf_op jit(solution)/shard_map/ppermute | solution.py:33
  112.4 42.2 %collective-permute-start.43 = (bf16[4,1864,128]{2,1,0:T(8,128)(2,1)S(1)}, bf16[4,1864,128]{2,1,0:T(8,128)(2,1)S(1)}, u32[]{:S(2)}, u32[]{:S(2)}) collective-permute-start(bf16[4,1864,128]{2,1,0:T(8,128)(2,1)S(1)} %get-tuple-element.87), channel_id=1, source_target_pairs={{0,1},{1,0},{2,3},{3,2},{4,5},{5,4},{6,7},{7,6},{8,9},{9,8},{10,11... | collective-permute-start | bytes 5726216 | tf_op jit(solution)/shard_map/ppermute | solution.py:28
  116.2 16.2 %collective-permute-start.51 = (bf16[448,608]{1,0:T(8,128)(2,1)S(1)}, bf16[448,608]{1,0:T(8,128)(2,1)S(1)}, u32[]{:S(2)}, u32[]{:S(2)}) collective-permute-start(bf16[448,608]{1,0:T(8,128)(2,1)S(1)} %get-tuple-element.96), channel_id=1, source_target_pairs={{0,2},{1,3},{6,4},{7,5},{8,10},{9,11},{14,12},{15,13},{16,18},{17,... | collective-permute-start | bytes 1634312 | tf_op jit(solution)/shard_map/ppermute | solution.py:51
  119.5 19.9 %collective-permute-start.54 = (bf16[448,608]{1,0:T(8,128)(2,1)S(1)}, bf16[448,608]{1,0:T(8,128)(2,1)S(1)}, u32[]{:S(2)}, u32[]{:S(2)}) collective-permute-start(bf16[448,608]{1,0:T(8,128)(2,1)S(1)} %get-tuple-element.97), channel_id=1, source_target_pairs={{0,8},{8,0},{16,24},{24,16},{1,9},{9,1},{17,25},{25,17},{2,10},{10... | collective-permute-start | bytes 1634312 | tf_op jit(solution)/shard_map/ppermute | solution.py:33
  120.5 27.1 %collective-permute-start.58 = (bf16[448,608]{1,0:T(8,128)(2,1)S(1)}, bf16[448,608]{1,0:T(8,128)(2,1)S(1)}, u32[]{:S(2)}, u32[]{:S(2)}) collective-permute-start(bf16[448,608]{1,0:T(8,128)(2,1)S(1)} %get-tuple-element.98), channel_id=1, source_target_pairs={{0,16},{8,24},{16,0},{24,8},{1,17},{9,25},{17,1},{25,9},{2,18},{10... | collective-permute-start | bytes 1634312 | tf_op jit(solution)/shard_map/ppermute | solution.py:33
  121.6 28.0 %collective-permute-start.62 = (bf16[448,608]{1,0:T(8,128)(2,1)S(1)}, bf16[448,608]{1,0:T(8,128)(2,1)S(1)}, u32[]{:S(2)}, u32[]{:S(2)}) collective-permute-start(bf16[448,608]{1,0:T(8,128)(2,1)S(1)} %get-tuple-element.99), channel_id=1, source_target_pairs={{0,24},{8,16},{16,8},{24,0},{1,25},{9,17},{17,9},{25,1},{2,26},{10... | collective-permute-start | bytes 1634312 | tf_op jit(solution)/shard_map/ppermute | solution.py:33
  132.4 17.9 %collective-permute-start.70 = (bf16[304,896]{1,0:T(8,128)(2,1)S(1)}, bf16[304,896]{1,0:T(8,128)(2,1)S(1)}, u32[]{:S(2)}, u32[]{:S(2)}) collective-permute-start(bf16[304,896]{1,0:T(8,128)(2,1)S(1)} %get-tuple-element.102), channel_id=1, source_target_pairs={{0,2},{1,3},{6,4},{7,5},{8,10},{9,11},{14,12},{15,13},{16,18},{17,... | collective-permute-start | bytes 1634312 | tf_op jit(solution)/shard_map/ppermute | solution.py:51
  139.4 23.8 %collective-permute-start.35 = (bf16[512,896]{1,0:T(8,128)(2,1)S(1)}, bf16[512,896]{1,0:T(8,128)(2,1)S(1)}, u32[]{:S(2)}, u32[]{:S(2)}) collective-permute-start(bf16[512,896]{1,0:T(8,128)(2,1)S(1)} %get-tuple-element.69), channel_id=1, source_target_pairs={{0,1},{1,0},{2,3},{3,2},{4,5},{5,4},{6,7},{7,6},{8,9},{9,8},{10,11... | collective-permute-start | bytes 2752520 | tf_op jit(solution)/shard_map/ppermute | solution.py:28
  147.7 14.3 %collective-permute-start.73 = (bf16[304,896]{1,0:T(8,128)(2,1)S(1)}, bf16[304,896]{1,0:T(8,128)(2,1)S(1)}, u32[]{:S(2)}, u32[]{:S(2)}) collective-permute-start(bf16[304,896]{1,0:T(8,128)(2,1)S(1)} %get-tuple-element.103), channel_id=1, source_target_pairs={{0,2},{1,3},{6,4},{7,5},{8,10},{9,11},{14,12},{15,13},{16,18},{17,... | collective-permute-start | bytes 1634312 | tf_op jit(solution)/shard_map/ppermute | solution.py:51
  149.6 18.0 %collective-permute-start.52 = (bf16[448,608]{1,0:T(8,128)(2,1)S(1)}, bf16[448,608]{1,0:T(8,128)(2,1)S(1)}, u32[]{:S(2)}, u32[]{:S(2)}) collective-permute-start(bf16[448,608]{1,0:T(8,128)(2,1)S(1)} %add.72), channel_id=1, source_target_pairs={{2,4},{3,5},{4,2},{5,3},{10,12},{11,13},{12,10},{13,11},{18,20},{1... | collective-permute-start | bytes 1634312 | tf_op jit(solution)/shard_map/ppermute | solution.py:51
  150.3 23.9 %collective-permute-start.55 = (bf16[448,608]{1,0:T(8,128)(2,1)S(1)}, bf16[448,608]{1,0:T(8,128)(2,1)S(1)}, u32[]{:S(2)}, u32[]{:S(2)}) collective-permute-start(bf16[448,608]{1,0:T(8,128)(2,1)S(1)} %collective-permute-done.54), channel_id=1, source_target_pairs={{0,2},{1,3},{6,4},{7,5},{8,10},{9,11},{14,12},{15,13},{16,18},{17,... | collective-permute-start | bytes 1634312 | tf_op jit(solution)/shard_map/ppermute | solution.py:51
  154.6 31.9 %collective-permute-start.59 = (bf16[448,608]{1,0:T(8,128)(2,1)S(1)}, bf16[448,608]{1,0:T(8,128)(2,1)S(1)}, u32[]{:S(2)}, u32[]{:S(2)}) collective-permute-start(bf16[448,608]{1,0:T(8,128)(2,1)S(1)} %collective-permute-done.58), channel_id=1, source_target_pairs={{0,2},{1,3},{6,4},{7,5},{8,10},{9,11},{14,12},{15,13},{16,18},{17,... | collective-permute-start | bytes 1634312 | tf_op jit(solution)/shard_map/ppermute | solution.py:51
  161.9 26.2 %collective-permute-start.44 = (bf16[1864,128]{1,0:T(8,128)(2,1)S(1)}, bf16[1864,128]{1,0:T(8,128)(2,1)S(1)}, u32[]{:S(2)}, u32[]{:S(2)}) collective-permute-start(bf16[1864,128]{1,0:T(8,128)(2,1)S(1)} %get-tuple-element.89), channel_id=1, source_target_pairs={{0,8},{8,0},{16,24},{24,16},{1,9},{9,1},{17,25},{25,17},{2,10},{10... | collective-permute-start | bytes 1431560 | tf_op jit(solution)/shard_map/ppermute | solution.py:33
  163.2 38.2 %collective-permute-start.63 = (bf16[448,608]{1,0:T(8,128)(2,1)S(1)}, bf16[448,608]{1,0:T(8,128)(2,1)S(1)}, u32[]{:S(2)}, u32[]{:S(2)}) collective-permute-start(bf16[448,608]{1,0:T(8,128)(2,1)S(1)} %collective-permute-done.62), channel_id=1, source_target_pairs={{0,2},{1,3},{6,4},{7,5},{8,10},{9,11},{14,12},{15,13},{16,18},{17,... | collective-permute-start | bytes 1634312 | tf_op jit(solution)/shard_map/ppermute | solution.py:51
  167.6 34.5 %collective-permute-start.71 = (bf16[304,896]{1,0:T(8,128)(2,1)S(1)}, bf16[304,896]{1,0:T(8,128)(2,1)S(1)}, u32[]{:S(2)}, u32[]{:S(2)}) collective-permute-start(bf16[304,896]{1,0:T(8,128)(2,1)S(1)} %add.80), channel_id=1, source_target_pairs={{2,4},{3,5},{4,2},{5,3},{10,12},{11,13},{12,10},{13,11},{18,20},{1... | collective-permute-start | bytes 1634312 | tf_op jit(solution)/shard_map/ppermute | solution.py:51
  174.2 16.5 %collective-permute-start.45 = (bf16[1864,128]{1,0:T(8,128)(2,1)S(1)}, bf16[1864,128]{1,0:T(8,128)(2,1)S(1)}, u32[]{:S(2)}, u32[]{:S(2)}) collective-permute-start(bf16[1864,128]{1,0:T(8,128)(2,1)S(1)} %get-tuple-element.90), channel_id=1, source_target_pairs={{0,16},{8,24},{16,0},{24,8},{1,17},{9,25},{17,1},{25,9},{2,18},{10... | collective-permute-start | bytes 1431560 | tf_op jit(solution)/shard_map/ppermute | solution.py:33
  188.1 14.8 %collective-permute-start.74 = (bf16[304,896]{1,0:T(8,128)(2,1)S(1)}, bf16[304,896]{1,0:T(8,128)(2,1)S(1)}, u32[]{:S(2)}, u32[]{:S(2)}) collective-permute-start(bf16[304,896]{1,0:T(8,128)(2,1)S(1)} %add.82), channel_id=1, source_target_pairs={{2,4},{3,5},{4,2},{5,3},{10,12},{11,13},{12,10},{13,11},{18,20},{1... | collective-permute-start | bytes 1634312 | tf_op jit(solution)/shard_map/ppermute | solution.py:51
  190.7 20.7 %collective-permute-start.53 = (bf16[448,608]{1,0:T(8,128)(2,1)S(1)}, bf16[448,608]{1,0:T(8,128)(2,1)S(1)}, u32[]{:S(2)}, u32[]{:S(2)}) collective-permute-start(bf16[448,608]{1,0:T(8,128)(2,1)S(1)} %add.73.total), channel_id=1, source_target_pairs={{2,0},{3,1},{4,6},{5,7},{10,8},{11,9},{12,14},{13,15},{18,16},{19,... | collective-permute-start | bytes 1634312 | tf_op jit(solution)/shard_map/ppermute | solution.py:51
  196.9 12.9 %collective-permute-start.47 = (bf16[1864,128]{1,0:T(8,128)(2,1)S(1)}, bf16[1864,128]{1,0:T(8,128)(2,1)S(1)}, u32[]{:S(2)}, u32[]{:S(2)}) collective-permute-start(bf16[1864,128]{1,0:T(8,128)(2,1)S(1)} %shard_map.196), channel_id=1, source_target_pairs={{0,2},{1,3},{6,4},{7,5},{8,10},{9,11},{14,12},{15,13},{16,18},{17,... | collective-permute-start | bytes 1431560 | tf_op jit(solution)/shard_map/ppermute | solution.py:51
  209.8 21.3 %collective-permute-start.72 = (bf16[304,896]{1,0:T(8,128)(2,1)S(1)}, bf16[304,896]{1,0:T(8,128)(2,1)S(1)}, u32[]{:S(2)}, u32[]{:S(2)}) collective-permute-start(bf16[304,896]{1,0:T(8,128)(2,1)S(1)} %add.81.total), channel_id=1, source_target_pairs={{2,0},{3,1},{4,6},{5,7},{10,8},{11,9},{12,14},{13,15},{18,16},{19,... | collective-permute-start | bytes 1634312 | tf_op jit(solution)/shard_map/ppermute | solution.py:51
  211.4 21.6 %collective-permute-start.48 = (bf16[1864,128]{1,0:T(8,128)(2,1)S(1)}, bf16[1864,128]{1,0:T(8,128)(2,1)S(1)}, u32[]{:S(2)}, u32[]{:S(2)}) collective-permute-start(bf16[1864,128]{1,0:T(8,128)(2,1)S(1)} %add.68), channel_id=1, source_target_pairs={{2,4},{3,5},{4,2},{5,3},{10,12},{11,13},{12,10},{13,11},{18,20},{1... | collective-permute-start | bytes 1431560 | tf_op jit(solution)/shard_map/ppermute | solution.py:51
  212.1 30.6 %collective-permute-start.75 = (bf16[304,896]{1,0:T(8,128)(2,1)S(1)}, bf16[304,896]{1,0:T(8,128)(2,1)S(1)}, u32[]{:S(2)}, u32[]{:S(2)}) collective-permute-start(bf16[304,896]{1,0:T(8,128)(2,1)S(1)} %add.83.total), channel_id=1, source_target_pairs={{2,0},{3,1},{4,6},{5,7},{10,8},{11,9},{12,14},{13,15},{18,16},{19,... | collective-permute-start | bytes 1634312 | tf_op jit(solution)/shard_map/ppermute | solution.py:51
  213.6 41.5 %collective-permute-start.57 = (bf16[448,608]{1,0:T(8,128)(2,1)S(1)}, bf16[448,608]{1,0:T(8,128)(2,1)S(1)}, u32[]{:S(2)}, u32[]{:S(2)}) collective-permute-start(bf16[448,608]{1,0:T(8,128)(2,1)S(1)} %add.75.total), channel_id=1, source_target_pairs={{2,0},{3,1},{4,6},{5,7},{10,8},{11,9},{12,14},{13,15},{18,16},{19,... | collective-permute-start | bytes 1634312 | tf_op jit(solution)/shard_map/ppermute | solution.py:51
  215.0 52.3 %collective-permute-start.61 = (bf16[448,608]{1,0:T(8,128)(2,1)S(1)}, bf16[448,608]{1,0:T(8,128)(2,1)S(1)}, u32[]{:S(2)}, u32[]{:S(2)}) collective-permute-start(bf16[448,608]{1,0:T(8,128)(2,1)S(1)} %add.77.total), channel_id=1, source_target_pairs={{2,0},{3,1},{4,6},{5,7},{10,8},{11,9},{12,14},{13,15},{18,16},{19,... | collective-permute-start | bytes 1634312 | tf_op jit(solution)/shard_map/ppermute | solution.py:51
  231.1 47.8 %collective-permute-start.65 = (bf16[448,608]{1,0:T(8,128)(2,1)S(1)}, bf16[448,608]{1,0:T(8,128)(2,1)S(1)}, u32[]{:S(2)}, u32[]{:S(2)}) collective-permute-start(bf16[448,608]{1,0:T(8,128)(2,1)S(1)} %add.79.total), channel_id=1, source_target_pairs={{2,0},{3,1},{4,6},{5,7},{10,8},{11,9},{12,14},{13,15},{18,16},{19,... | collective-permute-start | bytes 1634312 | tf_op jit(solution)/shard_map/ppermute | solution.py:51
  233.0 52.8 %collective-permute-start.76 = (bf16[304,896]{1,0:T(8,128)(2,1)S(1)}, bf16[304,896]{1,0:T(8,128)(2,1)S(1)}, u32[]{:S(2)}, u32[]{:S(2)}) collective-permute-start(bf16[304,896]{1,0:T(8,128)(2,1)S(1)} %shard_map.205.rest_0_), channel_id=1, source_target_pairs={{0,1},{1,0},{2,3},{3,2},{4,5},{5,4},{6,7},{7,6},{8,9},{9,8},{10,11... | collective-permute-start | bytes 1634312 | tf_op jit(solution)/shard_map/ppermute | solution.py:28
  242.8 43.5 %collective-permute-start.49 = (bf16[1864,128]{1,0:T(8,128)(2,1)S(1)}, bf16[1864,128]{1,0:T(8,128)(2,1)S(1)}, u32[]{:S(2)}, u32[]{:S(2)}) collective-permute-start(bf16[1864,128]{1,0:T(8,128)(2,1)S(1)} %add.69.total), channel_id=1, source_target_pairs={{2,0},{3,1},{4,6},{5,7},{10,8},{11,9},{12,14},{13,15},{18,16},{19,... | collective-permute-start | bytes 1431560 | tf_op jit(solution)/shard_map/ppermute | solution.py:51
  255.0 32.7 %collective-permute-start.77 = (bf16[304,896]{1,0:T(8,128)(2,1)S(1)}, bf16[304,896]{1,0:T(8,128)(2,1)S(1)}, u32[]{:S(2)}, u32[]{:S(2)}) collective-permute-start(bf16[304,896]{1,0:T(8,128)(2,1)S(1)} %shard_map.206.rest_1_), channel_id=1, source_target_pairs={{0,1},{1,0},{2,3},{3,2},{4,5},{5,4},{6,7},{7,6},{8,9},{9,8},{10,11... | collective-permute-start | bytes 1634312 | tf_op jit(solution)/shard_map/ppermute | solution.py:28
  267.3 15.4 %collective-permute-start.37 = (bf16[128,896]{1,0:T(8,128)(2,1)S(1)}, bf16[128,896]{1,0:T(8,128)(2,1)S(1)}, u32[]{:S(2)}, u32[]{:S(2)}) collective-permute-start(bf16[128,896]{1,0:T(8,128)(2,1)S(1)} %get-tuple-element.112), channel_id=1, source_target_pairs={{0,16},{8,24},{16,0},{24,8},{1,17},{9,25},{17,1},{25,9},{2,18},{10... | collective-permute-start | bytes 688136 | tf_op jit(solution)/shard_map/ppermute | solution.py:33
  282.8 15.4 %collective-permute-start.66 = (bf16[448,608]{1,0:T(8,128)(2,1)S(1)}, bf16[448,608]{1,0:T(8,128)(2,1)}, u32[]{:S(2)}, u32[]{:S(2)}) collective-permute-start(bf16[448,608]{1,0:T(8,128)(2,1)S(1)} %shard_map.200.rest_0_), channel_id=1, source_target_pairs={{0,1},{1,0},{2,3},{3,2},{4,5},{5,4},{6,7},{7,6},{8,9},{9,8},{10,11... | collective-permute-start | bytes 1634312 | tf_op jit(solution)/shard_map/ppermute | solution.py:28
  285.8 12.4 %collective-permute-start.67 = (bf16[448,608]{1,0:T(8,128)(2,1)S(1)}, bf16[448,608]{1,0:T(8,128)(2,1)}, u32[]{:S(2)}, u32[]{:S(2)}) collective-permute-start(bf16[448,608]{1,0:T(8,128)(2,1)S(1)} %shard_map.201.rest_1_), channel_id=1, source_target_pairs={{0,1},{1,0},{2,3},{3,2},{4,5},{5,4},{6,7},{7,6},{8,9},{9,8},{10,11... | collective-permute-start | bytes 1634312 | tf_op jit(solution)/shard_map/ppermute | solution.py:28
  285.8 12.4 %collective-permute-start.68 = (bf16[448,608]{1,0:T(8,128)(2,1)S(1)}, bf16[448,608]{1,0:T(8,128)(2,1)}, u32[]{:S(2)}, u32[]{:S(2)}) collective-permute-start(bf16[448,608]{1,0:T(8,128)(2,1)S(1)} %shard_map.202.rest_2_), channel_id=1, source_target_pairs={{0,1},{1,0},{2,3},{3,2},{4,5},{5,4},{6,7},{7,6},{8,9},{9,8},{10,11... | collective-permute-start | bytes 1634312 | tf_op jit(solution)/shard_map/ppermute | solution.py:28
  288.5 16.1 %collective-permute-start.50 = (bf16[1864,128]{1,0:T(8,128)(2,1)}, bf16[1864,128]{1,0:T(8,128)(2,1)}, u32[]{:S(2)}, u32[]{:S(2)}) collective-permute-start(bf16[1864,128]{1,0:T(8,128)(2,1)} %shard_map.197.mine), channel_id=1, source_target_pairs={{0,1},{1,0},{2,3},{3,2},{4,5},{5,4},{6,7},{7,6},{8,9},{9,8},{10,11... | collective-permute-start | bytes 1431560 | tf_op jit(solution)/shard_map/ppermute | solution.py:28
  (50 other events, 464.2 us)
where the time goes:
time: 309 us; the launch traced here: 308 us
  waiting for transfers between devices  150 us (49%)
  starting transfers between devices  82.7 us (27%)
  Pallas kernels  55.9 us (18%)
  local copies, waits for them, and re-layouts  14.5 us (5%)
  other arithmetic  3.79 us (1%)
    ppermute x21, waiting for transfers between devices, hop(): return lax.ppermute(value, 'replica', links)  88.8 us
    pallas_call x22, Pallas kernels, call(): pl.pallas_call(kernel, out_shape=outs, in_specs=[pl.BlockSpec(memory_spac...  55.9 us
    ppermute x30, waiting for transfers between devices, shard_swap(): return lax.ppermute(x, 'shard', [(i, i ^ k) for i in range(n)])  55.3 us
    ppermute x30, starting transfers between devices, shard_swap(): return lax.ppermute(x, 'shard', [(i, i ^ k) for i in range(n)])  38.1 us
    ppermute x21, starting transfers between devices, hop(): return lax.ppermute(value, 'replica', links)  37.8 us
    unnamed x40, local copies, waits for them, and re-layouts  7.91 us
  transfers between devices with their start and end apart: 78, of which 29 were waited for; matrix products, arithmetic and copies ran while one was open for 3% of the time, Pallas kernels for 11%

commit v1 on v0

--- a/solution.py
+++ b/solution.py
@@ -74,7 +74,7 @@
     return lax.dot_general(a, b, (((0,), (0,)), ((), ())), preferred_element_type=F32)
 
 
-GRANTS = {'pack': 12, 'attend': 3, 'mix': 4, 'down_back': 5, 'feed': 9, 'narrow': 4, 'back': 18, 'wide': 8, 'merge': 5, 'finish': 4, 'lay': 18, 'close': 6, 'ydown': 4, 'yout': 4, 'pick': 4, 'stack': 8}
+GRANTS = {'pack': 12, 'attend': 3, 'mix': 4, 'down_back': 5, 'feed': 9, 'narrow': 4, 'back': 18, 'wide': 8, 'merge': 5, 'finish': 4, 'lay': 18, 'close': 6, 'ydown': 4, 'open': 3, 'yout': 4, 'pick': 4, 'stack': 8}
 
 
 def call(kernel, name, outs, where, args, scratch=(), flops=0, space=pltpu.VMEM):
@@ -143,6 +143,27 @@
     )
 
 
+def open_kernel(where, w, g1, g2, b, block, extra):
+    half = w.shape[0] // 2
+    width = w.shape[1]
+    block[:half] = w[rows_at(where[1] * half, half)]
+    line = lax.broadcasted_iota(jnp.int32, extra.shape, 0)
+    value = jnp.zeros(extra.shape, F32)
+    for i, ref in enumerate((g1, g2, b)):
+        row = ref[...].astype(F32)[None]
+        row = jnp.concatenate([row, jnp.zeros((1, width - row.shape[1]), F32)], axis=1)
+        value = jnp.where(line == i, row, value)
+    extra[...] = value.astype(BF)
+    block[half:] = value.astype(BF)
+
+
+def open_rows(where, w, g1, g2, b):
+    half, width = w.shape[0] // 2, w.shape[1]
+    return call(
+        open_kernel, "open", [shape((half + 8, width)), shape((8, width))], where, [w, g1, g2, b]
+    )
+
+
 def place_rows(dst, s, c, own, mine, other):
     rows = own.shape[0]
     half = rows // 2
@@ -172,15 +193,18 @@
 
 def attend_kernel(shards, where, x, seg, own, extra, *rest):
     n = shards - 1
-    vectors, mine, other = rest[:n], rest[n : 2 * n], rest[2 * n : 3 * n]
+    riders, mine, other = rest[:n], rest[n : 2 * n], rest[2 * n : 3 * n]
     n1_ref, q_ref, k_ref, v_ref, p_ref, o_ref, w_ref, vec_ref, cos_ref, sin_ref = rest[3 * n :]
     s, c = where[0], where[1]
     width, joined_width = x.shape[1], own.shape[1]
     place_rows(w_ref, s, c, own, mine, other)
-    is_gain = lax.broadcasted_iota(jnp.int32, extra.shape, 0) < 2
-    vec = jnp.zeros(extra.shape, F32)
-    for k, piece in enumerate((extra,) + tuple(vectors)):
-        value = piece[...].astype(F32)
+    lines = extra.shape[0]
+    is_gain = lax.broadcasted_iota(jnp.int32, vec_ref.shape, 0) < 2
+    vec = jnp.zeros(vec_ref.shape, F32)
+    gap = jnp.zeros((lines, joined_width - width), F32)
+    for k, piece in enumerate((extra,) + tuple(riders)):
+        value = piece[piece.shape[0] - lines :].astype(F32)
+        value = jnp.concatenate([value, gap], axis=1)
         gains = pltpu.roll(value, (s ^ k) * (width // shards), 1)
         biases = pltpu.roll(value, (s ^ k) * (joined_width // shards), 1)
         vec = vec + jnp.where(is_gain, gains, biases)
@@ -237,18 +261,18 @@
         o_ref[:, i * LANES : (i + 1) * LANES] = mixed.astype(BF)
 
 
-def attend(where, x, seg, own, vectors, mine, other, shards):
+def attend(where, x, seg, own, extra, riders, mine, other, shards):
     tokens, width = x.shape
     joined = own.shape[1]
     outs = [
         shape((tokens, width)), shape((tokens, width)), shape((tokens, LANES)),
         shape((tokens, LANES)), shape((QUERY_HEADS, tokens, tokens), F32),
-        shape((tokens, width)), shape((width, joined)), shape(vectors[0].shape, F32),
+        shape((tokens, width)), shape((width, joined)), shape((extra.shape[0], joined), F32),
         shape((tokens, LANES), F32), shape((tokens, LANES), F32),
     ]
     return call(
         functools.partial(attend_kernel, shards), "attend", outs, where,
-        [x, seg, own, *vectors, *mine, *other],
+        [x, seg, own, extra, *riders, *mine, *other],
         flops=2 * tokens * width * joined + 8 * QUERY_HEADS * tokens * tokens * LANES,
     )
 
@@ -654,7 +678,7 @@
     replica = lax.axis_index("replica")
     core = replica & 1
     where = jnp.stack([shard, core, replica >> 1]).astype(jnp.int32)
-    count, width = tokens.shape
+    _, width = tokens.shape
     rows = norm1_gain.shape[0]
     half_rows = rows // 2
     joined = w_qkv.shape[1]
@@ -662,17 +686,14 @@
     slab = w_gate.shape[1] // (2 * shards)
     half = lax.dynamic_slice_in_dim(w_qkv, core * half_rows, half_rows, 0)
     qkv_mine = spread(half)[1:]
-    vectors = [
-        jnp.pad(v[None], ((0, 0), (0, joined - v.shape[0])))
-        for v in (norm1_gain, norm2_gain, b_qkv)
-    ]
-    vectors = jnp.concatenate(vectors + [jnp.zeros((5, joined), BF)], axis=0)
-    vectors = spread(vectors)
     qkv_other = [swap_core(p) for p in qkv_mine]
-    out_mine = spread(lax.dynamic_slice_in_dim(w_out, core * half_rows, half_rows, 0))[1:]
+    out_block, extra = open_rows(where, w_out, norm1_gain, norm2_gain, b_qkv)
+    out_mine = spread(out_block)[1:]
     out_other = [swap_core(p) for p in out_mine]
 
-    packed = pack(where, w_gate, w_up, shards)
+    packed = pack(
+        where, *(pltpu.with_memory_space_constraint(w, pltpu.HBM) for w in (w_gate, w_up)), shards
+    )
     direct = [shard_swap(packed[k], k) for k in range(1, shards)]
     passed = [pair_swap(w) for w in direct]
     dy = spread(cotangent)
@@ -680,7 +701,7 @@
 
     n_one, query, keys, values, probs, mixed, wqkv, vec, cosine, sine = attend(
         where, tokens, seg_ids,
-        w_qkv, vectors, qkv_mine, qkv_other, shards,
+        w_qkv, extra, out_mine, qkv_mine, qkv_other, shards,
     )
     hidden, n_two, wout = mix(where, tokens, mixed, vec, w_out, out_mine, out_other, shards)
     n_parts = spread(n_two)
@@ -694,12 +715,9 @@
 
     def plane_sum(keep, give):
         arrived = swap_core(give)
-        total = keep + arrived.astype(F32)
-        parts = [total[:count]]
-        for k in range(1, shards):
-            send = total[k * count : (k + 1) * count].astype(BF)
-            parts.append(shard_swap(send, k))
-        return parts
+        parts = (shards, -1, keep.shape[-1])
+        total = merge(where, keep.reshape(parts), arrived.reshape(parts))
+        return [total[0]] + [shard_swap(total[k], k) for k in range(1, shards)]
 
     dn = plane_sum(*narrow(where, d_gate, d_up, wgate, wup))
 
@@ -716,8 +734,7 @@
         where, dn, hidden, cotangent, tokens, vec, wout, wqkv, mixed, n_one, query, keys, values,
         probs, cosine, sine,
     )
-    parts = merge(where, keep, swap_core(give))
-    parts = [parts[0]] + [shard_swap(parts[k], k) for k in range(1, shards)]
+    parts = plane_sum(keep, give)
     tall, _ = layout_of(width, joined, rows)
     item = line_sum(where, finish(where, parts))
     qkv_part, out_part, vec_grads = close(where, item, swap_core(item), rows, width, joined, tall)

time: 309 us -> 316 us (1.023)
  waiting for transfers between devices: 150 us -> 160 us
  local copies, waits for them, and re-layouts: 14.5 us -> 11 us
  Pallas kernels: 55.9 us -> 59.1 us
    ppermute x21, waiting for transfers between devices: 88.8 us -> 97.5 us  [hop(): return lax.ppermute(value, 'replica', links)]
    ppermute x21, starting transfers between devices: 37.8 us -> 33.8 us  [hop(): return lax.ppermute(value, 'replica', links)]
    pallas_call x22 -> x25, Pallas kernels: 55.9 us -> 59.1 us  [call(): pl.pallas_call(kernel, out_shape=outs, in_specs=[pl.BlockSpec(memory_spac...]
    ppermute x30 -> x27, starting transfers between devices: 38.1 us -> 40.9 us  [shard_swap(): return lax.ppermute(x, 'shard', [(i, i ^ k) for i in range(n)])]
    ppermute x30 -> x27, waiting for transfers between devices: 55.3 us -> 56.6 us  [shard_swap(): return lax.ppermute(x, 'shard', [(i, i ^ k) for i in range(n)])]
    unnamed x40 -> x48, local copies, waits for them, and re-layouts: 7.91 us -> 8.71 us
  transfers between devices with their start and end apart: 78 -> 75, of which waited for: 29 -> 31; matrix products, arithmetic and copies ran while one was open for 3% -> 1% of each run, Pallas kernels for 11% -> 12%
where the time goes in v1:
time: 316 us; the launch traced here: 315 us
  waiting for transfers between devices  160 us (51%)
  starting transfers between devices  82 us (26%)
  Pallas kernels  59.1 us (19%)
  local copies, waits for them, and re-layouts  11 us (3%)
    ppermute x21, waiting for transfers between devices, hop(): return lax.ppermute(value, 'replica', links)  97.5 us
    pallas_call x25, Pallas kernels, call(): pl.pallas_call(kernel, out_shape=outs, in_specs=[pl.BlockSpec(memory_spac...  59.1 us
    ppermute x27, waiting for transfers between devices, shard_swap(): return lax.ppermute(x, 'shard', [(i, i ^ k) for i in range(n)])  56.6 us
    ppermute x27, starting transfers between devices, shard_swap(): return lax.ppermute(x, 'shard', [(i, i ^ k) for i in range(n)])  40.9 us
    ppermute x21, starting transfers between devices, hop(): return lax.ppermute(value, 'replica', links)  33.8 us
    unnamed x48, local copies, waits for them, and re-layouts  8.71 us
  transfers between devices with their start and end apart: 75, of which 31 were waited for; matrix products, arithmetic and copies ran while one was open for 1% of the time, Pallas kernels for 12%

profile of v1, /device:TPU:0, one launch (start us, length us, event | category | flops | bytes accessed | tf_op | source)
XLA Modules:
  0.0 315.4 jit_solution(7280253390853123790)
XLA Ops:
  4.3 3.0 collective-permute-start
  8.9 1.9 collective-permute-start.12
  13.5 3.0 collective-permute-start.14
  16.4 3.7 %collective-permute-done.1.rest_1_ = bf16[120,896]{1,0:T(8,128)(2,1)S(1)} collective-permute-done((bf16[120,896]{1,0:T(8,128)(2,1)S(1)}, bf16[120,896]{1,0:T(8,128)(2,1)S(1)}, u32[]{:S(2)}, u32[]{:S(2)}) %collective-permute-start.1) | collective-permute-done | bytes 215072 | tf_op jit(solution)/shard_map/ppermute | solution.py:33
  21.2 1.9 collective-permute-done.12.rest_1_
  23.1 2.0 collective-permute-start.4
  25.2 3.8 %collective-permute-done.13.rest_2_ = bf16[128,896]{1,0:T(8,128)(2,1)} collective-permute-done((bf16[128,896]{1,0:T(8,128)(2,1)}, bf16[128,896]{1,0:T(8,128)(2,1)}, u32[]{:S(2)}, u32[]{:S(2)}) %collective-permute-start.13) | collective-permute-done | bytes 229408 | tf_op jit(solution)/shard_map/ppermute | solution.py:33
  29.5 3.2 %shard_map.190 = (bf16[448,608]{1,0:T(8,128)(2,1)S(1)}, bf16[224,608]{1,0:T(8,128)(2,1)S(1)}, bf16[224,608]{1,0:T(8,128)(2,1)S(1)}, bf16[224,608]{1,0:T(8,128)(2,1)S(1)}) custom-call(s32[3]{0:T(128)S(1)} %pad_add_fusion.where, bf16[224,4864]{1,0:T(8,128)(2,1)} %gate.1, bf16[224,4864]{1,0:T(8,128)(2,1)} %up.1), custom_call_target="tpu_custom_call" | custom-call | bytes 5720064 | tf_op jit(solution)/shard_map/pallas_call | solution.py:85
  32.7 3.5 %collective-permute-start.26 = (bf16[224,608]{1,0:T(8,128)(2,1)S(1)}, bf16[224,608]{1,0:T(8,128)(2,1)S(1)}, u32[]{:S(2)}, u32[]{:S(2)}) collective-permute-start(bf16[224,608]{1,0:T(8,128)(2,1)S(1)} %get-tuple-element.76), channel_id=1, source_target_pairs={{0,8},{8,0},{16,24},{24,16},{1,9},{9,1},{17,25},{25,17},{2,10},{10... | collective-permute-start | bytes 817160 | tf_op jit(solution)/shard_map/ppermute | solution.py:33
  37.8 2.2 collective-permute-done.4.rest_4_
  40.6 5.6 %collective-permute-done.26.rest_9_ = bf16[224,608]{1,0:T(8,128)(2,1)S(1)} collective-permute-done((bf16[224,608]{1,0:T(8,128)(2,1)S(1)}, bf16[224,608]{1,0:T(8,128)(2,1)S(1)}, u32[]{:S(2)}, u32[]{:S(2)}) %collective-permute-start.26) | collective-permute-done | bytes 272416 | tf_op jit(solution)/shard_map/ppermute | solution.py:33
  46.2 5.7 %collective-permute-done.27.rest_10_ = bf16[224,608]{1,0:T(8,128)(2,1)S(1)} collective-permute-done((bf16[224,608]{1,0:T(8,128)(2,1)S(1)}, bf16[224,608]{1,0:T(8,128)(2,1)S(1)}, u32[]{:S(2)}, u32[]{:S(2)}) %collective-permute-start.27) | collective-permute-done | bytes 272416 | tf_op jit(solution)/shard_map/ppermute | solution.py:33
  55.9 4.3 %shard_map.187 = (bf16[128,896]{1,0:T(8,128)(2,1)S(1)}, bf16[128,896]{1,0:T(8,128)(2,1)S(1)}, bf16[128,128]{1,0:T(8,128)(2,1)S(1)}, bf16[128,128]{1,0:T(8,128)(2...) custom-call(s32[3]{0:T(128)S(1)} %pad_add_fusion.where, ...), custom_call_target="tpu_custom_call" | custom-call | flops 499122176 | bytes 6857216 | tf_op jit(solution)/shard_map/pallas_call | solution.py:85
  66.6 3.1 collective-permute-done.30.rest_13_
  70.2 2.8 collective-permute-done.20.rest_2_
  73.0 1.6 collective-permute-done.21.rest_3_
  74.6 3.8 %shard_map.189 = (f32[1024,608]{1,0:T(8,128)S(1)}, bf16[1024,896]{1,0:T(8,128)(2,1)S(1)}) custom-call(s32[3]{0:T(128)S(1)} %pad_add_fusion.where, bf16[1216,896]{1,0:T(8,128)(2,1)S(1)} %copy-done.23, bf16[128,896]{1,0:T(8,128)(2,1)S(1)} %copy-done.12, bf16[128,896]{1,0:T(8,128)(2,1)} %collective-permute-done.12.rest_1_, ...), custom_call_target="tpu_custom_call" | custom-call | flops 1115684864 | bytes 8339456 | tf_op jit(solution)/shard_map/pallas_call | solution.py:85
  78.4 6.9 %shard_map.191 = (bf16[304,896]{1,0:T(8,128)(2,1)S(1)}, bf16[304,896]{1,0:T(8,128)(2,1)S(1)}, bf16[1024,608]{1,0:T(8,128)(2,1)S(1)}, bf16[1024,608]{1,0:T(8,128)...) custom-call(s32[3]{0:T(128)S(1)} %pad_add_fusion.where, ...), custom_call_target="tpu_custom_call" | custom-call | flops 3347054592 | bytes 17178624 | tf_op jit(solution)/shard_map/pallas_call | solution.py:85
  85.3 4.6 %shard_map.195 = (f32[512,896]{1,0:T(8,128)S(1)}, bf16[512,896]{1,0:T(8,128)(2,1)S(1)}) custom-call(s32[3]{0:T(128)S(1)} %pad_add_fusion.where, bf16[1024,608]{1,0:T(8,128)(2,1)S(1)} %get-tuple-element.86.dgate, bf16[1024,608]{1,0:T(8,128)(2,1)S(1)} %get-tuple-element.87.dup, bf16[896,608]{1,0:T(8,128)(2,1)S(1)} %get-tuple-element.88.wg, ...), custom_call_target="tpu_custom_call" | custom-call | flops 2231369728 | bytes 7421952 | tf_op jit(solution)/shard_map/pallas_call | solution.py:85
  90.5 2.1 collective-permute-done.36
  96.9 5.0 %collective-permute-done.37.rest_1_ = bf16[128,896]{1,0:T(8,128)(2,1)S(1)} collective-permute-done((bf16[128,896]{1,0:T(8,128)(2,1)S(1)}, bf16[128,896]{1,0:T(8,128)(2,1)S(1)}, u32[]{:S(2)}, u32[]{:S(2)}) %collective-permute-start.37) | collective-permute-done | bytes 229408 | tf_op jit(solution)/shard_map/ppermute | solution.py:33
  101.8 5.0 %collective-permute-done.38.rest_2_ = bf16[128,896]{1,0:T(8,128)(2,1)S(1)} collective-permute-done((bf16[128,896]{1,0:T(8,128)(2,1)S(1)}, bf16[128,896]{1,0:T(8,128)(2,1)S(1)}, u32[]{:S(2)}, u32[]{:S(2)}) %collective-permute-start.38) | collective-permute-done | bytes 229408 | tf_op jit(solution)/shard_map/ppermute | solution.py:33
  106.8 7.0 %shard_map.197 = (f32[128,896]{1,0:T(8,128)}, f32[4,1864,128]{2,1,0:T(8,128)S(1)}, bf16[4,1864,128]{2,1,0:T(8,128)(2,1)S(1)}) custom-call(s32[3]{0:T(128)S(1)} %pad_add_fusion.where, f32[128,896]{1,0:T(8,128)S(1)} %get-tuple-element.92.rest_0_, bf16[128,896]{1,0:T(8,128)(2,1)S(1)} %collective-permute-done.37.rest_1_, ...), custom_call_target="tpu_custom_call" | custom-call | flops 939524096 | bytes 13758464 | tf_op jit(solution)/shard_map/pallas_call | solution.py:85
  113.9 3.8 %shard_map.202 = (bf16[448,608]{1,0:T(8,128)(2,1)S(1)}, bf16[448,608]{1,0:T(8,128)(2,1)S(1)}, bf16[448,608]{1,0:T(8,128)(2,1)S(1)}, bf16[448,608]{1,0:T(8,128)(2,1)S(1)}) custom-call(s32[3]{0:T(128)S(1)} %pad_add_fusion.where, bf16[1024,896]{1,0:T(8,128)(2,1)S(1)} %get-tuple-element.115.n, bf16[1024,608]{1,0:T(8,128)(2,1)S(1)} %get-tuple-element.86.dgate, ...), custom_call_target="tpu_custom_call" | custom-call | flops 2231369728 | bytes 6504448 | tf_op jit(solution)/shard_map/pallas_call | solution.py:85
  117.7 3.4 %collective-permute-start.48 = (bf16[448,608]{1,0:T(8,128)(2,1)S(1)}, bf16[448,608]{1,0:T(8,128)(2,1)S(1)}, u32[]{:S(2)}, u32[]{:S(2)}) collective-permute-start(bf16[448,608]{1,0:T(8,128)(2,1)S(1)} %get-tuple-element.116), channel_id=1, source_target_pairs={{0,2},{1,3},{6,4},{7,5},{8,10},{9,11},{14,12},{15,13},{16,18},{17,... | collective-permute-start | bytes 1634312 | tf_op jit(solution)/shard_map/ppermute | solution.py:51
  123.2 2.6 shard_map.192
  125.9 8.1 %collective-permute-done.48 = bf16[448,608]{1,0:T(8,128)(2,1)S(1)} collective-permute-done((bf16[448,608]{1,0:T(8,128)(2,1)S(1)}, bf16[448,608]{1,0:T(8,128)(2,1)S(1)}, u32[]{:S(2)}, u32[]{:S(2)}) %collective-permute-start.48) | collective-permute-done | bytes 544800 | tf_op jit(solution)/shard_map/ppermute | solution.py:51
  136.3 3.6 %collective-permute-start.67 = (bf16[304,896]{1,0:T(8,128)(2,1)S(1)}, bf16[304,896]{1,0:T(8,128)(2,1)S(1)}, u32[]{:S(2)}, u32[]{:S(2)}) collective-permute-start(bf16[304,896]{1,0:T(8,128)(2,1)S(1)} %get-tuple-element.122), channel_id=1, source_target_pairs={{0,2},{1,3},{6,4},{7,5},{8,10},{9,11},{14,12},{15,13},{16,18},{17,... | collective-permute-start | bytes 1634312 | tf_op jit(solution)/shard_map/ppermute | solution.py:51
  143.3 6.3 %collective-permute-done.59 = bf16[448,608]{1,0:T(8,128)(2,1)S(1)} collective-permute-done((bf16[448,608]{1,0:T(8,128)(2,1)S(1)}, bf16[448,608]{1,0:T(8,128)(2,1)S(1)}, u32[]{:S(2)}, u32[]{:S(2)}) %collective-permute-start.59) | collective-permute-done | bytes 544800 | tf_op jit(solution)/shard_map/ppermute | solution.py:33
  149.5 3.3 %collective-permute-start.41 = (bf16[1864,128]{1,0:T(8,128)(2,1)S(1)}, bf16[1864,128]{1,0:T(8,128)(2,1)S(1)}, u32[]{:S(2)}, u32[]{:S(2)}) collective-permute-start(bf16[1864,128]{1,0:T(8,128)(2,1)S(1)} %get-tuple-element.109), channel_id=1, source_target_pairs={{0,8},{8,0},{16,24},{24,16},{1,9},{9,1},{17,25},{25,17},{2,10},{10... | collective-permute-start | bytes 1431560 | tf_op jit(solution)/shard_map/ppermute | solution.py:33
  152.9 2.4 collective-permute-start.42
  155.3 7.3 %collective-permute-done.70 = bf16[304,896]{1,0:T(8,128)(2,1)S(1)} collective-permute-done((bf16[304,896]{1,0:T(8,128)(2,1)S(1)}, bf16[304,896]{1,0:T(8,128)(2,1)S(1)}, u32[]{:S(2)}, u32[]{:S(2)}) %collective-permute-start.70) | collective-permute-done | bytes 544800 | tf_op jit(solution)/shard_map/ppermute | solution.py:51
  164.1 4.4 %collective-permute-start.52 = (bf16[448,608]{1,0:T(8,128)(2,1)S(1)}, bf16[448,608]{1,0:T(8,128)(2,1)S(1)}, u32[]{:S(2)}, u32[]{:S(2)}) collective-permute-start(bf16[448,608]{1,0:T(8,128)(2,1)S(1)} %collective-permute-done.51), channel_id=1, source_target_pairs={{0,2},{1,3},{6,4},{7,5},{8,10},{9,11},{14,12},{15,13},{16,18},{17,... | collective-permute-start | bytes 1634312 | tf_op jit(solution)/shard_map/ppermute | solution.py:51
  172.2 2.7 collective-permute-done.43.rest_2_
  176.4 5.4 %collective-permute-done.52 = bf16[448,608]{1,0:T(8,128)(2,1)S(1)} collective-permute-done((bf16[448,608]{1,0:T(8,128)(2,1)S(1)}, bf16[448,608]{1,0:T(8,128)(2,1)S(1)}, u32[]{:S(2)}, u32[]{:S(2)}) %collective-permute-start.52) | collective-permute-done | bytes 544800 | tf_op jit(solution)/shard_map/ppermute | solution.py:51
  181.8 4.4 %collective-permute-start.44 = (bf16[1864,128]{1,0:T(8,128)(2,1)S(1)}, bf16[1864,128]{1,0:T(8,128)(2,1)S(1)}, u32[]{:S(2)}, u32[]{:S(2)}) collective-permute-start(bf16[1864,128]{1,0:T(8,128)(2,1)S(1)} %shard_map.199), channel_id=1, source_target_pairs={{0,2},{1,3},{6,4},{7,5},{8,10},{9,11},{14,12},{15,13},{16,18},{17,... | collective-permute-start | bytes 1431560 | tf_op jit(solution)/shard_map/ppermute | solution.py:51
  186.5 7.6 %collective-permute-done.56 = bf16[448,608]{1,0:T(8,128)(2,1)S(1)} collective-permute-done((bf16[448,608]{1,0:T(8,128)(2,1)S(1)}, bf16[448,608]{1,0:T(8,128)(2,1)S(1)}, u32[]{:S(2)}, u32[]{:S(2)}) %collective-permute-start.56) | collective-permute-done | bytes 544800 | tf_op jit(solution)/shard_map/ppermute | solution.py:51
  195.4 11.0 %collective-permute-done.60 = bf16[448,608]{1,0:T(8,128)(2,1)S(1)} collective-permute-done((bf16[448,608]{1,0:T(8,128)(2,1)S(1)}, bf16[448,608]{1,0:T(8,128)(2,1)S(1)}, u32[]{:S(2)}, u32[]{:S(2)}) %collective-permute-start.60) | collective-permute-done | bytes 544800 | tf_op jit(solution)/shard_map/ppermute | solution.py:51
  210.2 4.6 %collective-permute-done.33.rest_1_ = bf16[128,896]{1,0:T(8,128)(2,1)S(1)} collective-permute-done((bf16[128,896]{1,0:T(8,128)(2,1)S(1)}, bf16[128,896]{1,0:T(8,128)(2,1)S(1)}, u32[]{:S(2)}, u32[]{:S(2)}) %collective-permute-start.33) | collective-permute-done | bytes 229408 | tf_op jit(solution)/shard_map/ppermute | solution.py:33
  222.3 17.6 %collective-permute-done.69.arrived = bf16[304,896]{1,0:T(8,128)(2,1)S(1)} collective-permute-done((bf16[304,896]{1,0:T(8,128)(2,1)S(1)}, bf16[304,896]{1,0:T(8,128)(2,1)S(1)}, u32[]{:S(2)}, u32[]{:S(2)}) %collective-permute-start.69) | collective-permute-done | bytes 544800 | tf_op jit(solution)/shard_map/ppermute | solution.py:51
  242.1 9.6 %collective-permute-done.72.arrived = bf16[304,896]{1,0:T(8,128)(2,1)S(1)} collective-permute-done((bf16[304,896]{1,0:T(8,128)(2,1)S(1)}, bf16[304,896]{1,0:T(8,128)(2,1)S(1)}, u32[]{:S(2)}, u32[]{:S(2)}) %collective-permute-start.72) | collective-permute-done | bytes 544800 | tf_op jit(solution)/shard_map/ppermute | solution.py:51
  253.5 10.4 %collective-permute-done.54.arrived = bf16[448,608]{1,0:T(8,128)(2,1)S(1)} collective-permute-done((bf16[448,608]{1,0:T(8,128)(2,1)S(1)}, bf16[448,608]{1,0:T(8,128)(2,1)S(1)}, u32[]{:S(2)}, u32[]{:S(2)}) %collective-permute-start.54) | collective-permute-done | bytes 544800 | tf_op jit(solution)/shard_map/ppermute | solution.py:51
  263.9 12.3 %collective-permute-done.58.arrived = bf16[448,608]{1,0:T(8,128)(2,1)S(1)} collective-permute-done((bf16[448,608]{1,0:T(8,128)(2,1)S(1)}, bf16[448,608]{1,0:T(8,128)(2,1)S(1)}, u32[]{:S(2)}, u32[]{:S(2)}) %collective-permute-start.58) | collective-permute-done | bytes 544800 | tf_op jit(solution)/shard_map/ppermute | solution.py:51
  277.8 8.1 %collective-permute-done.62.arrived = bf16[448,608]{1,0:T(8,128)(2,1)S(1)} collective-permute-done((bf16[448,608]{1,0:T(8,128)(2,1)S(1)}, bf16[448,608]{1,0:T(8,128)(2,1)S(1)}, u32[]{:S(2)}, u32[]{:S(2)}) %collective-permute-start.62) | collective-permute-done | bytes 544800 | tf_op jit(solution)/shard_map/ppermute | solution.py:51
  289.9 2.9 collective-permute-done.35.rest_3_
  302.2 2.9 shard_map.210
  305.1 6.4 %shard_map.207 = (f32[224,4864]{1,0:T(8,128)}, f32[224,4864]{1,0:T(8,128)}) custom-call(s32[3]{0:T(128)S(1)} %pad_add_fusion.where, bf16[448,608]{1,0:T(8,128)(2,1)S(1)} %shard_map.203.rest_0_, bf16[448,608]{1,0:T(8,128)(2,1)S(1)} %shard_map.204.rest_1_, bf16[448,608]{1,0:T(8,128)(2,1)S(1)} %shard_map.205.rest_2_, bf16[448,608]{1,0:T(8,128)(2,1)S(1)} %shard_map.206.rest_3_, ...), custom_call_target="tpu_custom_call" | custom-call | bytes 13074432 | tf_op jit(solution)/shard_map/pallas_call | solution.py:85
  311.6 2.5 shard_map.201
  (194 shorter events, 74.5 us)
Async XLA Ops:
  7.3 12.8 %collective-permute-start.1 = (bf16[120,896]{1,0:T(8,128)(2,1)S(1)}, bf16[120,896]{1,0:T(8,128)(2,1)S(1)}, u32[]{:S(2)}, u32[]{:S(2)}) collective-permute-start(bf16[120,896]{1,0:T(8,128)(2,1)S(1)} %get-tuple-element.68), channel_id=1, source_target_pairs={{0,16},{8,24},{16,0},{24,8},{1,17},{9,25},{17,1},{25,9},{2,18},{10... | collective-permute-start | bytes 645128 | tf_op jit(solution)/shard_map/ppermute | solution.py:33
  8.8 12.3 %collective-permute-start.2 = (bf16[120,896]{1,0:T(8,128)(2,1)S(1)}, bf16[120,896]{1,0:T(8,128)(2,1)S(1)}, u32[]{:S(2)}, u32[]{:S(2)}) collective-permute-start(bf16[120,896]{1,0:T(8,128)(2,1)S(1)} %get-tuple-element.68), channel_id=1, source_target_pairs={{0,24},{8,16},{16,8},{24,0},{1,25},{9,17},{17,9},{25,1},{2,26},{10... | collective-permute-start | bytes 645128 | tf_op jit(solution)/shard_map/ppermute | solution.py:33
  8.9 14.3 %collective-permute-start.12 = (bf16[128,896]{1,0:T(8,128)(2,1)}, bf16[128,896]{1,0:T(8,128)(2,1)}, u32[]{:S(2)}, u32[]{:S(2)}) collective-permute-start(bf16[128,896]{1,0:T(8,128)(2,1)} %rest_5_.1), channel_id=1, source_target_pairs={{0,8},{8,0},{16,24},{24,16},{1,9},{9,1},{17,25},{25,17},{2,10},{10... | collective-permute-start | bytes 688136 | tf_op jit(solution)/shard_map/ppermute | solution.py:33
  10.8 18.2 %collective-permute-start.13 = (bf16[128,896]{1,0:T(8,128)(2,1)}, bf16[128,896]{1,0:T(8,128)(2,1)}, u32[]{:S(2)}, u32[]{:S(2)}) collective-permute-start(bf16[128,896]{1,0:T(8,128)(2,1)} %rest_5_.1), channel_id=1, source_target_pairs={{0,16},{8,24},{16,0},{24,8},{1,17},{9,25},{17,1},{25,9},{2,18},{10... | collective-permute-start | bytes 688136 | tf_op jit(solution)/shard_map/ppermute | solution.py:33
  13.5 19.2 %collective-permute-start.14 = (bf16[128,896]{1,0:T(8,128)(2,1)}, bf16[128,896]{1,0:T(8,128)(2,1)S(1)}, u32[]{:S(2)}, u32[]{:S(2)}) collective-permute-start(bf16[128,896]{1,0:T(8,128)(2,1)} %rest_5_.1), channel_id=1, source_target_pairs={{0,24},{8,16},{16,8},{24,0},{1,25},{9,17},{17,9},{25,1},{2,26},{10... | collective-permute-start | bytes 688136 | tf_op jit(solution)/shard_map/ppermute | solution.py:33
  20.1 16.1 %collective-permute-start.15 = (bf16[128,896]{1,0:T(8,128)(2,1)}, bf16[128,896]{1,0:T(8,128)(2,1)S(1)}, u32[]{:S(2)}, u32[]{:S(2)}) collective-permute-start(bf16[128,896]{1,0:T(8,128)(2,1)} %rest_5_.1), channel_id=1, source_target_pairs={{0,1},{1,0},{2,3},{3,2},{4,5},{5,4},{6,7},{7,6},{8,9},{9,8},{10,11... | collective-permute-start | bytes 688136 | tf_op jit(solution)/shard_map/ppermute | solution.py:28
  21.1 15.1 %collective-permute-start.3 = (bf16[112,1152]{1,0:T(8,128)(2,1)S(1)}, bf16[112,1152]{1,0:T(8,128)(2,1)S(1)}, u32[]{:S(2)}, u32[]{:S(2)}) collective-permute-start(bf16[112,1152]{1,0:T(8,128)(2,1)S(1)} %constant_dynamic-slice_fusion.2), channel_id=1, source_target_pairs={{0,8},{8,0},{16,24},{24,16},{1,9},{9,1},{17,25},{25,17},{2,10},{10... | collective-permute-start | bytes 774152 | tf_op jit(solution)/shard_map/ppermute | solution.py:33
  23.1 16.8 %collective-permute-start.4 = (bf16[112,1152]{1,0:T(8,128)(2,1)S(1)}, bf16[112,1152]{1,0:T(8,128)(2,1)S(1)}, u32[]{:S(2)}, u32[]{:S(2)}) collective-permute-start(bf16[112,1152]{1,0:T(8,128)(2,1)S(1)} %constant_dynamic-slice_fusion.2), channel_id=1, source_target_pairs={{0,16},{8,24},{16,0},{24,8},{1,17},{9,25},{17,1},{25,9},{2,18},{10... | collective-permute-start | bytes 774152 | tf_op jit(solution)/shard_map/ppermute | solution.py:33
  32.7 13.5 %collective-permute-start.26 = (bf16[224,608]{1,0:T(8,128)(2,1)S(1)}, bf16[224,608]{1,0:T(8,128)(2,1)S(1)}, u32[]{:S(2)}, u32[]{:S(2)}) collective-permute-start(bf16[224,608]{1,0:T(8,128)(2,1)S(1)} %get-tuple-element.76), channel_id=1, source_target_pairs={{0,8},{8,0},{16,24},{24,16},{1,9},{9,1},{17,25},{25,17},{2,10},{10... | collective-permute-start | bytes 817160 | tf_op jit(solution)/shard_map/ppermute | solution.py:33
  36.2 15.6 %collective-permute-start.27 = (bf16[224,608]{1,0:T(8,128)(2,1)S(1)}, bf16[224,608]{1,0:T(8,128)(2,1)S(1)}, u32[]{:S(2)}, u32[]{:S(2)}) collective-permute-start(bf16[224,608]{1,0:T(8,128)(2,1)S(1)} %get-tuple-element.77), channel_id=1, source_target_pairs={{0,16},{8,24},{16,0},{24,8},{1,17},{9,25},{17,1},{25,9},{2,18},{10... | collective-permute-start | bytes 817160 | tf_op jit(solution)/shard_map/ppermute | solution.py:33
  36.3 15.6 %collective-permute-start.28 = (bf16[224,608]{1,0:T(8,128)(2,1)S(1)}, bf16[224,608]{1,0:T(8,128)(2,1)S(1)}, u32[]{:S(2)}, u32[]{:S(2)}) collective-permute-start(bf16[224,608]{1,0:T(8,128)(2,1)S(1)} %get-tuple-element.78), channel_id=1, source_target_pairs={{0,24},{8,16},{16,8},{24,0},{1,25},{9,17},{17,9},{25,1},{2,26},{10... | collective-permute-start | bytes 817160 | tf_op jit(solution)/shard_map/ppermute | solution.py:33
  40.0 12.4 %collective-permute-start.9 = (bf16[120,896]{1,0:T(8,128)(2,1)S(1)}, bf16[120,896]{1,0:T(8,128)(2,1)S(1)}, u32[]{:S(2)}, u32[]{:S(2)}) collective-permute-start(bf16[120,896]{1,0:T(8,128)(2,1)S(1)} %collective-permute-done.rest_0_), channel_id=1, source_target_pairs={{0,1},{1,0},{2,3},{3,2},{4,5},{5,4},{6,7},{7,6},{8,9},{9,8},{10,11... | collective-permute-start | bytes 645128 | tf_op jit(solution)/shard_map/ppermute | solution.py:28
  40.6 12.9 %collective-permute-start.6 = (bf16[112,1152]{1,0:T(8,128)(2,1)S(1)}, bf16[112,1152]{1,0:T(8,128)(2,1)S(1)}, u32[]{:S(2)}, u32[]{:S(2)}) collective-permute-start(bf16[112,1152]{1,0:T(8,128)(2,1)S(1)} %collective-permute-done.3.rest_3_), channel_id=1, source_target_pairs={{0,1},{1,0},{2,3},{3,2},{4,5},{5,4},{6,7},{7,6},{8,9},{9,8},{10,11... | collective-permute-start | bytes 774152 | tf_op jit(solution)/shard_map/ppermute | solution.py:28
  55.4 14.3 %collective-permute-start.30 = (bf16[224,608]{1,0:T(8,128)(2,1)S(1)}, bf16[224,608]{1,0:T(8,128)(2,1)S(1)}, u32[]{:S(2)}, u32[]{:S(2)}) collective-permute-start(bf16[224,608]{1,0:T(8,128)(2,1)S(1)} %collective-permute-done.27.rest_10_), channel_id=1, source_target_pairs={{0,2},{1,3},{2,0},{3,1},{4,6},{5,7},{6,4},{7,5},{8,10},{9,11},{10,... | collective-permute-start | bytes 817160 | tf_op jit(solution)/shard_map/ppermute | solution.py:38
  65.0 13.4 %collective-permute-start.31 = (bf16[224,608]{1,0:T(8,128)(2,1)S(1)}, bf16[224,608]{1,0:T(8,128)(2,1)S(1)}, u32[]{:S(2)}, u32[]{:S(2)}) collective-permute-start(bf16[224,608]{1,0:T(8,128)(2,1)S(1)} %collective-permute-done.28.rest_11_), channel_id=1, source_target_pairs={{0,2},{1,3},{2,0},{3,1},{4,6},{5,7},{6,4},{7,5},{8,10},{9,11},{10,... | collective-permute-start | bytes 817160 | tf_op jit(solution)/shard_map/ppermute | solution.py:38
  94.5 12.3 %collective-permute-start.38 = (bf16[128,896]{1,0:T(8,128)(2,1)S(1)}, bf16[128,896]{1,0:T(8,128)(2,1)S(1)}, u32[]{:S(2)}, u32[]{:S(2)}) collective-permute-start(bf16[128,896]{1,0:T(8,128)(2,1)S(1)} %get-tuple-element.94), channel_id=1, source_target_pairs={{0,16},{8,24},{16,0},{24,8},{1,17},{9,25},{17,1},{25,9},{2,18},{10... | collective-permute-start | bytes 688136 | tf_op jit(solution)/shard_map/ppermute | solution.py:33
  113.9 27.5 %collective-permute-start.40 = (bf16[4,1864,128]{2,1,0:T(8,128)(2,1)S(1)}, bf16[4,1864,128]{2,1,0:T(8,128)(2,1)S(1)}, u32[]{:S(2)}, u32[]{:S(2)}) collective-permute-start(bf16[4,1864,128]{2,1,0:T(8,128)(2,1)S(1)} %get-tuple-element.107), channel_id=1, source_target_pairs={{0,1},{1,0},{2,3},{3,2},{4,5},{5,4},{6,7},{7,6},{8,9},{9,8},{10,11... | collective-permute-start | bytes 5726216 | tf_op jit(solution)/shard_map/ppermute | solution.py:28
  117.7 16.3 %collective-permute-start.48 = (bf16[448,608]{1,0:T(8,128)(2,1)S(1)}, bf16[448,608]{1,0:T(8,128)(2,1)S(1)}, u32[]{:S(2)}, u32[]{:S(2)}) collective-permute-start(bf16[448,608]{1,0:T(8,128)(2,1)S(1)} %get-tuple-element.116), channel_id=1, source_target_pairs={{0,2},{1,3},{6,4},{7,5},{8,10},{9,11},{14,12},{15,13},{16,18},{17,... | collective-permute-start | bytes 1634312 | tf_op jit(solution)/shard_map/ppermute | solution.py:51
  121.1 15.2 %collective-permute-start.51 = (bf16[448,608]{1,0:T(8,128)(2,1)S(1)}, bf16[448,608]{1,0:T(8,128)(2,1)S(1)}, u32[]{:S(2)}, u32[]{:S(2)}) collective-permute-start(bf16[448,608]{1,0:T(8,128)(2,1)S(1)} %get-tuple-element.117), channel_id=1, source_target_pairs={{0,8},{8,0},{16,24},{24,16},{1,9},{9,1},{17,25},{25,17},{2,10},{10... | collective-permute-start | bytes 1634312 | tf_op jit(solution)/shard_map/ppermute | solution.py:33
  122.4 17.5 %collective-permute-start.55 = (bf16[448,608]{1,0:T(8,128)(2,1)S(1)}, bf16[448,608]{1,0:T(8,128)(2,1)S(1)}, u32[]{:S(2)}, u32[]{:S(2)}) collective-permute-start(bf16[448,608]{1,0:T(8,128)(2,1)S(1)} %get-tuple-element.118), channel_id=1, source_target_pairs={{0,16},{8,24},{16,0},{24,8},{1,17},{9,25},{17,1},{25,9},{2,18},{10... | collective-permute-start | bytes 1634312 | tf_op jit(solution)/shard_map/ppermute | solution.py:33
  125.8 38.3 %collective-permute-start.32 = (bf16[512,896]{1,0:T(8,128)(2,1)S(1)}, bf16[512,896]{1,0:T(8,128)(2,1)S(1)}, u32[]{:S(2)}, u32[]{:S(2)}) collective-permute-start(bf16[512,896]{1,0:T(8,128)(2,1)S(1)} %get-tuple-element.81), channel_id=1, source_target_pairs={{0,1},{1,0},{2,3},{3,2},{4,5},{5,4},{6,7},{7,6},{8,9},{9,8},{10,11... | collective-permute-start | bytes 2752520 | tf_op jit(solution)/shard_map/ppermute | solution.py:28
  134.0 15.6 %collective-permute-start.59 = (bf16[448,608]{1,0:T(8,128)(2,1)S(1)}, bf16[448,608]{1,0:T(8,128)(2,1)S(1)}, u32[]{:S(2)}, u32[]{:S(2)}) collective-permute-start(bf16[448,608]{1,0:T(8,128)(2,1)S(1)} %get-tuple-element.119), channel_id=1, source_target_pairs={{0,24},{8,16},{16,8},{24,0},{1,25},{9,17},{17,9},{25,1},{2,26},{10... | collective-permute-start | bytes 1634312 | tf_op jit(solution)/shard_map/ppermute | solution.py:33
  136.3 16.6 %collective-permute-start.67 = (bf16[304,896]{1,0:T(8,128)(2,1)S(1)}, bf16[304,896]{1,0:T(8,128)(2,1)S(1)}, u32[]{:S(2)}, u32[]{:S(2)}) collective-permute-start(bf16[304,896]{1,0:T(8,128)(2,1)S(1)} %get-tuple-element.122), channel_id=1, source_target_pairs={{0,2},{1,3},{6,4},{7,5},{8,10},{9,11},{14,12},{15,13},{16,18},{17,... | collective-permute-start | bytes 1634312 | tf_op jit(solution)/shard_map/ppermute | solution.py:51
  139.9 22.8 %collective-permute-start.70 = (bf16[304,896]{1,0:T(8,128)(2,1)S(1)}, bf16[304,896]{1,0:T(8,128)(2,1)S(1)}, u32[]{:S(2)}, u32[]{:S(2)}) collective-permute-start(bf16[304,896]{1,0:T(8,128)(2,1)S(1)} %get-tuple-element.123), channel_id=1, source_target_pairs={{0,2},{1,3},{6,4},{7,5},{8,10},{9,11},{14,12},{15,13},{16,18},{17,... | collective-permute-start | bytes 1634312 | tf_op jit(solution)/shard_map/ppermute | solution.py:51
  141.4 27.1 %collective-permute-start.49 = (bf16[448,608]{1,0:T(8,128)(2,1)S(1)}, bf16[448,608]{1,0:T(8,128)(2,1)S(1)}, u32[]{:S(2)}, u32[]{:S(2)}) collective-permute-start(bf16[448,608]{1,0:T(8,128)(2,1)S(1)} %add.57), channel_id=1, source_target_pairs={{2,4},{3,5},{4,2},{5,3},{10,12},{11,13},{12,10},{13,11},{18,20},{1... | collective-permute-start | bytes 1634312 | tf_op jit(solution)/shard_map/ppermute | solution.py:51
  149.5 20.3 %collective-permute-start.41 = (bf16[1864,128]{1,0:T(8,128)(2,1)S(1)}, bf16[1864,128]{1,0:T(8,128)(2,1)S(1)}, u32[]{:S(2)}, u32[]{:S(2)}) collective-permute-start(bf16[1864,128]{1,0:T(8,128)(2,1)S(1)} %get-tuple-element.109), channel_id=1, source_target_pairs={{0,8},{8,0},{16,24},{24,16},{1,9},{9,1},{17,25},{25,17},{2,10},{10... | collective-permute-start | bytes 1431560 | tf_op jit(solution)/shard_map/ppermute | solution.py:33
  152.9 18.5 %collective-permute-start.42 = (bf16[1864,128]{1,0:T(8,128)(2,1)S(1)}, bf16[1864,128]{1,0:T(8,128)(2,1)S(1)}, u32[]{:S(2)}, u32[]{:S(2)}) collective-permute-start(bf16[1864,128]{1,0:T(8,128)(2,1)S(1)} %get-tuple-element.110), channel_id=1, source_target_pairs={{0,16},{8,24},{16,0},{24,8},{1,17},{9,25},{17,1},{25,9},{2,18},{10... | collective-permute-start | bytes 1431560 | tf_op jit(solution)/shard_map/ppermute | solution.py:33
  164.1 17.7 %collective-permute-start.52 = (bf16[448,608]{1,0:T(8,128)(2,1)S(1)}, bf16[448,608]{1,0:T(8,128)(2,1)S(1)}, u32[]{:S(2)}, u32[]{:S(2)}) collective-permute-start(bf16[448,608]{1,0:T(8,128)(2,1)S(1)} %collective-permute-done.51), channel_id=1, source_target_pairs={{0,2},{1,3},{6,4},{7,5},{8,10},{9,11},{14,12},{15,13},{16,18},{17,... | collective-permute-start | bytes 1634312 | tf_op jit(solution)/shard_map/ppermute | solution.py:51
  168.5 25.6 %collective-permute-start.56 = (bf16[448,608]{1,0:T(8,128)(2,1)S(1)}, bf16[448,608]{1,0:T(8,128)(2,1)S(1)}, u32[]{:S(2)}, u32[]{:S(2)}) collective-permute-start(bf16[448,608]{1,0:T(8,128)(2,1)S(1)} %collective-permute-done.55), channel_id=1, source_target_pairs={{0,2},{1,3},{6,4},{7,5},{8,10},{9,11},{14,12},{15,13},{16,18},{17,... | collective-permute-start | bytes 1634312 | tf_op jit(solution)/shard_map/ppermute | solution.py:51
  169.9 36.5 %collective-permute-start.60 = (bf16[448,608]{1,0:T(8,128)(2,1)S(1)}, bf16[448,608]{1,0:T(8,128)(2,1)S(1)}, u32[]{:S(2)}, u32[]{:S(2)}) collective-permute-start(bf16[448,608]{1,0:T(8,128)(2,1)S(1)} %collective-permute-done.59), channel_id=1, source_target_pairs={{0,2},{1,3},{6,4},{7,5},{8,10},{9,11},{14,12},{15,13},{16,18},{17,... | collective-permute-start | bytes 1634312 | tf_op jit(solution)/shard_map/ppermute | solution.py:51
  171.4 35.9 %collective-permute-start.68 = (bf16[304,896]{1,0:T(8,128)(2,1)S(1)}, bf16[304,896]{1,0:T(8,128)(2,1)S(1)}, u32[]{:S(2)}, u32[]{:S(2)}) collective-permute-start(bf16[304,896]{1,0:T(8,128)(2,1)S(1)} %add.65), channel_id=1, source_target_pairs={{2,4},{3,5},{4,2},{5,3},{10,12},{11,13},{12,10},{13,11},{18,20},{1... | collective-permute-start | bytes 1634312 | tf_op jit(solution)/shard_map/ppermute | solution.py:51
  174.9 33.8 %collective-permute-start.71 = (bf16[304,896]{1,0:T(8,128)(2,1)S(1)}, bf16[304,896]{1,0:T(8,128)(2,1)S(1)}, u32[]{:S(2)}, u32[]{:S(2)}) collective-permute-start(bf16[304,896]{1,0:T(8,128)(2,1)S(1)} %add.67), channel_id=1, source_target_pairs={{2,4},{3,5},{4,2},{5,3},{10,12},{11,13},{12,10},{13,11},{18,20},{1... | collective-permute-start | bytes 1634312 | tf_op jit(solution)/shard_map/ppermute | solution.py:51
  181.8 33.8 %collective-permute-start.44 = (bf16[1864,128]{1,0:T(8,128)(2,1)S(1)}, bf16[1864,128]{1,0:T(8,128)(2,1)S(1)}, u32[]{:S(2)}, u32[]{:S(2)}) collective-permute-start(bf16[1864,128]{1,0:T(8,128)(2,1)S(1)} %shard_map.199), channel_id=1, source_target_pairs={{0,2},{1,3},{6,4},{7,5},{8,10},{9,11},{14,12},{15,13},{16,18},{17,... | collective-permute-start | bytes 1431560 | tf_op jit(solution)/shard_map/ppermute | solution.py:51
  194.1 23.1 %collective-permute-start.50 = (bf16[448,608]{1,0:T(8,128)(2,1)S(1)}, bf16[448,608]{1,0:T(8,128)(2,1)S(1)}, u32[]{:S(2)}, u32[]{:S(2)}) collective-permute-start(bf16[448,608]{1,0:T(8,128)(2,1)S(1)} %add.58.total), channel_id=1, source_target_pairs={{2,0},{3,1},{4,6},{5,7},{10,8},{11,9},{12,14},{13,15},{18,16},{19,... | collective-permute-start | bytes 1634312 | tf_op jit(solution)/shard_map/ppermute | solution.py:51
  215.7 24.3 %collective-permute-start.69 = (bf16[304,896]{1,0:T(8,128)(2,1)S(1)}, bf16[304,896]{1,0:T(8,128)(2,1)S(1)}, u32[]{:S(2)}, u32[]{:S(2)}) collective-permute-start(bf16[304,896]{1,0:T(8,128)(2,1)S(1)} %add.66.total), channel_id=1, source_target_pairs={{2,0},{3,1},{4,6},{5,7},{10,8},{11,9},{12,14},{13,15},{18,16},{19,... | collective-permute-start | bytes 1634312 | tf_op jit(solution)/shard_map/ppermute | solution.py:51
  217.3 24.6 %collective-permute-start.45 = (bf16[1864,128]{1,0:T(8,128)(2,1)S(1)}, bf16[1864,128]{1,0:T(8,128)(2,1)S(1)}, u32[]{:S(2)}, u32[]{:S(2)}) collective-permute-start(bf16[1864,128]{1,0:T(8,128)(2,1)S(1)} %add.53), channel_id=1, source_target_pairs={{2,4},{3,5},{4,2},{5,3},{10,12},{11,13},{12,10},{13,11},{18,20},{1... | collective-permute-start | bytes 1431560 | tf_op jit(solution)/shard_map/ppermute | solution.py:51
  218.0 33.7 %collective-permute-start.72 = (bf16[304,896]{1,0:T(8,128)(2,1)S(1)}, bf16[304,896]{1,0:T(8,128)(2,1)S(1)}, u32[]{:S(2)}, u32[]{:S(2)}) collective-permute-start(bf16[304,896]{1,0:T(8,128)(2,1)S(1)} %add.68.total), channel_id=1, source_target_pairs={{2,0},{3,1},{4,6},{5,7},{10,8},{11,9},{12,14},{13,15},{18,16},{19,... | collective-permute-start | bytes 1634312 | tf_op jit(solution)/shard_map/ppermute | solution.py:51
  219.4 44.5 %collective-permute-start.54 = (bf16[448,608]{1,0:T(8,128)(2,1)S(1)}, bf16[448,608]{1,0:T(8,128)(2,1)S(1)}, u32[]{:S(2)}, u32[]{:S(2)}) collective-permute-start(bf16[448,608]{1,0:T(8,128)(2,1)S(1)} %add.60.total), channel_id=1, source_target_pairs={{2,0},{3,1},{4,6},{5,7},{10,8},{11,9},{12,14},{13,15},{18,16},{19,... | collective-permute-start | bytes 1634312 | tf_op jit(solution)/shard_map/ppermute | solution.py:51
  220.9 55.3 %collective-permute-start.58 = (bf16[448,608]{1,0:T(8,128)(2,1)S(1)}, bf16[448,608]{1,0:T(8,128)(2,1)S(1)}, u32[]{:S(2)}, u32[]{:S(2)}) collective-permute-start(bf16[448,608]{1,0:T(8,128)(2,1)S(1)} %add.62.total), channel_id=1, source_target_pairs={{2,0},{3,1},{4,6},{5,7},{10,8},{11,9},{12,14},{13,15},{18,16},{19,... | collective-permute-start | bytes 1634312 | tf_op jit(solution)/shard_map/ppermute | solution.py:51
  240.0 45.9 %collective-permute-start.62 = (bf16[448,608]{1,0:T(8,128)(2,1)S(1)}, bf16[448,608]{1,0:T(8,128)(2,1)S(1)}, u32[]{:S(2)}, u32[]{:S(2)}) collective-permute-start(bf16[448,608]{1,0:T(8,128)(2,1)S(1)} %add.64.total), channel_id=1, source_target_pairs={{2,0},{3,1},{4,6},{5,7},{10,8},{11,9},{12,14},{13,15},{18,16},{19,... | collective-permute-start | bytes 1634312 | tf_op jit(solution)/shard_map/ppermute | solution.py:51
  241.9 50.9 %collective-permute-start.73 = (bf16[304,896]{1,0:T(8,128)(2,1)S(1)}, bf16[304,896]{1,0:T(8,128)(2,1)S(1)}, u32[]{:S(2)}, u32[]{:S(2)}) collective-permute-start(bf16[304,896]{1,0:T(8,128)(2,1)S(1)} %shard_map.208.rest_0_), channel_id=1, source_target_pairs={{0,1},{1,0},{2,3},{3,2},{4,5},{5,4},{6,7},{7,6},{8,9},{9,8},{10,11... | collective-permute-start | bytes 1634312 | tf_op jit(solution)/shard_map/ppermute | solution.py:28
  251.6 41.7 %collective-permute-start.46 = (bf16[1864,128]{1,0:T(8,128)(2,1)S(1)}, bf16[1864,128]{1,0:T(8,128)(2,1)S(1)}, u32[]{:S(2)}, u32[]{:S(2)}) collective-permute-start(bf16[1864,128]{1,0:T(8,128)(2,1)S(1)} %add.54.total), channel_id=1, source_target_pairs={{2,0},{3,1},{4,6},{5,7},{10,8},{11,9},{12,14},{13,15},{18,16},{19,... | collective-permute-start | bytes 1431560 | tf_op jit(solution)/shard_map/ppermute | solution.py:51
  263.9 30.8 %collective-permute-start.74 = (bf16[304,896]{1,0:T(8,128)(2,1)S(1)}, bf16[304,896]{1,0:T(8,128)(2,1)S(1)}, u32[]{:S(2)}, u32[]{:S(2)}) collective-permute-start(bf16[304,896]{1,0:T(8,128)(2,1)S(1)} %shard_map.209.rest_1_), channel_id=1, source_target_pairs={{0,1},{1,0},{2,3},{3,2},{4,5},{5,4},{6,7},{7,6},{8,9},{9,8},{10,11... | collective-permute-start | bytes 1634312 | tf_op jit(solution)/shard_map/ppermute | solution.py:28
  276.2 13.6 %collective-permute-start.34 = (bf16[128,896]{1,0:T(8,128)(2,1)S(1)}, bf16[128,896]{1,0:T(8,128)(2,1)S(1)}, u32[]{:S(2)}, u32[]{:S(2)}) collective-permute-start(bf16[128,896]{1,0:T(8,128)(2,1)S(1)} %get-tuple-element.84), channel_id=1, source_target_pairs={{0,16},{8,24},{16,0},{24,8},{1,17},{9,25},{17,1},{25,9},{2,18},{10... | collective-permute-start | bytes 688136 | tf_op jit(solution)/shard_map/ppermute | solution.py:33
  289.8 15.3 %collective-permute-start.63 = (bf16[448,608]{1,0:T(8,128)(2,1)S(1)}, bf16[448,608]{1,0:T(8,128)(2,1)}, u32[]{:S(2)}, u32[]{:S(2)}) collective-permute-start(bf16[448,608]{1,0:T(8,128)(2,1)S(1)} %shard_map.203.rest_0_), channel_id=1, source_target_pairs={{0,1},{1,0},{2,3},{3,2},{4,5},{5,4},{6,7},{7,6},{8,9},{9,8},{10,11... | collective-permute-start | bytes 1634312 | tf_op jit(solution)/shard_map/ppermute | solution.py:28
  292.8 12.3 %collective-permute-start.64 = (bf16[448,608]{1,0:T(8,128)(2,1)S(1)}, bf16[448,608]{1,0:T(8,128)(2,1)}, u32[]{:S(2)}, u32[]{:S(2)}) collective-permute-start(bf16[448,608]{1,0:T(8,128)(2,1)S(1)} %shard_map.204.rest_1_), channel_id=1, source_target_pairs={{0,1},{1,0},{2,3},{3,2},{4,5},{5,4},{6,7},{7,6},{8,9},{9,8},{10,11... | collective-permute-start | bytes 1634312 | tf_op jit(solution)/shard_map/ppermute | solution.py:28
  292.8 12.3 %collective-permute-start.65 = (bf16[448,608]{1,0:T(8,128)(2,1)S(1)}, bf16[448,608]{1,0:T(8,128)(2,1)}, u32[]{:S(2)}, u32[]{:S(2)}) collective-permute-start(bf16[448,608]{1,0:T(8,128)(2,1)S(1)} %shard_map.205.rest_2_), channel_id=1, source_target_pairs={{0,1},{1,0},{2,3},{3,2},{4,5},{5,4},{6,7},{7,6},{8,9},{9,8},{10,11... | collective-permute-start | bytes 1634312 | tf_op jit(solution)/shard_map/ppermute | solution.py:28
  295.6 16.0 %collective-permute-start.47 = (bf16[1864,128]{1,0:T(8,128)(2,1)}, bf16[1864,128]{1,0:T(8,128)(2,1)}, u32[]{:S(2)}, u32[]{:S(2)}) collective-permute-start(bf16[1864,128]{1,0:T(8,128)(2,1)} %shard_map.200.mine), channel_id=1, source_target_pairs={{0,1},{1,0},{2,3},{3,2},{4,5},{5,4},{6,7},{7,6},{8,9},{9,8},{10,11... | collective-permute-start | bytes 1431560 | tf_op jit(solution)/shard_map/ppermute | solution.py:28
  (51 other events, 464.0 us)

commit v2 on v1

--- a/solution.py
+++ b/solution.py
@@ -74,7 +74,7 @@
     return lax.dot_general(a, b, (((0,), (0,)), ((), ())), preferred_element_type=F32)
 
 
-GRANTS = {'pack': 12, 'attend': 3, 'mix': 4, 'down_back': 5, 'feed': 9, 'narrow': 4, 'back': 18, 'wide': 8, 'merge': 5, 'finish': 4, 'lay': 18, 'close': 6, 'ydown': 4, 'open': 3, 'yout': 4, 'pick': 4, 'stack': 8}
+GRANTS = {'pack': 12, 'attend': 5, 'down_back': 5, 'feed': 9, 'narrow': 4, 'back': 18, 'wide': 8, 'merge': 5, 'finish': 4, 'lay': 18, 'close': 6, 'ydown': 4, 'open': 3, 'yout': 4, 'pick': 4, 'stack': 8}
 
 
 def call(kernel, name, outs, where, args, scratch=(), flops=0, space=pltpu.VMEM):
@@ -99,6 +99,19 @@
 
 def rows_at(start, size):
     return pl.ds(pl.multiple_of(start, 8 if size % 16 else 16), size)
+
+
+def mark_kernel(where, out):
+    for i in range(out.shape[0]):
+        out[i] = where[i]
+
+
+def mark(where):
+    smem = pl.BlockSpec(memory_space=pltpu.SMEM)
+    return pl.pallas_call(
+        mark_kernel, out_shape=shape(where.shape, jnp.int32), in_specs=[smem], out_specs=smem,
+        compiler_params=pltpu.CompilerParams(vmem_limit_bytes=1 << 20),
+    )(where)
 
 
 def pack_kernel(shards, where, gate, up, *rest):
@@ -143,35 +156,81 @@
     )
 
 
-def open_kernel(where, w, g1, g2, b, block, extra):
-    half = w.shape[0] // 2
-    width = w.shape[1]
-    block[:half] = w[rows_at(where[1] * half, half)]
+def open_kernel(where, wq, wo, g1, g2, b, send, extra, one, two, three, sems):
+    half = wq.shape[0] // 2
+    width = wo.shape[1]
+    first = wq.shape[1] // LANES
+    count = send.shape[0]
+    vectors = ((g1, one), (g2, two), (b, three))
+    vector_copies = [
+        pltpu.make_async_copy(src, dst, sems.at[count + i]) for i, (src, dst) in enumerate(vectors)
+    ]
+    for copy in vector_copies:
+        copy.start()
+    at = rows_at(where[1] * half, half)
+    for parity in range(2):
+
+        @pl.when((where[2] & 1) == parity)
+        def _(parity=parity):
+            copies = []
+            for i in range(count):
+                block = parity * count + i
+                source = wq if block < first else wo
+                start = (block if block < first else block - first) * LANES
+                copy = pltpu.make_async_copy(
+                    source.at[at, pl.ds(start, LANES)], send.at[i, pl.ds(0, half)], sems.at[i]
+                )
+                copy.start()
+                copies.append(copy)
+            for copy in copies:
+                copy.wait()
+
     line = lax.broadcasted_iota(jnp.int32, extra.shape, 0)
     value = jnp.zeros(extra.shape, F32)
-    for i, ref in enumerate((g1, g2, b)):
-        row = ref[...].astype(F32)[None]
+    for i, copy in enumerate(vector_copies):
+        copy.wait()
+        row = vectors[i][1][...].astype(F32)[None]
         row = jnp.concatenate([row, jnp.zeros((1, width - row.shape[1]), F32)], axis=1)
         value = jnp.where(line == i, row, value)
     extra[...] = value.astype(BF)
-    block[half:] = value.astype(BF)
-
-
-def open_rows(where, w, g1, g2, b):
-    half, width = w.shape[0] // 2, w.shape[1]
-    return call(
-        open_kernel, "open", [shape((half + 8, width)), shape((8, width))], where, [w, g1, g2, b]
-    )
-
-
-def place_rows(dst, s, c, own, mine, other):
-    rows = own.shape[0]
-    half = rows // 2
-    dst[rows_at(s * rows, rows)] = own[...]
-    for k in range(1, len(mine) + 1):
-        base = (s ^ k) * rows
-        dst[rows_at(base + c * half, half)] = mine[k - 1][:half]
-        dst[rows_at(base + (1 - c) * half, half)] = other[k - 1][:half]
+    for parity in range(2):
+
+        @pl.when((where[2] & 1) == parity)
+        def _(parity=parity):
+            for i in range(count):
+                block = parity * count + i - first
+                lanes = slice(block * LANES, (block + 1) * LANES)
+                tail = jnp.zeros((8, LANES), BF) if block < 0 else extra[:, lanes]
+                send[i, half:] = tail
+
+
+def open_rows(where, wq, wo, g1, g2, b):
+    half = wq.shape[0] // 2
+    count = (wq.shape[1] + wo.shape[1]) // LANES // 2
+    outs = [shape((count, half + 8, LANES)), shape((8, wo.shape[1]))]
+    args = [pltpu.with_memory_space_constraint(v, pltpu.HBM) for v in (wq, wo, g1, g2, b)]
+    scratch = [pltpu.VMEM(v.shape, BF) for v in (g1, g2, b)]
+    scratch.append(pltpu.SemaphoreType.DMA((count + 3,)))
+    return call(open_kernel, "open", outs, where, args, scratch, space=pltpu.HBM)
+
+
+def place_blocks(w_ref, wo_ref, riders, s, low, high, core):
+    half = low[0].shape[1] - 8
+    rows = 2 * half
+    first = w_ref.shape[1] // LANES
+    for k in range(1, len(low) + 1):
+        at = rows_at((s ^ k) * rows + core * half, half)
+        count = low[k - 1].shape[0]
+        for block in range(2 * count):
+            piece = (low if block < count else high)[k - 1]
+            if block < first:
+                lanes = slice(block * LANES, (block + 1) * LANES)
+                w_ref[at, lanes] = piece[block % count, :half]
+            else:
+                lanes = slice((block - first) * LANES, (block - first + 1) * LANES)
+                wo_ref[at, lanes] = piece[block % count, :half]
+                if riders is not None:
+                    riders[k - 1, :, lanes] = piece[block % count, half:]
 
 
 def lane_kinds(x):
@@ -191,19 +250,32 @@
     return jnp.where(first, pltpu.roll(x, LANES - HALF, 1), pltpu.roll(x, HALF, 1))
 
 
-def attend_kernel(shards, where, x, seg, own, extra, *rest):
+def attend_kernel(shards, where, x, seg, own, own_out, extra, *rest):
     n = shards - 1
-    riders, mine, other = rest[:n], rest[n : 2 * n], rest[2 * n : 3 * n]
-    n1_ref, q_ref, k_ref, v_ref, p_ref, o_ref, w_ref, vec_ref, cos_ref, sin_ref = rest[3 * n :]
+    direct, passed, direct_other, passed_other = (rest[i * n : (i + 1) * n] for i in range(4))
+    n1_ref, q_ref, k_ref, v_ref, p_ref, o_ref, w_ref, vec_ref, cos_ref, sin_ref = rest[
+        4 * n : 4 * n + 10
+    ]
+    h_ref, n2_ref, wo_ref, riders = rest[4 * n + 10 :]
     s, c = where[0], where[1]
     width, joined_width = x.shape[1], own.shape[1]
-    place_rows(w_ref, s, c, own, mine, other)
+    w_ref[rows_at(s * own.shape[0], own.shape[0])] = own[...]
+    wo_ref[rows_at(s * own.shape[0], own.shape[0])] = own_out[...]
+    for parity in range(2):
+
+        @pl.when((where[2] & 1) == parity)
+        def _(parity=parity):
+            pair = (direct, passed)
+            place_blocks(w_ref, wo_ref, riders, s, pair[parity], pair[1 - parity], c)
+            pair = (direct_other, passed_other)
+            place_blocks(w_ref, wo_ref, None, s, pair[parity], pair[1 - parity], 1 - c)
+
     lines = extra.shape[0]
     is_gain = lax.broadcasted_iota(jnp.int32, vec_ref.shape, 0) < 2
     vec = jnp.zeros(vec_ref.shape, F32)
     gap = jnp.zeros((lines, joined_width - width), F32)
-    for k, piece in enumerate((extra,) + tuple(riders)):
-        value = piece[piece.shape[0] - lines :].astype(F32)
+    for k in range(shards):
+        value = (extra[...] if k == 0 else riders[k - 1]).astype(F32)
         value = jnp.concatenate([value, gap], axis=1)
         gains = pltpu.roll(value, (s ^ k) * (width // shards), 1)
         biases = pltpu.roll(value, (s ^ k) * (joined_width // shards), 1)
@@ -260,8 +332,13 @@
             mixed = mixed + dot(p.astype(BF), value_kinds[g][side])
         o_ref[:, i * LANES : (i + 1) * LANES] = mixed.astype(BF)
 
-
-def attend(where, x, seg, own, extra, riders, mine, other, shards):
+    h = xf + dot(o_ref[...], wo_ref[...])
+    h_ref[...] = h
+    root = lax.rsqrt(jnp.mean(h * h, axis=1, keepdims=True) + EPS)
+    n2_ref[...] = (h * root * vec[1:2, :width]).astype(BF)
+
+
+def attend(where, x, seg, own, own_out, extra, pieces, shards):
     tokens, width = x.shape
     joined = own.shape[1]
     outs = [
@@ -269,32 +346,13 @@
         shape((tokens, LANES)), shape((QUERY_HEADS, tokens, tokens), F32),
         shape((tokens, width)), shape((width, joined)), shape((extra.shape[0], joined), F32),
         shape((tokens, LANES), F32), shape((tokens, LANES), F32),
+        shape(x.shape, F32), shape(x.shape), shape((width, width)),
     ]
     return call(
         functools.partial(attend_kernel, shards), "attend", outs, where,
-        [x, seg, own, extra, *riders, *mine, *other],
-        flops=2 * tokens * width * joined + 8 * QUERY_HEADS * tokens * tokens * LANES,
-    )
-
-
-def mix_kernel(shards, where, x, o, vec, own, *rest):
-    n = shards - 1
-    mine, other = rest[:n], rest[n : 2 * n]
-    h_ref, n2_ref, w_ref = rest[2 * n :]
-    place_rows(w_ref, where[0], where[1], own, mine, other)
-    width = x.shape[1]
-    h = x[...].astype(F32) + dot(o[...], w_ref[...])
-    h_ref[...] = h
-    root = lax.rsqrt(jnp.mean(h * h, axis=1, keepdims=True) + EPS)
-    n2_ref[...] = (h * root * vec[1:2, :width]).astype(BF)
-
-
-def mix(where, x, o, vec, own, mine, other, shards):
-    tokens, width = x.shape
-    outs = [shape(x.shape, F32), shape(x.shape), shape((width, width))]
-    return call(
-        functools.partial(mix_kernel, shards), "mix", outs, where,
-        [x, o, vec, own, *mine, *other], flops=2 * tokens * width * width,
+        [x, seg, own, own_out, extra, *pieces],
+        [pltpu.VMEM((shards - 1,) + extra.shape, BF)],
+        flops=2 * tokens * width * (joined + width) + 8 * QUERY_HEADS * tokens * tokens * LANES,
     )
 
 
@@ -305,9 +363,9 @@
         dy_ref[i * tokens : (i + 1) * tokens] = parts[i][...]
     slab = dact_ref.shape[1]
     w = down[rows_at(where[1] * slab, slab)]
-    step = 2 * tokens
-
-    @pl.loop(0, pieces // 2)
+    step = 4 * tokens
+
+    @pl.loop(0, pieces // 4)
     def _(i):
         at = pl.ds(pl.multiple_of(i * step, step), step)
         dact_ref[at] = dot_t(dy_ref[at], w)
@@ -345,9 +403,9 @@
 
     for i in range(pieces):
         n_ref[i * tokens : (i + 1) * tokens] = parts[i][...]
-    step = 2 * tokens
-
-    @pl.loop(0, pieces // 2)
+    step = 4 * tokens
+
+    @pl.loop(0, pieces // 4)
     def _(i):
         at = pl.ds(pl.multiple_of(i * step, step), step)
         block = n_ref[at]
@@ -429,19 +487,12 @@
 
 def narrow_kernel(where, dgate, dup, wg, wu, keep, give):
     count = keep.shape[0]
-    step = count // 2
-
-    def block(i):
-        at = pl.ds(pl.multiple_of(i * step, step), step)
+
+    def block(at):
         return dot_t(dgate[at], wg[...]) + dot_t(dup[at], wu[...])
 
-    @pl.loop(0, 2)
-    def _(i):
-        give[pl.ds(pl.multiple_of(i * step, step), step)] = block(i + 2).astype(BF)
-
-    @pl.loop(0, 2)
-    def _(i):
-        keep[pl.ds(pl.multiple_of(i * step, step), step)] = block(i)
+    give[...] = block(slice(count, 2 * count)).astype(BF)
+    keep[...] = block(slice(0, count))
 
 
 def narrow(where, dgate, dup, wg, wu):
@@ -552,15 +603,10 @@
 
 def down_kernel(where, act, down, keep, give):
     count = keep.shape[0]
-    step = count // 2
     slab = act.shape[1]
     w = down[rows_at(where[1] * slab, slab)]
-
-    @pl.loop(0, 2)
-    def _(i):
-        at = pl.multiple_of(i * step, step)
-        give[pl.ds(at, step)] = dot(act[pl.ds(at + count, step)], w).astype(BF)
-        keep[pl.ds(at, step)] = dot(act[pl.ds(at, step)], w)
+    give[...] = dot(act[count:], w).astype(BF)
+    keep[...] = dot(act[:count], w)
 
 
 def down_project(where, act, down):
@@ -649,8 +695,8 @@
     return call(finish_kernel, "finish", [shape(parts[0].shape)], where, parts)[0]
 
 
-def close_kernel(tall, where, mine, other, qkv_ref, out_ref, vec_ref):
-    c = where[1]
+def close_kernel(tall, where, mine, other, qkv_ref, out_ref, one_ref, two_ref, bias_ref):
+    s, c = where[0], where[1]
     half = qkv_ref.shape[0] // 2
     for source, side in ((mine, c), (other, 1 - c)):
         at = pl.ds(pl.multiple_of(side * half, 8), half)
@@ -660,13 +706,17 @@
         for b in range(out_ref.shape[1] // LANES):
             base = tall + b * half
             out_ref[at, b * LANES : (b + 1) * LANES] = source[base : base + half].astype(F32)
-    for b in range(qkv_ref.shape[1] // LANES):
-        base = b * (half + 8) + half
-        vec_ref[:, b * LANES : (b + 1) * LANES] = mine[base : base + 8].astype(F32)
+    starts = [b * (half + 8) + half for b in range(qkv_ref.shape[1] // LANES)]
+    vec = jnp.concatenate([mine[at : at + 8].astype(F32) for at in starts], axis=1)
+    width = vec.shape[1]
+    for i, ref in enumerate((one_ref, two_ref, bias_ref)):
+        turned = pltpu.roll(vec, lax.rem(width - s * ref.shape[0], width), 1)
+        ref[...] = turned[i, : ref.shape[0]]
 
 
 def close(where, mine, other, rows, width, joined, tall):
-    outs = [shape((rows, joined), F32), shape((rows, width), F32), shape((8, joined), F32)]
+    outs = [shape((rows, joined), F32), shape((rows, width), F32)]
+    outs += [shape((n,), F32) for n in (rows, rows, joined * rows // width)]
     return call(functools.partial(close_kernel, tall), "close", outs, where, [mine, other])
 
 
@@ -680,16 +730,12 @@
     where = jnp.stack([shard, core, replica >> 1]).astype(jnp.int32)
     _, width = tokens.shape
     rows = norm1_gain.shape[0]
-    half_rows = rows // 2
     joined = w_qkv.shape[1]
-    bias_rows = b_qkv.shape[0]
     slab = w_gate.shape[1] // (2 * shards)
-    half = lax.dynamic_slice_in_dim(w_qkv, core * half_rows, half_rows, 0)
-    qkv_mine = spread(half)[1:]
-    qkv_other = [swap_core(p) for p in qkv_mine]
-    out_block, extra = open_rows(where, w_out, norm1_gain, norm2_gain, b_qkv)
-    out_mine = spread(out_block)[1:]
-    out_other = [swap_core(p) for p in out_mine]
+    block, extra = open_rows(where, w_qkv, w_out, norm1_gain, norm2_gain, b_qkv)
+    pieces = spread(block)[1:]
+    pieces += [pair_swap(p) for p in pieces]
+    pieces += [swap_core(p) for p in pieces]
 
     packed = pack(
         where, *(pltpu.with_memory_space_constraint(w, pltpu.HBM) for w in (w_gate, w_up)), shards
@@ -699,11 +745,9 @@
     dy = spread(cotangent)
     dy = dy + [swap_core(p) for p in dy]
 
-    n_one, query, keys, values, probs, mixed, wqkv, vec, cosine, sine = attend(
-        where, tokens, seg_ids,
-        w_qkv, extra, out_mine, qkv_mine, qkv_other, shards,
-    )
-    hidden, n_two, wout = mix(where, tokens, mixed, vec, w_out, out_mine, out_other, shards)
+    (
+        n_one, query, keys, values, probs, mixed, wqkv, vec, cosine, sine, hidden, n_two, wout
+    ) = attend(where, tokens, seg_ids, w_qkv, w_out, extra, pieces, shards)
     n_parts = spread(n_two)
     n_parts = n_parts + [swap_core(p) for p in n_parts]
 
@@ -724,7 +768,8 @@
     grads = wide(where, n_all, d_gate, d_up, shards)
     grads = [grads[0]] + [shard_swap(grads[k], k) for k in range(1, shards)]
     grads = [line_sum(where, g) for g in grads]
-    gate_part, up_part = lay(where, grads, [swap_core(g) for g in grads])
+    marked = mark(where)
+    gate_part, up_part = lay(marked, grads, [swap_core(g) for g in grads])
 
     down_part = stack(where, [down_one, down_two], [swap_core(down_one), swap_core(down_two)])
     y = plane_sum(*down_project(where, act, w_down))
@@ -737,10 +782,9 @@
     parts = plane_sum(keep, give)
     tall, _ = layout_of(width, joined, rows)
     item = line_sum(where, finish(where, parts))
-    qkv_part, out_part, vec_grads = close(where, item, swap_core(item), rows, width, joined, tall)
-    one_part = lax.dynamic_slice(vec_grads[0], (shard * rows,), (rows,))
-    two_part = lax.dynamic_slice(vec_grads[1], (shard * rows,), (rows,))
-    bias_part = lax.dynamic_slice(vec_grads[2], (shard * bias_rows,), (bias_rows,))
+    qkv_part, out_part, one_part, two_part, bias_part = close(
+        where, item, swap_core(item), rows, width, joined, tall
+    )
     return (
         layer_out,
         grad_tokens,

time: 316 us -> 316 us (level)
  waiting for transfers between devices: 160 us -> 176 us
  local copies, waits for them, and re-layouts: 11 us -> 0.04 us
    ppermute x21, waiting for transfers between devices: 97.5 us -> 119 us  [hop(): return lax.ppermute(value, 'replica', links)]
    unnamed x48 -> x12, local copies, waits for them, and re-layouts: 8.71 us -> 0.04 us
    ppermute x27 -> x24, waiting for transfers between devices: 56.6 us -> 50.3 us  [shard_swap(): return lax.ppermute(x, 'shard', [(i, i ^ k) for i in range(n)])]
    ppermute x27 -> x24, starting transfers between devices: 40.9 us -> 35.5 us  [shard_swap(): return lax.ppermute(x, 'shard', [(i, i ^ k) for i in range(n)])]
    pallas_call x25 -> x24, Pallas kernels: 59.1 us -> 55 us  [call(): pl.pallas_call(kernel, out_shape=outs, in_specs=[pl.BlockSpec(memory_spac...]
    ppermute x3 -> x6, starting transfers between devices: 3.62 us -> 6.84 us  [pair_swap(): return lax.ppermute(x, 'replica', [(i, i ^ 2) for i in range(n)])]
  transfers between devices with their start and end apart: 75 -> 75, of which waited for: 31 -> 30; matrix products, arithmetic and copies ran while one was open for 1% -> 1% of each run, Pallas kernels for 12% -> 11%
where the time goes in v2:
time: 316 us
  waiting for transfers between devices  176 us (56%)
  starting transfers between devices  79.9 us (25%)
  Pallas kernels  56.1 us (18%)
    ppermute x21, waiting for transfers between devices, hop(): return lax.ppermute(value, 'replica', links)  119 us
    pallas_call x24, Pallas kernels, call(): pl.pallas_call(kernel, out_shape=outs, in_specs=[pl.BlockSpec(memory_spac...  55 us
    ppermute x24, waiting for transfers between devices, shard_swap(): return lax.ppermute(x, 'shard', [(i, i ^ k) for i in range(n)])  50.3 us
    ppermute x24, starting transfers between devices, shard_swap(): return lax.ppermute(x, 'shard', [(i, i ^ k) for i in range(n)])  35.5 us
    ppermute x21, starting transfers between devices, hop(): return lax.ppermute(value, 'replica', links)  33.1 us
    ppermute x6, starting transfers between devices, pair_swap(): return lax.ppermute(x, 'replica', [(i, i ^ 2) for i in range(n)])  6.84 us
  transfers between devices with their start and end apart: 75, of which 30 were waited for; matrix products, arithmetic and copies ran while one was open for 1% of the time, Pallas kernels for 11%

profile of v2, /device:TPU:0, one launch (start us, length us, event | category | flops | bytes accessed | tf_op | source)
XLA Modules:
  0.0 315.6 jit_solution(12130599446243669770)
XLA Ops:
  0.6 3.0 collective-permute-start.12
  6.9 2.0 collective-permute-start
  10.3 2.0 collective-permute-start.1
  12.4 4.0 %collective-permute-done.13.rest_2_ = bf16[128,896]{1,0:T(8,128)(2,1)S(1)} collective-permute-done((bf16[128,896]{1,0:T(8,128)(2,1)}, bf16[128,896]{1,0:T(8,128)(2,1)S(1)}, u32[]{:S(2)}, u32[]{:S(2)}) %collective-permute-start.13) | collective-permute-done | bytes 229408 | tf_op jit(solution)/shard_map/ppermute | solution.py:33
  16.9 3.2 %shard_map.189 = (bf16[448,608]{1,0:T(8,128)(2,1)S(1)}, bf16[224,608]{1,0:T(8,128)(2,1)S(1)}, bf16[224,608]{1,0:T(8,128)(2,1)S(1)}, bf16[224,608]{1,0:T(8,128)(2,1)S(1)}) custom-call(s32[3]{0:T(128)S(1)} %pad_add_fusion.where, bf16[224,4864]{1,0:T(8,128)(2,1)} %gate.1, bf16[224,4864]{1,0:T(8,128)(2,1)} %up.1), custom_call_target="tpu_custom_call" | custom-call | bytes 5720064 | tf_op jit(solution)/shard_map/pallas_call | solution.py:85
  20.1 3.4 %collective-permute-start.26 = (bf16[224,608]{1,0:T(8,128)(2,1)S(1)}, bf16[224,608]{1,0:T(8,128)(2,1)S(1)}, u32[]{:S(2)}, u32[]{:S(2)}) collective-permute-start(bf16[224,608]{1,0:T(8,128)(2,1)S(1)} %get-tuple-element.76), channel_id=1, source_target_pairs={{0,8},{8,0},{16,24},{24,16},{1,9},{9,1},{17,25},{25,17},{2,10},{10... | collective-permute-start | bytes 817160 | tf_op jit(solution)/shard_map/ppermute | solution.py:33
  25.1 1.8 collective-permute-done.1.rest_1_
  28.9 4.3 %collective-permute-done.26.rest_9_ = bf16[224,608]{1,0:T(8,128)(2,1)S(1)} collective-permute-done((bf16[224,608]{1,0:T(8,128)(2,1)S(1)}, bf16[224,608]{1,0:T(8,128)(2,1)S(1)}, u32[]{:S(2)}, u32[]{:S(2)}) %collective-permute-start.26) | collective-permute-done | bytes 272416 | tf_op jit(solution)/shard_map/ppermute | solution.py:33
  34.6 4.1 %collective-permute-done.27.rest_10_ = bf16[224,608]{1,0:T(8,128)(2,1)S(1)} collective-permute-done((bf16[224,608]{1,0:T(8,128)(2,1)S(1)}, bf16[224,608]{1,0:T(8,128)(2,1)S(1)}, u32[]{:S(2)}, u32[]{:S(2)}) %collective-permute-start.27) | collective-permute-done | bytes 272416 | tf_op jit(solution)/shard_map/ppermute | solution.py:33
  44.6 5.2 %shard_map.187 = (bf16[128,896]{1,0:T(8,128)(2,1)S(1)}, bf16[128,896]{1,0:T(8,128)(2,1)S(1)}, bf16[128,128]{1,0:T(8,128)(2,1)S(1)}, bf16[128,128]{1,0:T(8,128)(2...) custom-call(s32[3]{0:T(128)S(1)} %pad_add_fusion.where, ...), custom_call_target="tpu_custom_call" | custom-call | flops 704643072 | bytes 10308096 | tf_op jit(solution)/shard_map/pallas_call | solution.py:85
  55.2 3.2 %collective-permute-done.30.rest_13_ = bf16[224,608]{1,0:T(8,128)(2,1)S(1)} collective-permute-done((bf16[224,608]{1,0:T(8,128)(2,1)S(1)}, bf16[224,608]{1,0:T(8,128)(2,1)S(1)}, u32[]{:S(2)}, u32[]{:S(2)}) %collective-permute-start.30) | collective-permute-done | bytes 272416 | tf_op jit(solution)/shard_map/ppermute | solution.py:38
  58.8 3.0 collective-permute-done.20.rest_2_
  61.9 1.8 collective-permute-done.21.rest_3_
  63.7 2.8 shard_map.188
  66.5 6.5 %shard_map.190 = (bf16[304,896]{1,0:T(8,128)(2,1)S(1)}, bf16[304,896]{1,0:T(8,128)(2,1)S(1)}, bf16[1024,608]{1,0:T(8,128)(2,1)S(1)}, bf16[1024,608]{1,0:T(8,128)...) custom-call(s32[3]{0:T(128)S(1)} %pad_add_fusion.where, ...), custom_call_target="tpu_custom_call" | custom-call | flops 3347054592 | bytes 17178624 | tf_op jit(solution)/shard_map/pallas_call | solution.py:85
  73.1 3.9 %shard_map.194 = (f32[512,896]{1,0:T(8,128)S(1)}, bf16[512,896]{1,0:T(8,128)(2,1)S(1)}) custom-call(s32[3]{0:T(128)S(1)} %pad_add_fusion.where, bf16[1024,608]{1,0:T(8,128)(2,1)S(1)} %get-tuple-element.86.dgate, bf16[1024,608]{1,0:T(8,128)(2,1)S(1)} %get-tuple-element.87.dup, bf16[896,608]{1,0:T(8,128)(2,1)S(1)} %get-tuple-element.88.wg, ...), custom_call_target="tpu_custom_call" | custom-call | flops 2231369728 | bytes 7421952 | tf_op jit(solution)/shard_map/pallas_call | solution.py:85
  77.5 2.1 collective-permute-done.36
  83.9 5.0 %collective-permute-done.37.rest_1_ = bf16[128,896]{1,0:T(8,128)(2,1)S(1)} collective-permute-done((bf16[128,896]{1,0:T(8,128)(2,1)S(1)}, bf16[128,896]{1,0:T(8,128)(2,1)S(1)}, u32[]{:S(2)}, u32[]{:S(2)}) %collective-permute-start.37) | collective-permute-done | bytes 229408 | tf_op jit(solution)/shard_map/ppermute | solution.py:33
  88.9 4.8 %collective-permute-done.38.rest_2_ = bf16[128,896]{1,0:T(8,128)(2,1)S(1)} collective-permute-done((bf16[128,896]{1,0:T(8,128)(2,1)S(1)}, bf16[128,896]{1,0:T(8,128)(2,1)S(1)}, u32[]{:S(2)}, u32[]{:S(2)}) %collective-permute-start.38) | collective-permute-done | bytes 229408 | tf_op jit(solution)/shard_map/ppermute | solution.py:33
  93.6 7.1 %shard_map.196 = (f32[128,896]{1,0:T(8,128)}, f32[4,1864,128]{2,1,0:T(8,128)S(1)}, bf16[4,1864,128]{2,1,0:T(8,128)(2,1)S(1)}) custom-call(s32[3]{0:T(128)S(1)} %pad_add_fusion.where, f32[128,896]{1,0:T(8,128)S(1)} %get-tuple-element.92.rest_0_, bf16[128,896]{1,0:T(8,128)(2,1)S(1)} %collective-permute-done.37.rest_1_, ...), custom_call_target="tpu_custom_call" | custom-call | flops 939524096 | bytes 13758464 | tf_op jit(solution)/shard_map/pallas_call | solution.py:85
  100.7 3.8 %shard_map.202 = (bf16[448,608]{1,0:T(8,128)(2,1)S(1)}, bf16[448,608]{1,0:T(8,128)(2,1)S(1)}, bf16[448,608]{1,0:T(8,128)(2,1)S(1)}, bf16[448,608]{1,0:T(8,128)(2,1)S(1)}) custom-call(s32[3]{0:T(128)S(1)} %pad_add_fusion.where, bf16[1024,896]{1,0:T(8,128)(2,1)S(1)} %get-tuple-element.119.n, bf16[1024,608]{1,0:T(8,128)(2,1)S(1)} %get-tuple-element.86.dgate, ...), custom_call_target="tpu_custom_call" | custom-call | flops 2231369728 | bytes 6504448 | tf_op jit(solution)/shard_map/pallas_call | solution.py:85
  104.5 3.5 %collective-permute-start.48 = (bf16[448,608]{1,0:T(8,128)(2,1)S(1)}, bf16[448,608]{1,0:T(8,128)(2,1)S(1)}, u32[]{:S(2)}, u32[]{:S(2)}) collective-permute-start(bf16[448,608]{1,0:T(8,128)(2,1)S(1)} %get-tuple-element.120), channel_id=1, source_target_pairs={{0,2},{1,3},{6,4},{7,5},{8,10},{9,11},{14,12},{15,13},{16,18},{17,... | collective-permute-start | bytes 1634312 | tf_op jit(solution)/shard_map/ppermute | solution.py:51
  111.6 2.3 shard_map.191
  113.8 6.8 %collective-permute-done.48 = bf16[448,608]{1,0:T(8,128)(2,1)S(1)} collective-permute-done((bf16[448,608]{1,0:T(8,128)(2,1)S(1)}, bf16[448,608]{1,0:T(8,128)(2,1)S(1)}, u32[]{:S(2)}, u32[]{:S(2)}) %collective-permute-start.48) | collective-permute-done | bytes 544800 | tf_op jit(solution)/shard_map/ppermute | solution.py:51
  120.6 3.3 %collective-permute-done.51 = bf16[448,608]{1,0:T(8,128)(2,1)S(1)} collective-permute-done((bf16[448,608]{1,0:T(8,128)(2,1)S(1)}, bf16[448,608]{1,0:T(8,128)(2,1)S(1)}, u32[]{:S(2)}, u32[]{:S(2)}) %collective-permute-start.51) | collective-permute-done | bytes 544800 | tf_op jit(solution)/shard_map/ppermute | solution.py:33
  125.2 9.6 %collective-permute-done.55 = bf16[448,608]{1,0:T(8,128)(2,1)S(1)} collective-permute-done((bf16[448,608]{1,0:T(8,128)(2,1)S(1)}, bf16[448,608]{1,0:T(8,128)(2,1)S(1)}, u32[]{:S(2)}, u32[]{:S(2)}) %collective-permute-start.55) | collective-permute-done | bytes 544800 | tf_op jit(solution)/shard_map/ppermute | solution.py:33
  140.5 2.0 collective-permute-start.41
  142.5 7.1 %collective-permute-done.70 = bf16[304,896]{1,0:T(8,128)(2,1)S(1)} collective-permute-done((bf16[304,896]{1,0:T(8,128)(2,1)S(1)}, bf16[304,896]{1,0:T(8,128)(2,1)S(1)}, u32[]{:S(2)}, u32[]{:S(2)}) %collective-permute-start.70) | collective-permute-done | bytes 544800 | tf_op jit(solution)/shard_map/ppermute | solution.py:51
  149.6 1.9 collective-permute-start.42
  153.0 8.9 %collective-permute-done.52 = bf16[448,608]{1,0:T(8,128)(2,1)S(1)} collective-permute-done((bf16[448,608]{1,0:T(8,128)(2,1)S(1)}, bf16[448,608]{1,0:T(8,128)(2,1)S(1)}, u32[]{:S(2)}, u32[]{:S(2)}) %collective-permute-start.52) | collective-permute-done | bytes 544800 | tf_op jit(solution)/shard_map/ppermute | solution.py:51
  161.9 4.4 %collective-permute-start.60 = (bf16[448,608]{1,0:T(8,128)(2,1)S(1)}, bf16[448,608]{1,0:T(8,128)(2,1)S(1)}, u32[]{:S(2)}, u32[]{:S(2)}) collective-permute-start(bf16[448,608]{1,0:T(8,128)(2,1)S(1)} %collective-permute-done.59), channel_id=1, source_target_pairs={{0,2},{1,3},{6,4},{7,5},{8,10},{9,11},{14,12},{15,13},{16,18},{17,... | collective-permute-start | bytes 1634312 | tf_op jit(solution)/shard_map/ppermute | solution.py:51
  166.6 7.6 %collective-permute-done.56 = bf16[448,608]{1,0:T(8,128)(2,1)S(1)} collective-permute-done((bf16[448,608]{1,0:T(8,128)(2,1)S(1)}, bf16[448,608]{1,0:T(8,128)(2,1)S(1)}, u32[]{:S(2)}, u32[]{:S(2)}) %collective-permute-start.56) | collective-permute-done | bytes 544800 | tf_op jit(solution)/shard_map/ppermute | solution.py:51
  178.1 7.7 %collective-permute-done.60 = bf16[448,608]{1,0:T(8,128)(2,1)S(1)} collective-permute-done((bf16[448,608]{1,0:T(8,128)(2,1)S(1)}, bf16[448,608]{1,0:T(8,128)(2,1)S(1)}, u32[]{:S(2)}, u32[]{:S(2)}) %collective-permute-start.60) | collective-permute-done | bytes 544800 | tf_op jit(solution)/shard_map/ppermute | solution.py:51
  185.8 5.6 %collective-permute-start.44 = (bf16[1864,128]{1,0:T(8,128)(2,1)S(1)}, bf16[1864,128]{1,0:T(8,128)(2,1)S(1)}, u32[]{:S(2)}, u32[]{:S(2)}) collective-permute-start(bf16[1864,128]{1,0:T(8,128)(2,1)S(1)} %shard_map.198), channel_id=1, source_target_pairs={{0,2},{1,3},{6,4},{7,5},{8,10},{9,11},{14,12},{15,13},{16,18},{17,... | collective-permute-start | bytes 1431560 | tf_op jit(solution)/shard_map/ppermute | solution.py:51
  196.8 3.2 %collective-permute-done.44 = bf16[1864,128]{1,0:T(8,128)(2,1)S(1)} collective-permute-done((bf16[1864,128]{1,0:T(8,128)(2,1)S(1)}, bf16[1864,128]{1,0:T(8,128)(2,1)S(1)}, u32[]{:S(2)}, u32[]{:S(2)}) %collective-permute-start.44) | collective-permute-done | bytes 477216 | tf_op jit(solution)/shard_map/ppermute | solution.py:51
  201.5 4.6 %collective-permute-done.33.rest_1_ = bf16[128,896]{1,0:T(8,128)(2,1)S(1)} collective-permute-done((bf16[128,896]{1,0:T(8,128)(2,1)S(1)}, bf16[128,896]{1,0:T(8,128)(2,1)S(1)}, u32[]{:S(2)}, u32[]{:S(2)}) %collective-permute-start.33) | collective-permute-done | bytes 229408 | tf_op jit(solution)/shard_map/ppermute | solution.py:33
  209.5 18.0 %collective-permute-done.69.arrived = bf16[304,896]{1,0:T(8,128)(2,1)S(1)} collective-permute-done((bf16[304,896]{1,0:T(8,128)(2,1)S(1)}, bf16[304,896]{1,0:T(8,128)(2,1)S(1)}, u32[]{:S(2)}, u32[]{:S(2)}) %collective-permute-start.69) | collective-permute-done | bytes 544800 | tf_op jit(solution)/shard_map/ppermute | solution.py:51
  228.9 10.8 %collective-permute-done.72.arrived = bf16[304,896]{1,0:T(8,128)(2,1)S(1)} collective-permute-done((bf16[304,896]{1,0:T(8,128)(2,1)S(1)}, bf16[304,896]{1,0:T(8,128)(2,1)S(1)}, u32[]{:S(2)}, u32[]{:S(2)}) %collective-permute-start.72) | collective-permute-done | bytes 544800 | tf_op jit(solution)/shard_map/ppermute | solution.py:51
  242.5 10.2 %collective-permute-done.50.arrived = bf16[448,608]{1,0:T(8,128)(2,1)S(1)} collective-permute-done((bf16[448,608]{1,0:T(8,128)(2,1)S(1)}, bf16[448,608]{1,0:T(8,128)(2,1)S(1)}, u32[]{:S(2)}, u32[]{:S(2)}) %collective-permute-start.50) | collective-permute-done | bytes 544800 | tf_op jit(solution)/shard_map/ppermute | solution.py:51
  254.0 15.7 %collective-permute-done.54.arrived = bf16[448,608]{1,0:T(8,128)(2,1)S(1)} collective-permute-done((bf16[448,608]{1,0:T(8,128)(2,1)S(1)}, bf16[448,608]{1,0:T(8,128)(2,1)S(1)}, u32[]{:S(2)}, u32[]{:S(2)}) %collective-permute-start.54) | collective-permute-done | bytes 544800 | tf_op jit(solution)/shard_map/ppermute | solution.py:51
  269.7 12.3 %collective-permute-done.58.arrived = bf16[448,608]{1,0:T(8,128)(2,1)S(1)} collective-permute-done((bf16[448,608]{1,0:T(8,128)(2,1)S(1)}, bf16[448,608]{1,0:T(8,128)(2,1)S(1)}, u32[]{:S(2)}, u32[]{:S(2)}) %collective-permute-start.58) | collective-permute-done | bytes 544800 | tf_op jit(solution)/shard_map/ppermute | solution.py:51
  282.0 1.9 collective-permute-start.34
  284.0 10.3 %collective-permute-done.62.arrived = bf16[448,608]{1,0:T(8,128)(2,1)S(1)} collective-permute-done((bf16[448,608]{1,0:T(8,128)(2,1)S(1)}, bf16[448,608]{1,0:T(8,128)(2,1)S(1)}, u32[]{:S(2)}, u32[]{:S(2)}) %collective-permute-start.62) | collective-permute-done | bytes 544800 | tf_op jit(solution)/shard_map/ppermute | solution.py:51
  294.3 2.0 collective-permute-start.35
  298.8 2.4 collective-permute-done.35.rest_3_
  305.4 2.9 shard_map.210
  308.3 5.4 %shard_map.207 = (f32[224,4864]{1,0:T(8,128)}, f32[224,4864]{1,0:T(8,128)}) custom-call(s32[3]{0:T(128)S(1)} %shard_map.201.where, bf16[448,608]{1,0:T(8,128)(2,1)S(1)} %shard_map.203.rest_0_, bf16[448,608]{1,0:T(8,128)(2,1)S(1)} %shard_map.204.rest_1_, bf16[448,608]{1,0:T(8,128)(2,1)S(1)} %shard_map.205.rest_2_, bf16[448,608]{1,0:T(8,128)(2,1)S(1)} %shard_map.206.rest_3_, ...), custom_call_target="tpu_custom_call" | custom-call | bytes 13074432 | tf_op jit(solution)/shard_map/pallas_call | solution.py:85
  313.7 1.8 shard_map.200
  (154 shorter events, 64.8 us)
Async XLA Ops:
  3.7 12.7 %collective-permute-start.13 = (bf16[128,896]{1,0:T(8,128)(2,1)}, bf16[128,896]{1,0:T(8,128)(2,1)S(1)}, u32[]{:S(2)}, u32[]{:S(2)}) collective-permute-start(bf16[128,896]{1,0:T(8,128)(2,1)} %rest_5_.1), channel_id=1, source_target_pairs={{0,16},{8,24},{16,0},{24,8},{1,17},{9,25},{17,1},{25,9},{2,18},{10... | collective-permute-start | bytes 688136 | tf_op jit(solution)/shard_map/ppermute | solution.py:33
  5.2 14.9 %collective-permute-start.14 = (bf16[128,896]{1,0:T(8,128)(2,1)}, bf16[128,896]{1,0:T(8,128)(2,1)S(1)}, u32[]{:S(2)}, u32[]{:S(2)}) collective-permute-start(bf16[128,896]{1,0:T(8,128)(2,1)} %rest_5_.1), channel_id=1, source_target_pairs={{0,24},{8,16},{16,8},{24,0},{1,25},{9,17},{17,9},{25,1},{2,26},{10... | collective-permute-start | bytes 688136 | tf_op jit(solution)/shard_map/ppermute | solution.py:33
  5.2 18.3 %collective-permute-start.15 = (bf16[128,896]{1,0:T(8,128)(2,1)}, bf16[128,896]{1,0:T(8,128)(2,1)S(1)}, u32[]{:S(2)}, u32[]{:S(2)}) collective-permute-start(bf16[128,896]{1,0:T(8,128)(2,1)} %rest_5_.1), channel_id=1, source_target_pairs={{0,1},{1,0},{2,3},{3,2},{4,5},{5,4},{6,7},{7,6},{8,9},{9,8},{10,11... | collective-permute-start | bytes 688136 | tf_op jit(solution)/shard_map/ppermute | solution.py:28
  6.9 16.6 %collective-permute-start = (bf16[8,120,128]{2,1,0:T(8,128)(2,1)S(1)}, bf16[8,120,128]{2,1,0:T(8,128)(2,1)S(1)}, u32[]{:S(2)}, u32[]{:S(2)}) collective-permute-start(bf16[8,120,128]{2,1,0:T(8,128)(2,1)S(1)} %get-tuple-element.70), channel_id=1, source_target_pairs={{0,8},{8,0},{16,24},{24,16},{1,9},{9,1},{17,25},{25,17},{2,10},{10... | collective-permute-start | bytes 737288 | tf_op jit(solution)/shard_map/ppermute | solution.py:33
  10.3 16.5 %collective-permute-start.1 = (bf16[8,120,128]{2,1,0:T(8,128)(2,1)S(1)}, bf16[8,120,128]{2,1,0:T(8,128)(2,1)S(1)}, u32[]{:S(2)}, u32[]{:S(2)}) collective-permute-start(bf16[8,120,128]{2,1,0:T(8,128)(2,1)S(1)} %get-tuple-element.70), channel_id=1, source_target_pairs={{0,16},{8,24},{16,0},{24,8},{1,17},{9,25},{17,1},{25,9},{2,18},{10... | collective-permute-start | bytes 737288 | tf_op jit(solution)/shard_map/ppermute | solution.py:33
  16.4 11.6 %collective-permute-start.2 = (bf16[8,120,128]{2,1,0:T(8,128)(2,1)S(1)}, bf16[8,120,128]{2,1,0:T(8,128)(2,1)S(1)}, u32[]{:S(2)}, u32[]{:S(2)}) collective-permute-start(bf16[8,120,128]{2,1,0:T(8,128)(2,1)S(1)} %get-tuple-element.70), channel_id=1, source_target_pairs={{0,24},{8,16},{16,8},{24,0},{1,25},{9,17},{17,9},{25,1},{2,26},{10... | collective-permute-start | bytes 737288 | tf_op jit(solution)/shard_map/ppermute | solution.py:33
  20.1 13.1 %collective-permute-start.26 = (bf16[224,608]{1,0:T(8,128)(2,1)S(1)}, bf16[224,608]{1,0:T(8,128)(2,1)S(1)}, u32[]{:S(2)}, u32[]{:S(2)}) collective-permute-start(bf16[224,608]{1,0:T(8,128)(2,1)S(1)} %get-tuple-element.76), channel_id=1, source_target_pairs={{0,8},{8,0},{16,24},{24,16},{1,9},{9,1},{17,25},{25,17},{2,10},{10... | collective-permute-start | bytes 817160 | tf_op jit(solution)/shard_map/ppermute | solution.py:33
  23.5 15.2 %collective-permute-start.27 = (bf16[224,608]{1,0:T(8,128)(2,1)S(1)}, bf16[224,608]{1,0:T(8,128)(2,1)S(1)}, u32[]{:S(2)}, u32[]{:S(2)}) collective-permute-start(bf16[224,608]{1,0:T(8,128)(2,1)S(1)} %get-tuple-element.77), channel_id=1, source_target_pairs={{0,16},{8,24},{16,0},{24,8},{1,17},{9,25},{17,1},{25,9},{2,18},{10... | collective-permute-start | bytes 817160 | tf_op jit(solution)/shard_map/ppermute | solution.py:33
  23.5 15.2 %collective-permute-start.28 = (bf16[224,608]{1,0:T(8,128)(2,1)S(1)}, bf16[224,608]{1,0:T(8,128)(2,1)S(1)}, u32[]{:S(2)}, u32[]{:S(2)}) collective-permute-start(bf16[224,608]{1,0:T(8,128)(2,1)S(1)} %get-tuple-element.78), channel_id=1, source_target_pairs={{0,24},{8,16},{16,8},{24,0},{1,25},{9,17},{17,9},{25,1},{2,26},{10... | collective-permute-start | bytes 817160 | tf_op jit(solution)/shard_map/ppermute | solution.py:33
  26.8 12.4 %collective-permute-start.3 = (bf16[8,120,128]{2,1,0:T(8,128)(2,1)S(1)}, bf16[8,120,128]{2,1,0:T(8,128)(2,1)S(1)}, u32[]{:S(2)}, u32[]{:S(2)}) collective-permute-start(bf16[8,120,128]{2,1,0:T(8,128)(2,1)S(1)} %collective-permute-done.rest_0_), channel_id=1, source_target_pairs={{0,2},{1,3},{2,0},{3,1},{4,6},{5,7},{6,4},{7,5},{8,10},{9,11},{10,... | collective-permute-start | bytes 737288 | tf_op jit(solution)/shard_map/ppermute | solution.py:38
  42.5 11.3 %collective-permute-start.29 = (bf16[224,608]{1,0:T(8,128)(2,1)S(1)}, bf16[224,608]{1,0:T(8,128)(2,1)S(1)}, u32[]{:S(2)}, u32[]{:S(2)}) collective-permute-start(bf16[224,608]{1,0:T(8,128)(2,1)S(1)} %collective-permute-done.26.rest_9_), channel_id=1, source_target_pairs={{0,2},{1,3},{2,0},{3,1},{4,6},{5,7},{6,4},{7,5},{8,10},{9,11},{10,... | collective-permute-start | bytes 817160 | tf_op jit(solution)/shard_map/ppermute | solution.py:38
  44.1 14.3 %collective-permute-start.30 = (bf16[224,608]{1,0:T(8,128)(2,1)S(1)}, bf16[224,608]{1,0:T(8,128)(2,1)S(1)}, u32[]{:S(2)}, u32[]{:S(2)}) collective-permute-start(bf16[224,608]{1,0:T(8,128)(2,1)S(1)} %collective-permute-done.27.rest_10_), channel_id=1, source_target_pairs={{0,2},{1,3},{2,0},{3,1},{4,6},{5,7},{6,4},{7,5},{8,10},{9,11},{10,... | collective-permute-start | bytes 817160 | tf_op jit(solution)/shard_map/ppermute | solution.py:38
  52.4 11.3 %collective-permute-start.21 = (bf16[128,896]{1,0:T(8,128)(2,1)S(1)}, bf16[128,896]{1,0:T(8,128)(2,1)S(1)}, u32[]{:S(2)}, u32[]{:S(2)}) collective-permute-start(bf16[128,896]{1,0:T(8,128)(2,1)S(1)} %get-tuple-element.74.rest_0_), channel_id=1, source_target_pairs={{0,24},{8,16},{16,8},{24,0},{1,25},{9,17},{17,9},{25,1},{2,26},{10... | collective-permute-start | bytes 688136 | tf_op jit(solution)/shard_map/ppermute | solution.py:33
  53.8 12.7 %collective-permute-start.31 = (bf16[224,608]{1,0:T(8,128)(2,1)S(1)}, bf16[224,608]{1,0:T(8,128)(2,1)S(1)}, u32[]{:S(2)}, u32[]{:S(2)}) collective-permute-start(bf16[224,608]{1,0:T(8,128)(2,1)S(1)} %collective-permute-done.28.rest_11_), channel_id=1, source_target_pairs={{0,2},{1,3},{2,0},{3,1},{4,6},{5,7},{6,4},{7,5},{8,10},{9,11},{10,... | collective-permute-start | bytes 817160 | tf_op jit(solution)/shard_map/ppermute | solution.py:38
  81.3 12.3 %collective-permute-start.38 = (bf16[128,896]{1,0:T(8,128)(2,1)S(1)}, bf16[128,896]{1,0:T(8,128)(2,1)S(1)}, u32[]{:S(2)}, u32[]{:S(2)}) collective-permute-start(bf16[128,896]{1,0:T(8,128)(2,1)S(1)} %get-tuple-element.94), channel_id=1, source_target_pairs={{0,16},{8,24},{16,0},{24,8},{1,17},{9,25},{17,1},{25,9},{2,18},{10... | collective-permute-start | bytes 688136 | tf_op jit(solution)/shard_map/ppermute | solution.py:33
  100.7 37.5 %collective-permute-start.40 = (bf16[4,1864,128]{2,1,0:T(8,128)(2,1)S(1)}, bf16[4,1864,128]{2,1,0:T(8,128)(2,1)S(1)}, u32[]{:S(2)}, u32[]{:S(2)}) collective-permute-start(bf16[4,1864,128]{2,1,0:T(8,128)(2,1)S(1)} %get-tuple-element.109), channel_id=1, source_target_pairs={{0,1},{1,0},{2,3},{3,2},{4,5},{5,4},{6,7},{7,6},{8,9},{9,8},{10,11... | collective-permute-start | bytes 5726216 | tf_op jit(solution)/shard_map/ppermute | solution.py:28
  104.5 16.1 %collective-permute-start.48 = (bf16[448,608]{1,0:T(8,128)(2,1)S(1)}, bf16[448,608]{1,0:T(8,128)(2,1)S(1)}, u32[]{:S(2)}, u32[]{:S(2)}) collective-permute-start(bf16[448,608]{1,0:T(8,128)(2,1)S(1)} %get-tuple-element.120), channel_id=1, source_target_pairs={{0,2},{1,3},{6,4},{7,5},{8,10},{9,11},{14,12},{15,13},{16,18},{17,... | collective-permute-start | bytes 1634312 | tf_op jit(solution)/shard_map/ppermute | solution.py:51
  108.0 15.9 %collective-permute-start.51 = (bf16[448,608]{1,0:T(8,128)(2,1)S(1)}, bf16[448,608]{1,0:T(8,128)(2,1)S(1)}, u32[]{:S(2)}, u32[]{:S(2)}) collective-permute-start(bf16[448,608]{1,0:T(8,128)(2,1)S(1)} %get-tuple-element.121), channel_id=1, source_target_pairs={{0,8},{8,0},{16,24},{24,16},{1,9},{9,1},{17,25},{25,17},{2,10},{10... | collective-permute-start | bytes 1634312 | tf_op jit(solution)/shard_map/ppermute | solution.py:33
  109.5 25.3 %collective-permute-start.55 = (bf16[448,608]{1,0:T(8,128)(2,1)S(1)}, bf16[448,608]{1,0:T(8,128)(2,1)S(1)}, u32[]{:S(2)}, u32[]{:S(2)}) collective-permute-start(bf16[448,608]{1,0:T(8,128)(2,1)S(1)} %get-tuple-element.122), channel_id=1, source_target_pairs={{0,16},{8,24},{16,0},{24,8},{1,17},{9,25},{17,1},{25,9},{2,18},{10... | collective-permute-start | bytes 1634312 | tf_op jit(solution)/shard_map/ppermute | solution.py:33
  110.2 26.5 %collective-permute-start.59 = (bf16[448,608]{1,0:T(8,128)(2,1)S(1)}, bf16[448,608]{1,0:T(8,128)(2,1)S(1)}, u32[]{:S(2)}, u32[]{:S(2)}) collective-permute-start(bf16[448,608]{1,0:T(8,128)(2,1)S(1)} %get-tuple-element.123), channel_id=1, source_target_pairs={{0,24},{8,16},{16,8},{24,0},{1,25},{9,17},{17,9},{25,1},{2,26},{10... | collective-permute-start | bytes 1634312 | tf_op jit(solution)/shard_map/ppermute | solution.py:33
  120.6 30.9 %collective-permute-start.32 = (bf16[512,896]{1,0:T(8,128)(2,1)S(1)}, bf16[512,896]{1,0:T(8,128)(2,1)S(1)}, u32[]{:S(2)}, u32[]{:S(2)}) collective-permute-start(bf16[512,896]{1,0:T(8,128)(2,1)S(1)} %get-tuple-element.81), channel_id=1, source_target_pairs={{0,1},{1,0},{2,3},{3,2},{4,5},{5,4},{6,7},{7,6},{8,9},{9,8},{10,11... | collective-permute-start | bytes 2752520 | tf_op jit(solution)/shard_map/ppermute | solution.py:28
  123.9 16.6 %collective-permute-start.67 = (bf16[304,896]{1,0:T(8,128)(2,1)S(1)}, bf16[304,896]{1,0:T(8,128)(2,1)S(1)}, u32[]{:S(2)}, u32[]{:S(2)}) collective-permute-start(bf16[304,896]{1,0:T(8,128)(2,1)S(1)} %get-tuple-element.126), channel_id=1, source_target_pairs={{0,2},{1,3},{6,4},{7,5},{8,10},{9,11},{14,12},{15,13},{16,18},{17,... | collective-permute-start | bytes 1634312 | tf_op jit(solution)/shard_map/ppermute | solution.py:51
  134.9 14.8 %collective-permute-start.70 = (bf16[304,896]{1,0:T(8,128)(2,1)S(1)}, bf16[304,896]{1,0:T(8,128)(2,1)S(1)}, u32[]{:S(2)}, u32[]{:S(2)}) collective-permute-start(bf16[304,896]{1,0:T(8,128)(2,1)S(1)} %get-tuple-element.127), channel_id=1, source_target_pairs={{0,2},{1,3},{6,4},{7,5},{8,10},{9,11},{14,12},{15,13},{16,18},{17,... | collective-permute-start | bytes 1634312 | tf_op jit(solution)/shard_map/ppermute | solution.py:51
  136.7 25.3 %collective-permute-start.52 = (bf16[448,608]{1,0:T(8,128)(2,1)S(1)}, bf16[448,608]{1,0:T(8,128)(2,1)S(1)}, u32[]{:S(2)}, u32[]{:S(2)}) collective-permute-start(bf16[448,608]{1,0:T(8,128)(2,1)S(1)} %collective-permute-done.51), channel_id=1, source_target_pairs={{0,2},{1,3},{6,4},{7,5},{8,10},{9,11},{14,12},{15,13},{16,18},{17,... | collective-permute-start | bytes 1634312 | tf_op jit(solution)/shard_map/ppermute | solution.py:51
  138.2 36.0 %collective-permute-start.56 = (bf16[448,608]{1,0:T(8,128)(2,1)S(1)}, bf16[448,608]{1,0:T(8,128)(2,1)S(1)}, u32[]{:S(2)}, u32[]{:S(2)}) collective-permute-start(bf16[448,608]{1,0:T(8,128)(2,1)S(1)} %collective-permute-done.55), channel_id=1, source_target_pairs={{0,2},{1,3},{6,4},{7,5},{8,10},{9,11},{14,12},{15,13},{16,18},{17,... | collective-permute-start | bytes 1634312 | tf_op jit(solution)/shard_map/ppermute | solution.py:51
  140.5 34.4 %collective-permute-start.41 = (bf16[1864,128]{1,0:T(8,128)(2,1)S(1)}, bf16[1864,128]{1,0:T(8,128)(2,1)S(1)}, u32[]{:S(2)}, u32[]{:S(2)}) collective-permute-start(bf16[1864,128]{1,0:T(8,128)(2,1)S(1)} %get-tuple-element.111), channel_id=1, source_target_pairs={{0,8},{8,0},{16,24},{24,16},{1,9},{9,1},{17,25},{25,17},{2,10},{10... | collective-permute-start | bytes 1431560 | tf_op jit(solution)/shard_map/ppermute | solution.py:33
  149.6 26.1 %collective-permute-start.42 = (bf16[1864,128]{1,0:T(8,128)(2,1)S(1)}, bf16[1864,128]{1,0:T(8,128)(2,1)S(1)}, u32[]{:S(2)}, u32[]{:S(2)}) collective-permute-start(bf16[1864,128]{1,0:T(8,128)(2,1)S(1)} %get-tuple-element.112), channel_id=1, source_target_pairs={{0,16},{8,24},{16,0},{24,8},{1,17},{9,25},{17,1},{25,9},{2,18},{10... | collective-permute-start | bytes 1431560 | tf_op jit(solution)/shard_map/ppermute | solution.py:33
  151.6 25.0 %collective-permute-start.43 = (bf16[1864,128]{1,0:T(8,128)(2,1)S(1)}, bf16[1864,128]{1,0:T(8,128)(2,1)S(1)}, u32[]{:S(2)}, u32[]{:S(2)}) collective-permute-start(bf16[1864,128]{1,0:T(8,128)(2,1)S(1)} %get-tuple-element.113), channel_id=1, source_target_pairs={{0,24},{8,16},{16,8},{24,0},{1,25},{9,17},{17,9},{25,1},{2,26},{10... | collective-permute-start | bytes 1431560 | tf_op jit(solution)/shard_map/ppermute | solution.py:33
  161.9 23.9 %collective-permute-start.60 = (bf16[448,608]{1,0:T(8,128)(2,1)S(1)}, bf16[448,608]{1,0:T(8,128)(2,1)S(1)}, u32[]{:S(2)}, u32[]{:S(2)}) collective-permute-start(bf16[448,608]{1,0:T(8,128)(2,1)S(1)} %collective-permute-done.59), channel_id=1, source_target_pairs={{0,2},{1,3},{6,4},{7,5},{8,10},{9,11},{14,12},{15,13},{16,18},{17,... | collective-permute-start | bytes 1634312 | tf_op jit(solution)/shard_map/ppermute | solution.py:51
  174.2 17.5 %collective-permute-start.49 = (bf16[448,608]{1,0:T(8,128)(2,1)S(1)}, bf16[448,608]{1,0:T(8,128)(2,1)S(1)}, u32[]{:S(2)}, u32[]{:S(2)}) collective-permute-start(bf16[448,608]{1,0:T(8,128)(2,1)S(1)} %add.44), channel_id=1, source_target_pairs={{2,4},{3,5},{4,2},{5,3},{10,12},{11,13},{12,10},{13,11},{18,20},{1... | collective-permute-start | bytes 1634312 | tf_op jit(solution)/shard_map/ppermute | solution.py:51
  174.9 17.6 %collective-permute-start.68 = (bf16[304,896]{1,0:T(8,128)(2,1)S(1)}, bf16[304,896]{1,0:T(8,128)(2,1)S(1)}, u32[]{:S(2)}, u32[]{:S(2)}) collective-permute-start(bf16[304,896]{1,0:T(8,128)(2,1)S(1)} %add.52), channel_id=1, source_target_pairs={{2,4},{3,5},{4,2},{5,3},{10,12},{11,13},{12,10},{13,11},{18,20},{1... | collective-permute-start | bytes 1634312 | tf_op jit(solution)/shard_map/ppermute | solution.py:51
  175.8 17.5 %collective-permute-start.71 = (bf16[304,896]{1,0:T(8,128)(2,1)S(1)}, bf16[304,896]{1,0:T(8,128)(2,1)S(1)}, u32[]{:S(2)}, u32[]{:S(2)}) collective-permute-start(bf16[304,896]{1,0:T(8,128)(2,1)S(1)} %add.54), channel_id=1, source_target_pairs={{2,4},{3,5},{4,2},{5,3},{10,12},{11,13},{12,10},{13,11},{18,20},{1... | collective-permute-start | bytes 1634312 | tf_op jit(solution)/shard_map/ppermute | solution.py:51
  176.6 18.1 %collective-permute-start.53 = (bf16[448,608]{1,0:T(8,128)(2,1)S(1)}, bf16[448,608]{1,0:T(8,128)(2,1)S(1)}, u32[]{:S(2)}, u32[]{:S(2)}) collective-permute-start(bf16[448,608]{1,0:T(8,128)(2,1)S(1)} %add.46), channel_id=1, source_target_pairs={{2,4},{3,5},{4,2},{5,3},{10,12},{11,13},{12,10},{13,11},{18,20},{1... | collective-permute-start | bytes 1634312 | tf_op jit(solution)/shard_map/ppermute | solution.py:51
  185.8 14.2 %collective-permute-start.44 = (bf16[1864,128]{1,0:T(8,128)(2,1)S(1)}, bf16[1864,128]{1,0:T(8,128)(2,1)S(1)}, u32[]{:S(2)}, u32[]{:S(2)}) collective-permute-start(bf16[1864,128]{1,0:T(8,128)(2,1)S(1)} %shard_map.198), channel_id=1, source_target_pairs={{0,2},{1,3},{6,4},{7,5},{8,10},{9,11},{14,12},{15,13},{16,18},{17,... | collective-permute-start | bytes 1431560 | tf_op jit(solution)/shard_map/ppermute | solution.py:51
  191.8 15.0 %collective-permute-start.57 = (bf16[448,608]{1,0:T(8,128)(2,1)S(1)}, bf16[448,608]{1,0:T(8,128)(2,1)S(1)}, u32[]{:S(2)}, u32[]{:S(2)}) collective-permute-start(bf16[448,608]{1,0:T(8,128)(2,1)S(1)} %add.48), channel_id=1, source_target_pairs={{2,4},{3,5},{4,2},{5,3},{10,12},{11,13},{12,10},{13,11},{18,20},{1... | collective-permute-start | bytes 1634312 | tf_op jit(solution)/shard_map/ppermute | solution.py:51
  192.5 15.6 %collective-permute-start.61 = (bf16[448,608]{1,0:T(8,128)(2,1)S(1)}, bf16[448,608]{1,0:T(8,128)(2,1)S(1)}, u32[]{:S(2)}, u32[]{:S(2)}) collective-permute-start(bf16[448,608]{1,0:T(8,128)(2,1)S(1)} %add.50), channel_id=1, source_target_pairs={{2,4},{3,5},{4,2},{5,3},{10,12},{11,13},{12,10},{13,11},{18,20},{1... | collective-permute-start | bytes 1634312 | tf_op jit(solution)/shard_map/ppermute | solution.py:51
  193.3 34.2 %collective-permute-start.69 = (bf16[304,896]{1,0:T(8,128)(2,1)S(1)}, bf16[304,896]{1,0:T(8,128)(2,1)S(1)}, u32[]{:S(2)}, u32[]{:S(2)}) collective-permute-start(bf16[304,896]{1,0:T(8,128)(2,1)S(1)} %add.53.total), channel_id=1, source_target_pairs={{2,0},{3,1},{4,6},{5,7},{10,8},{11,9},{12,14},{13,15},{18,16},{19,... | collective-permute-start | bytes 1634312 | tf_op jit(solution)/shard_map/ppermute | solution.py:51
  194.8 45.0 %collective-permute-start.72 = (bf16[304,896]{1,0:T(8,128)(2,1)S(1)}, bf16[304,896]{1,0:T(8,128)(2,1)S(1)}, u32[]{:S(2)}, u32[]{:S(2)}) collective-permute-start(bf16[304,896]{1,0:T(8,128)(2,1)S(1)} %add.55.total), channel_id=1, source_target_pairs={{2,0},{3,1},{4,6},{5,7},{10,8},{11,9},{12,14},{13,15},{18,16},{19,... | collective-permute-start | bytes 1634312 | tf_op jit(solution)/shard_map/ppermute | solution.py:51
  206.0 35.6 %collective-permute-start.45 = (bf16[1864,128]{1,0:T(8,128)(2,1)S(1)}, bf16[1864,128]{1,0:T(8,128)(2,1)S(1)}, u32[]{:S(2)}, u32[]{:S(2)}) collective-permute-start(bf16[1864,128]{1,0:T(8,128)(2,1)S(1)} %add.42), channel_id=1, source_target_pairs={{2,4},{3,5},{4,2},{5,3},{10,12},{11,13},{12,10},{13,11},{18,20},{1... | collective-permute-start | bytes 1431560 | tf_op jit(solution)/shard_map/ppermute | solution.py:51
  206.7 45.9 %collective-permute-start.50 = (bf16[448,608]{1,0:T(8,128)(2,1)S(1)}, bf16[448,608]{1,0:T(8,128)(2,1)S(1)}, u32[]{:S(2)}, u32[]{:S(2)}) collective-permute-start(bf16[448,608]{1,0:T(8,128)(2,1)S(1)} %add.45.total), channel_id=1, source_target_pairs={{2,0},{3,1},{4,6},{5,7},{10,8},{11,9},{12,14},{13,15},{18,16},{19,... | collective-permute-start | bytes 1634312 | tf_op jit(solution)/shard_map/ppermute | solution.py:51
  208.1 61.7 %collective-permute-start.54 = (bf16[448,608]{1,0:T(8,128)(2,1)S(1)}, bf16[448,608]{1,0:T(8,128)(2,1)S(1)}, u32[]{:S(2)}, u32[]{:S(2)}) collective-permute-start(bf16[448,608]{1,0:T(8,128)(2,1)S(1)} %add.47.total), channel_id=1, source_target_pairs={{2,0},{3,1},{4,6},{5,7},{10,8},{11,9},{12,14},{13,15},{18,16},{19,... | collective-permute-start | bytes 1634312 | tf_op jit(solution)/shard_map/ppermute | solution.py:51
  227.5 54.5 %collective-permute-start.58 = (bf16[448,608]{1,0:T(8,128)(2,1)S(1)}, bf16[448,608]{1,0:T(8,128)(2,1)S(1)}, u32[]{:S(2)}, u32[]{:S(2)}) collective-permute-start(bf16[448,608]{1,0:T(8,128)(2,1)S(1)} %add.49.total), channel_id=1, source_target_pairs={{2,0},{3,1},{4,6},{5,7},{10,8},{11,9},{12,14},{13,15},{18,16},{19,... | collective-permute-start | bytes 1634312 | tf_op jit(solution)/shard_map/ppermute | solution.py:51
  239.8 54.5 %collective-permute-start.62 = (bf16[448,608]{1,0:T(8,128)(2,1)S(1)}, bf16[448,608]{1,0:T(8,128)(2,1)S(1)}, u32[]{:S(2)}, u32[]{:S(2)}) collective-permute-start(bf16[448,608]{1,0:T(8,128)(2,1)S(1)} %add.51.total), channel_id=1, source_target_pairs={{2,0},{3,1},{4,6},{5,7},{10,8},{11,9},{12,14},{13,15},{18,16},{19,... | collective-permute-start | bytes 1634312 | tf_op jit(solution)/shard_map/ppermute | solution.py:51
  241.7 59.5 %collective-permute-start.73 = (bf16[304,896]{1,0:T(8,128)(2,1)S(1)}, bf16[304,896]{1,0:T(8,128)(2,1)S(1)}, u32[]{:S(2)}, u32[]{:S(2)}) collective-permute-start(bf16[304,896]{1,0:T(8,128)(2,1)S(1)} %shard_map.208.rest_0_), channel_id=1, source_target_pairs={{0,1},{1,0},{2,3},{3,2},{4,5},{5,4},{6,7},{7,6},{8,9},{9,8},{10,11... | collective-permute-start | bytes 1634312 | tf_op jit(solution)/shard_map/ppermute | solution.py:28
  252.7 49.0 %collective-permute-start.46 = (bf16[1864,128]{1,0:T(8,128)(2,1)S(1)}, bf16[1864,128]{1,0:T(8,128)(2,1)S(1)}, u32[]{:S(2)}, u32[]{:S(2)}) collective-permute-start(bf16[1864,128]{1,0:T(8,128)(2,1)S(1)} %add.43.total), channel_id=1, source_target_pairs={{2,0},{3,1},{4,6},{5,7},{10,8},{11,9},{12,14},{13,15},{18,16},{19,... | collective-permute-start | bytes 1431560 | tf_op jit(solution)/shard_map/ppermute | solution.py:51
  269.7 32.7 %collective-permute-start.74 = (bf16[304,896]{1,0:T(8,128)(2,1)S(1)}, bf16[304,896]{1,0:T(8,128)(2,1)S(1)}, u32[]{:S(2)}, u32[]{:S(2)}) collective-permute-start(bf16[304,896]{1,0:T(8,128)(2,1)S(1)} %shard_map.209.rest_1_), channel_id=1, source_target_pairs={{0,1},{1,0},{2,3},{3,2},{4,5},{5,4},{6,7},{7,6},{8,9},{9,8},{10,11... | collective-permute-start | bytes 1634312 | tf_op jit(solution)/shard_map/ppermute | solution.py:28
  282.0 16.7 %collective-permute-start.34 = (bf16[128,896]{1,0:T(8,128)(2,1)S(1)}, bf16[128,896]{1,0:T(8,128)(2,1)S(1)}, u32[]{:S(2)}, u32[]{:S(2)}) collective-permute-start(bf16[128,896]{1,0:T(8,128)(2,1)S(1)} %get-tuple-element.84), channel_id=1, source_target_pairs={{0,16},{8,24},{16,0},{24,8},{1,17},{9,25},{17,1},{25,9},{2,18},{10... | collective-permute-start | bytes 688136 | tf_op jit(solution)/shard_map/ppermute | solution.py:33
  302.4 11.3 %collective-permute-start.47 = (bf16[1864,128]{1,0:T(8,128)(2,1)S(1)}, bf16[1864,128]{1,0:T(8,128)(2,1)S(1)}, u32[]{:S(2)}, u32[]{:S(2)}) collective-permute-start(bf16[1864,128]{1,0:T(8,128)(2,1)S(1)} %shard_map.199.mine), channel_id=1, source_target_pairs={{0,1},{1,0},{2,3},{3,2},{4,5},{5,4},{6,7},{7,6},{8,9},{9,8},{10,11... | collective-permute-start | bytes 1431560 | tf_op jit(solution)/shard_map/ppermute | solution.py:28
  (33 other events, 368.8 us)

commit v3 on v2

--- a/solution.py
+++ b/solution.py
@@ -74,7 +74,7 @@
     return lax.dot_general(a, b, (((0,), (0,)), ((), ())), preferred_element_type=F32)
 
 
-GRANTS = {'pack': 12, 'attend': 5, 'down_back': 5, 'feed': 9, 'narrow': 4, 'back': 18, 'wide': 8, 'merge': 5, 'finish': 4, 'lay': 18, 'close': 6, 'ydown': 4, 'open': 3, 'yout': 4, 'pick': 4, 'stack': 8}
+GRANTS = {'pack': 12, 'attend': 5, 'down_back': 5, 'feed': 9, 'narrow': 4, 'back': 18, 'wide': 8, 'merge': 5, 'finish': 4, 'lay': 24, 'close': 6, 'ydown': 4, 'open': 3, 'yout': 4, 'pick': 4, 'stack': 8}
 
 
 def call(kernel, name, outs, where, args, scratch=(), flops=0, space=pltpu.VMEM):
@@ -99,19 +99,6 @@
 
 def rows_at(start, size):
     return pl.ds(pl.multiple_of(start, 8 if size % 16 else 16), size)
-
-
-def mark_kernel(where, out):
-    for i in range(out.shape[0]):
-        out[i] = where[i]
-
-
-def mark(where):
-    smem = pl.BlockSpec(memory_space=pltpu.SMEM)
-    return pl.pallas_call(
-        mark_kernel, out_shape=shape(where.shape, jnp.int32), in_specs=[smem], out_specs=smem,
-        compiler_params=pltpu.CompilerParams(vmem_limit_bytes=1 << 20),
-    )(where)
 
 
 def pack_kernel(shards, where, gate, up, *rest):
@@ -439,22 +426,50 @@
     )
 
 
+def dense_plan(rows, slab):
+    whole, rest = slab // LANES, slab % LANES
+    fold = LANES // math.gcd(rest, LANES) if rest else 1
+    if rest == 0 or rows % (8 * fold):
+        fold = 1
+    part = rows // fold
+    blocks = -(-fold * rest // LANES)
+    return whole, rest, fold, part, blocks, whole * rows + blocks * part
+
+
 def wide_kernel(shards, where, n, dgate, dup, *rest):
     outs, acc = rest[:shards], rest[shards]
-    rows = outs[0].shape[0] // 2
+    width, slab = acc.shape
+    rows = width // shards
+    whole, rest, fold, part, blocks, tall = dense_plan(rows, slab)
     s = where[0]
-    acc[...] = t_dot(n[...], dgate[...])
-    for k in range(shards):
-        outs[k][:rows] = acc[rows_at((s ^ k) * rows, rows)].astype(BF)
-    acc[...] = t_dot(n[...], dup[...])
-    for k in range(shards):
-        outs[k][rows:] = acc[rows_at((s ^ k) * rows, rows)].astype(BF)
+    for m, d in enumerate((dgate, dup)):
+        acc[...] = t_dot(n[...], d[...])
+        for k in range(shards):
+            top = (s ^ k) * rows
+            base = m * tall
+            for b in range(whole):
+                lanes = slice(b * LANES, (b + 1) * LANES)
+                outs[k][base : base + rows] = acc[rows_at(top, rows), lanes].astype(BF)
+                base += rows
+            if rest:
+                folded = [
+                    acc[pl.ds(pl.multiple_of(top + i * part, 8), part), whole * LANES :]
+                    for i in range(fold)
+                ]
+                gap = blocks * LANES - fold * rest
+                if gap:
+                    folded.append(jnp.zeros((part, gap), F32))
+                folded = jnp.concatenate(folded, axis=1) if len(folded) > 1 else folded[0]
+                for b in range(blocks):
+                    lanes = slice(b * LANES, (b + 1) * LANES)
+                    outs[k][base : base + part] = folded[:, lanes].astype(BF)
+                    base += part
 
 
 def wide(where, n, dgate, dup, shards):
     total, width = n.shape
     slab = dgate.shape[1]
-    outs = [shape((2 * width // shards, slab))] * shards
+    outs = [shape((2 * dense_plan(width // shards, slab)[-1], LANES))] * shards
     return call(
         functools.partial(wide_kernel, shards), "wide", outs, where, [n, dgate, dup],
         [pltpu.VMEM((width, slab), F32)], flops=4 * total * width * slab,
@@ -464,24 +479,43 @@
 def lay_kernel(shards, where, *rest):
     mine, other = rest[:shards], rest[shards : 2 * shards]
     gate_ref, up_ref, stage = rest[2 * shards :]
-    rows, slab = gate_ref.shape[0], stage.shape[2]
+    rows, slab = stage.shape[1] // 2, stage.shape[2]
+    whole, rest, fold, part, blocks, tall = dense_plan(rows, slab)
     s, c = where[0], where[1]
-    for k in range(shards):
-        stage[k] = mine[k][...]
-        stage[shards + k] = other[k][...]
-    for j in range(2 * shards):
-        at = ((j // 2) ^ s) + jnp.where(c == j % 2, 0, shards)
-        gate_ref[:, j * slab : (j + 1) * slab] = stage[at, :rows].astype(F32)
-        up_ref[:, j * slab : (j + 1) * slab] = stage[at, rows:].astype(F32)
-
-
-def lay(where, mine, other):
+    for k, source in enumerate((*mine, *other)):
+        for m in range(2):
+            base = m * tall
+            for b in range(whole):
+                lanes = slice(b * LANES, (b + 1) * LANES)
+                stage[k, m * rows : (m + 1) * rows, lanes] = source[base : base + rows].astype(F32)
+                base += rows
+            if rest:
+                folded = [
+                    source[base + b * part : base + (b + 1) * part].astype(F32)
+                    for b in range(blocks)
+                ]
+                folded = jnp.concatenate(folded, axis=1) if blocks > 1 else folded[0]
+                for i in range(fold):
+                    at = slice(m * rows + i * part, m * rows + (i + 1) * part)
+                    stage[k, at, whole * LANES :] = folded[:, i * rest : (i + 1) * rest]
+    step = rows // 4 if rows % 32 == 0 else rows
+
+    @pl.loop(0, rows // step)
+    def _(i):
+        top = pl.multiple_of(i * step, 8)
+        for j in range(2 * shards):
+            at = ((j // 2) ^ s) + jnp.where(c == j % 2, 0, shards)
+            lanes = slice(j * slab, (j + 1) * slab)
+            gate_ref[pl.ds(top, step), lanes] = stage[at, pl.ds(top, step)]
+            up_ref[pl.ds(top, step), lanes] = stage[at, pl.ds(pl.multiple_of(top + rows, 8), step)]
+
+
+def lay(where, mine, other, rows, slab):
     shards = len(mine)
-    rows, slab = mine[0].shape[0] // 2, mine[0].shape[1]
     outs = [shape((rows, 2 * shards * slab), F32)] * 2
     return call(
         functools.partial(lay_kernel, shards), "lay", outs, where, [*mine, *other],
-        [pltpu.VMEM((2 * shards, 2 * rows, slab), BF)],
+        [pltpu.VMEM((2 * shards, 2 * rows, slab), F32)],
     )
 
 
@@ -577,7 +611,9 @@
 
     blank = jnp.zeros((5, LANES), F32)
     for target, side in ((keep, c), (give, 1 - c)):
-        for k in range(shards):
+
+        @pl.loop(0, shards)
+        def _(k, target=target, side=side):
             at = rows_at((s ^ k) * rows + side * half, half)
             for b in range(joined // LANES):
                 lanes = slice(b * LANES, (b + 1) * LANES)
@@ -691,21 +727,32 @@
     rest[-1][...] = value.astype(BF)
 
 
-def finish(where, parts):
-    return call(finish_kernel, "finish", [shape(parts[0].shape)], where, parts)[0]
-
-
-def close_kernel(tall, where, mine, other, qkv_ref, out_ref, one_ref, two_ref, bias_ref):
+def finish_cut_kernel(tall, where, own, *rest):
+    arrived, (first, second) = rest[:-2], rest[-2:]
+    for out, at in ((first, slice(0, tall)), (second, slice(tall, own.shape[0]))):
+        value = own[at]
+        for piece in arrived:
+            value = value + piece[at].astype(F32)
+        out[...] = value.astype(BF)
+
+
+def finish(where, parts, tall):
+    outs = [shape((tall, LANES)), shape((parts[0].shape[0] - tall, LANES))]
+    return call(functools.partial(finish_cut_kernel, tall), "finish", outs, where, parts)
+
+
+def close_kernel(where, mine, mine_out, other, other_out, *refs):
+    qkv_ref, out_ref, one_ref, two_ref, bias_ref = refs
     s, c = where[0], where[1]
     half = qkv_ref.shape[0] // 2
-    for source, side in ((mine, c), (other, 1 - c)):
+    for source, source_out, side in ((mine, mine_out, c), (other, other_out, 1 - c)):
         at = pl.ds(pl.multiple_of(side * half, 8), half)
         for b in range(qkv_ref.shape[1] // LANES):
             base = b * (half + 8)
             qkv_ref[at, b * LANES : (b + 1) * LANES] = source[base : base + half].astype(F32)
         for b in range(out_ref.shape[1] // LANES):
-            base = tall + b * half
-            out_ref[at, b * LANES : (b + 1) * LANES] = source[base : base + half].astype(F32)
+            base = b * half
+            out_ref[at, b * LANES : (b + 1) * LANES] = source_out[base : base + half].astype(F32)
     starts = [b * (half + 8) + half for b in range(qkv_ref.shape[1] // LANES)]
     vec = jnp.concatenate([mine[at : at + 8].astype(F32) for at in starts], axis=1)
     width = vec.shape[1]
@@ -714,10 +761,10 @@
         ref[...] = turned[i, : ref.shape[0]]
 
 
-def close(where, mine, other, rows, width, joined, tall):
+def close(where, parts, rows, width, joined):
     outs = [shape((rows, joined), F32), shape((rows, width), F32)]
     outs += [shape((n,), F32) for n in (rows, rows, joined * rows // width)]
-    return call(functools.partial(close_kernel, tall), "close", outs, where, [mine, other])
+    return call(close_kernel, "close", outs, where, parts)
 
 
 def body(
@@ -768,8 +815,7 @@
     grads = wide(where, n_all, d_gate, d_up, shards)
     grads = [grads[0]] + [shard_swap(grads[k], k) for k in range(1, shards)]
     grads = [line_sum(where, g) for g in grads]
-    marked = mark(where)
-    gate_part, up_part = lay(marked, grads, [swap_core(g) for g in grads])
+    gate_part, up_part = lay(where, grads, [swap_core(g) for g in grads], rows, slab)
 
     down_part = stack(where, [down_one, down_two], [swap_core(down_one), swap_core(down_two)])
     y = plane_sum(*down_project(where, act, w_down))
@@ -781,9 +827,11 @@
     )
     parts = plane_sum(keep, give)
     tall, _ = layout_of(width, joined, rows)
-    item = line_sum(where, finish(where, parts))
+    first, second = finish(where, parts, tall)
+    first, second = line_sum(where, first), line_sum(where, second)
+    swapped = swap_core(first), swap_core(second)
     qkv_part, out_part, one_part, two_part, bias_part = close(
-        where, item, swap_core(item), rows, width, joined, tall
+        where, [first, second, *swapped], rows, width, joined
     )
     return (
         layer_out,

time: 316 us -> 297 us (0.940)
  waiting for transfers between devices: 176 us -> 142 us
  starting transfers between devices: 79.9 us -> 93.4 us
    ppermute x21 -> x24, waiting for transfers between devices: 119 us -> 69.4 us  [hop(): return lax.ppermute(value, 'replica', links)]
    ppermute x21 -> x24, starting transfers between devices: 33.1 us -> 49.1 us  [hop(): return lax.ppermute(value, 'replica', links)]
    ppermute x24, waiting for transfers between devices: 50.3 us -> 63.1 us  [shard_swap(): return lax.ppermute(x, 'shard', [(i, i ^ k) for i in range(n)])]
    ppermute x6, waiting for transfers between devices: 4.44 us -> 9.67 us  [pair_swap(): return lax.ppermute(x, 'replica', [(i, i ^ 2) for i in range(n)])]
    pallas_call x24 -> x25, Pallas kernels: 55 us -> 56.9 us  [call(): pl.pallas_call(kernel, out_shape=outs, in_specs=[pl.BlockSpec(memory_spac...]
  transfers between devices with their start and end apart: 75 -> 79, of which waited for: 30 -> 29; matrix products, arithmetic and copies ran while one was open for 1% -> 1% of each run, Pallas kernels for 11% -> 15%
where the time goes in v3:
time: 297 us; the launch traced here: 296 us
  waiting for transfers between devices  142 us (48%)
  starting transfers between devices  93.4 us (31%)
  Pallas kernels  56.9 us (19%)
    ppermute x24, waiting for transfers between devices, hop(): return lax.ppermute(value, 'replica', links)  69.4 us
    ppermute x24, waiting for transfers between devices, shard_swap(): return lax.ppermute(x, 'shard', [(i, i ^ k) for i in range(n)])  63.1 us
    pallas_call x25, Pallas kernels, call(): pl.pallas_call(kernel, out_shape=outs, in_specs=[pl.BlockSpec(memory_spac...  56.9 us
    ppermute x24, starting transfers between devices, hop(): return lax.ppermute(value, 'replica', links)  49.1 us
    ppermute x24, starting transfers between devices, shard_swap(): return lax.ppermute(x, 'shard', [(i, i ^ k) for i in range(n)])  32.6 us
    ppermute x6, waiting for transfers between devices, pair_swap(): return lax.ppermute(x, 'replica', [(i, i ^ 2) for i in range(n)])  9.67 us
    ppermute x6, starting transfers between devices, pair_swap(): return lax.ppermute(x, 'replica', [(i, i ^ 2) for i in range(n)])  7.2 us
  transfers between devices with their start and end apart: 79, of which 29 were waited for; matrix products, arithmetic and copies ran while one was open for 1% of the time, Pallas kernels for 15%

profile of v3, /device:TPU:0, one launch (start us, length us, event | category | flops | bytes accessed | tf_op | source)
XLA Modules:
  0.0 296.0 jit_solution(12324648310495769372)
XLA Ops:
  1.2 3.5 %collective-permute-start.14 = (bf16[128,896]{1,0:T(8,128)(2,1)}, bf16[128,896]{1,0:T(8,128)(2,1)S(1)}, u32[]{:S(2)}, u32[]{:S(2)}) collective-permute-start(bf16[128,896]{1,0:T(8,128)(2,1)} %rest_5_.1), channel_id=1, source_target_pairs={{0,24},{8,16},{16,8},{24,0},{1,25},{9,17},{17,9},{25,1},{2,26},{10... | collective-permute-start | bytes 688136 | tf_op jit(solution)/shard_map/ppermute | solution.py:33
  7.1 2.9 collective-permute-start.2
  11.4 2.0 collective-permute-start
  13.4 3.2 %shard_map.189 = (bf16[448,608]{1,0:T(8,128)(2,1)S(1)}, bf16[224,608]{1,0:T(8,128)(2,1)S(1)}, bf16[224,608]{1,0:T(8,128)(2,1)S(1)}, bf16[224,608]{1,0:T(8,128)(2,1)S(1)}) custom-call(s32[3]{0:T(128)S(1)} %pad_add_fusion.where, bf16[224,4864]{1,0:T(8,128)(2,1)} %gate.1, bf16[224,4864]{1,0:T(8,128)(2,1)} %up.1), custom_call_target="tpu_custom_call" | custom-call | bytes 5720064 | tf_op jit(solution)/shard_map/pallas_call | solution.py:85
  16.6 1.8 collective-permute-start.26
  19.2 2.5 collective-permute-done.2.rest_2_
  21.6 2.9 collective-permute-start.28
  24.6 2.1 collective-permute-done.1.rest_1_
  29.0 4.6 %collective-permute-done.26.rest_9_ = bf16[224,608]{1,0:T(8,128)(2,1)S(1)} collective-permute-done((bf16[224,608]{1,0:T(8,128)(2,1)S(1)}, bf16[224,608]{1,0:T(8,128)(2,1)S(1)}, u32[]{:S(2)}, u32[]{:S(2)}) %collective-permute-start.26) | collective-permute-done | bytes 272416 | tf_op jit(solution)/shard_map/ppermute | solution.py:33
  35.6 3.3 %collective-permute-done.28.rest_11_ = bf16[224,608]{1,0:T(8,128)(2,1)S(1)} collective-permute-done((bf16[224,608]{1,0:T(8,128)(2,1)S(1)}, bf16[224,608]{1,0:T(8,128)(2,1)S(1)}, u32[]{:S(2)}, u32[]{:S(2)}) %collective-permute-start.28) | collective-permute-done | bytes 272416 | tf_op jit(solution)/shard_map/ppermute | solution.py:33
  39.5 2.9 collective-permute-done.4.rest_4_
  42.4 3.3 %collective-permute-done.3.rest_3_ = bf16[8,120,128]{2,1,0:T(8,128)(2,1)S(1)} collective-permute-done((bf16[8,120,128]{2,1,0:T(8,128)(2,1)S(1)}, bf16[8,120,128]{2,1,0:T(8,128)(2,1)S(1)}, u32[]{:S(2)}, u32[]{:S(2)}) %collective-permute-start.3) | collective-permute-done | bytes 245792 | tf_op jit(solution)/shard_map/ppermute | solution.py:38
  48.9 5.2 %shard_map.187 = (bf16[128,896]{1,0:T(8,128)(2,1)S(1)}, bf16[128,896]{1,0:T(8,128)(2,1)S(1)}, bf16[128,128]{1,0:T(8,128)(2,1)S(1)}, bf16[128,128]{1,0:T(8,128)(2...) custom-call(s32[3]{0:T(128)S(1)} %pad_add_fusion.where, ...), custom_call_target="tpu_custom_call" | custom-call | flops 704643072 | bytes 10308096 | tf_op jit(solution)/shard_map/pallas_call | solution.py:85
  54.1 2.5 collective-permute-start.21
  59.2 3.4 %collective-permute-done.30.rest_13_ = bf16[224,608]{1,0:T(8,128)(2,1)S(1)} collective-permute-done((bf16[224,608]{1,0:T(8,128)(2,1)S(1)}, bf16[224,608]{1,0:T(8,128)(2,1)S(1)}, u32[]{:S(2)}, u32[]{:S(2)}) %collective-permute-start.30) | collective-permute-done | bytes 272416 | tf_op jit(solution)/shard_map/ppermute | solution.py:38
  63.6 3.8 %collective-permute-done.20.rest_2_ = bf16[128,896]{1,0:T(8,128)(2,1)S(1)} collective-permute-done((bf16[128,896]{1,0:T(8,128)(2,1)S(1)}, bf16[128,896]{1,0:T(8,128)(2,1)S(1)}, u32[]{:S(2)}, u32[]{:S(2)}) %collective-permute-start.20) | collective-permute-done | bytes 229408 | tf_op jit(solution)/shard_map/ppermute | solution.py:33
  67.8 2.8 shard_map.188
  70.7 6.5 %shard_map.190 = (bf16[304,896]{1,0:T(8,128)(2,1)S(1)}, bf16[304,896]{1,0:T(8,128)(2,1)S(1)}, bf16[1024,608]{1,0:T(8,128)(2,1)S(1)}, bf16[1024,608]{1,0:T(8,128)...) custom-call(s32[3]{0:T(128)S(1)} %pad_add_fusion.where, ...), custom_call_target="tpu_custom_call" | custom-call | flops 3347054592 | bytes 17178624 | tf_op jit(solution)/shard_map/pallas_call | solution.py:85
  77.1 3.9 %shard_map.194 = (f32[512,896]{1,0:T(8,128)S(1)}, bf16[512,896]{1,0:T(8,128)(2,1)S(1)}) custom-call(s32[3]{0:T(128)S(1)} %pad_add_fusion.where, bf16[1024,608]{1,0:T(8,128)(2,1)S(1)} %get-tuple-element.88.dgate, bf16[1024,608]{1,0:T(8,128)(2,1)S(1)} %get-tuple-element.89.dup, bf16[896,608]{1,0:T(8,128)(2,1)S(1)} %get-tuple-element.90.wg, ...), custom_call_target="tpu_custom_call" | custom-call | flops 2231369728 | bytes 7421952 | tf_op jit(solution)/shard_map/pallas_call | solution.py:85
  81.2 3.1 %collective-permute-start.71 = (bf16[304,896]{1,0:T(8,128)(2,1)S(1)}, bf16[304,896]{1,0:T(8,128)(2,1)S(1)}, u32[]{:S(2)}, u32[]{:S(2)}) collective-permute-start(bf16[304,896]{1,0:T(8,128)(2,1)S(1)} %get-tuple-element.130), channel_id=1, source_target_pairs={{0,2},{1,3},{6,4},{7,5},{8,10},{9,11},{14,12},{15,13},{16,18},{17,... | collective-permute-start | bytes 1634312 | tf_op jit(solution)/shard_map/ppermute | solution.py:51
  88.6 2.4 collective-permute-start.74
  91.0 3.8 %shard_map.202 = (bf16[2128,128]{1,0:T(8,128)(2,1)S(1)}, bf16[2128,128]{1,0:T(8,128)(2,1)S(1)}, bf16[2128,128]{1,0:T(8,128)(2,1)S(1)}, bf16[2128,128]{1,0:T(8,128)(2,1)S(1)}) custom-call(s32[3]{0:T(128)S(1)} %pad_add_fusion.where, bf16[1024,896]{1,0:T(8,128)(2,1)S(1)} %get-tuple-element.123.n, bf16[1024,608]{1,0:T(8,128)(2,1)S(1)} %get-tuple-element.88.dgate, ...), custom_call_target="tpu_custom_call" | custom-call | flops 2231369728 | bytes 6504448 | tf_op jit(solution)/shard_map/pallas_call | solution.py:85
  96.4 1.9 collective-permute-done.38.rest_2_
  99.4 7.1 %shard_map.196 = (f32[128,896]{1,0:T(8,128)}, f32[4,1864,128]{2,1,0:T(8,128)S(1)}, bf16[4,1864,128]{2,1,0:T(8,128)(2,1)S(1)}) custom-call(s32[3]{0:T(128)S(1)} %pad_add_fusion.where, f32[128,896]{1,0:T(8,128)S(1)} %get-tuple-element.94.rest_0_, bf16[128,896]{1,0:T(8,128)(2,1)S(1)} %collective-permute-done.37.rest_1_, ...), custom_call_target="tpu_custom_call" | custom-call | flops 939524096 | bytes 13758464 | tf_op jit(solution)/shard_map/pallas_call | solution.py:85
  108.7 2.3 shard_map.191
  111.1 2.4 collective-permute-start.52
  113.7 19.3 %collective-permute-done.59 = bf16[2128,128]{1,0:T(8,128)(2,1)S(1)} collective-permute-done((bf16[2128,128]{1,0:T(8,128)(2,1)S(1)}, bf16[2128,128]{1,0:T(8,128)(2,1)S(1)}, u32[]{:S(2)}, u32[]{:S(2)}) %collective-permute-start.59) | collective-permute-done | bytes 544800 | tf_op jit(solution)/shard_map/ppermute | solution.py:33
  133.6 5.6 %collective-permute-start.56 = (bf16[2128,128]{1,0:T(8,128)(2,1)S(1)}, bf16[2128,128]{1,0:T(8,128)(2,1)S(1)}, u32[]{:S(2)}, u32[]{:S(2)}) collective-permute-start(bf16[2128,128]{1,0:T(8,128)(2,1)S(1)} %collective-permute-done.55), channel_id=1, source_target_pairs={{0,2},{1,3},{6,4},{7,5},{8,10},{9,11},{14,12},{15,13},{16,18},{17,... | collective-permute-start | bytes 1634312 | tf_op jit(solution)/shard_map/ppermute | solution.py:51
  140.1 2.6 collective-permute-start.60
  142.7 9.8 %collective-permute-start.64 = (bf16[2128,128]{1,0:T(8,128)(2,1)S(1)}, bf16[2128,128]{1,0:T(8,128)(2,1)S(1)}, u32[]{:S(2)}, u32[]{:S(2)}) collective-permute-start(bf16[2128,128]{1,0:T(8,128)(2,1)S(1)} %collective-permute-done.63), channel_id=1, source_target_pairs={{0,2},{1,3},{6,4},{7,5},{8,10},{9,11},{14,12},{15,13},{16,18},{17,... | collective-permute-start | bytes 1634312 | tf_op jit(solution)/shard_map/ppermute | solution.py:51
  154.9 8.7 %collective-permute-done.60 = bf16[2128,128]{1,0:T(8,128)(2,1)S(1)} collective-permute-done((bf16[2128,128]{1,0:T(8,128)(2,1)S(1)}, bf16[2128,128]{1,0:T(8,128)(2,1)S(1)}, u32[]{:S(2)}, u32[]{:S(2)}) %collective-permute-start.60) | collective-permute-done | bytes 544800 | tf_op jit(solution)/shard_map/ppermute | solution.py:51
  164.5 9.2 %collective-permute-done.64 = bf16[2128,128]{1,0:T(8,128)(2,1)S(1)} collective-permute-done((bf16[2128,128]{1,0:T(8,128)(2,1)S(1)}, bf16[2128,128]{1,0:T(8,128)(2,1)S(1)}, u32[]{:S(2)}, u32[]{:S(2)}) %collective-permute-start.64) | collective-permute-done | bytes 544800 | tf_op jit(solution)/shard_map/ppermute | solution.py:51
  175.0 1.7 collective-permute-start.35
  179.1 6.3 %collective-permute-done.34.rest_2_ = bf16[128,896]{1,0:T(8,128)(2,1)S(1)} collective-permute-done((bf16[128,896]{1,0:T(8,128)(2,1)S(1)}, bf16[128,896]{1,0:T(8,128)(2,1)S(1)}, u32[]{:S(2)}, u32[]{:S(2)}) %collective-permute-start.34) | collective-permute-done | bytes 229408 | tf_op jit(solution)/shard_map/ppermute | solution.py:33
  185.9 1.7 collective-permute-start.43
  190.0 4.7 %collective-permute-done.41.rest_0_ = bf16[1864,128]{1,0:T(8,128)(2,1)S(1)} collective-permute-done((bf16[1864,128]{1,0:T(8,128)(2,1)S(1)}, bf16[1864,128]{1,0:T(8,128)(2,1)S(1)}, u32[]{:S(2)}, u32[]{:S(2)}) %collective-permute-start.41) | collective-permute-done | bytes 477216 | tf_op jit(solution)/shard_map/ppermute | solution.py:33
  196.2 10.9 %collective-permute-done.42.rest_1_ = bf16[1864,128]{1,0:T(8,128)(2,1)S(1)} collective-permute-done((bf16[1864,128]{1,0:T(8,128)(2,1)S(1)}, bf16[1864,128]{1,0:T(8,128)(2,1)S(1)}, u32[]{:S(2)}, u32[]{:S(2)}) %collective-permute-start.42) | collective-permute-done | bytes 477216 | tf_op jit(solution)/shard_map/ppermute | solution.py:33
  210.7 5.8 %collective-permute-start.44 = (bf16[1080,128]{1,0:T(8,128)(2,1)S(1)}, bf16[1080,128]{1,0:T(8,128)(2,1)S(1)}, u32[]{:S(2)}, u32[]{:S(2)}) collective-permute-start(bf16[1080,128]{1,0:T(8,128)(2,1)S(1)} %get-tuple-element.116), channel_id=1, source_target_pairs={{0,2},{1,3},{6,4},{7,5},{8,10},{9,11},{14,12},{15,13},{16,18},{17,... | collective-permute-start | bytes 829448 | tf_op jit(solution)/shard_map/ppermute | solution.py:51
  218.1 2.4 collective-permute-done.44
  225.3 9.8 %collective-permute-done.54.arrived = bf16[2128,128]{1,0:T(8,128)(2,1)S(1)} collective-permute-done((bf16[2128,128]{1,0:T(8,128)(2,1)S(1)}, bf16[2128,128]{1,0:T(8,128)(2,1)S(1)}, u32[]{:S(2)}, u32[]{:S(2)}) %collective-permute-start.54) | collective-permute-done | bytes 544800 | tf_op jit(solution)/shard_map/ppermute | solution.py:51
  235.1 11.7 %collective-permute-done.58.arrived = bf16[2128,128]{1,0:T(8,128)(2,1)S(1)} collective-permute-done((bf16[2128,128]{1,0:T(8,128)(2,1)S(1)}, bf16[2128,128]{1,0:T(8,128)(2,1)S(1)}, u32[]{:S(2)}, u32[]{:S(2)}) %collective-permute-start.58) | collective-permute-done | bytes 544800 | tf_op jit(solution)/shard_map/ppermute | solution.py:51
  248.3 4.9 %collective-permute-done.47 = bf16[784,128]{1,0:T(8,128)(2,1)S(1)} collective-permute-done((bf16[784,128]{1,0:T(8,128)(2,1)S(1)}, bf16[784,128]{1,0:T(8,128)(2,1)S(1)}, u32[]{:S(2)}, u32[]{:S(2)}) %collective-permute-start.47) | collective-permute-done | bytes 200736 | tf_op jit(solution)/shard_map/ppermute | solution.py:51
  255.2 3.3 %collective-permute-done.62.arrived = bf16[2128,128]{1,0:T(8,128)(2,1)S(1)} collective-permute-done((bf16[2128,128]{1,0:T(8,128)(2,1)S(1)}, bf16[2128,128]{1,0:T(8,128)(2,1)S(1)}, u32[]{:S(2)}, u32[]{:S(2)}) %collective-permute-start.62) | collective-permute-done | bytes 544800 | tf_op jit(solution)/shard_map/ppermute | solution.py:51
  259.1 11.0 %collective-permute-done.66.arrived = bf16[2128,128]{1,0:T(8,128)(2,1)S(1)} collective-permute-done((bf16[2128,128]{1,0:T(8,128)(2,1)S(1)}, bf16[2128,128]{1,0:T(8,128)(2,1)S(1)}, u32[]{:S(2)}, u32[]{:S(2)}) %collective-permute-start.66) | collective-permute-done | bytes 544800 | tf_op jit(solution)/shard_map/ppermute | solution.py:51
  275.1 6.8 %collective-permute-done.49.arrived = bf16[784,128]{1,0:T(8,128)(2,1)S(1)} collective-permute-done((bf16[784,128]{1,0:T(8,128)(2,1)S(1)}, bf16[784,128]{1,0:T(8,128)(2,1)S(1)}, u32[]{:S(2)}, u32[]{:S(2)}) %collective-permute-start.49) | collective-permute-done | bytes 200736 | tf_op jit(solution)/shard_map/ppermute | solution.py:51
  284.5 2.9 shard_map.210
  287.4 6.8 %shard_map.207 = (f32[224,4864]{1,0:T(8,128)}, f32[224,4864]{1,0:T(8,128)}) custom-call(s32[3]{0:T(128)S(1)} %pad_add_fusion.where, bf16[2128,128]{1,0:T(8,128)(2,1)S(1)} %shard_map.203.rest_0_, bf16[2128,128]{1,0:T(8,128)(2,1)S(1)} %shard_map.204.rest_1_, bf16[2128,128]{1,0:T(8,128)(2,1)S(1)} %shard_map.205.rest_2_, ...), custom_call_target="tpu_custom_call" | custom-call | bytes 13074432 | tf_op jit(solution)/shard_map/pallas_call | solution.py:85
  294.2 1.8 shard_map.201
  (164 shorter events, 61.1 us)
Async XLA Ops:
  5.2 13.1 %collective-permute-start.12 = (bf16[128,896]{1,0:T(8,128)(2,1)}, bf16[128,896]{1,0:T(8,128)(2,1)S(1)}, u32[]{:S(2)}, u32[]{:S(2)}) collective-permute-start(bf16[128,896]{1,0:T(8,128)(2,1)} %rest_5_.1), channel_id=1, source_target_pairs={{0,8},{8,0},{16,24},{24,16},{1,9},{9,1},{17,25},{25,17},{2,10},{10... | collective-permute-start | bytes 688136 | tf_op jit(solution)/shard_map/ppermute | solution.py:33
  7.1 14.6 %collective-permute-start.2 = (bf16[8,120,128]{2,1,0:T(8,128)(2,1)S(1)}, bf16[8,120,128]{2,1,0:T(8,128)(2,1)S(1)}, u32[]{:S(2)}, u32[]{:S(2)}) collective-permute-start(bf16[8,120,128]{2,1,0:T(8,128)(2,1)S(1)} %get-tuple-element.72), channel_id=1, source_target_pairs={{0,24},{8,16},{16,8},{24,0},{1,25},{9,17},{17,9},{25,1},{2,26},{10... | collective-permute-start | bytes 737288 | tf_op jit(solution)/shard_map/ppermute | solution.py:33
  10.0 16.7 %collective-permute-start.1 = (bf16[8,120,128]{2,1,0:T(8,128)(2,1)S(1)}, bf16[8,120,128]{2,1,0:T(8,128)(2,1)S(1)}, u32[]{:S(2)}, u32[]{:S(2)}) collective-permute-start(bf16[8,120,128]{2,1,0:T(8,128)(2,1)S(1)} %get-tuple-element.72), channel_id=1, source_target_pairs={{0,16},{8,24},{16,0},{24,8},{1,17},{9,25},{17,1},{25,9},{2,18},{10... | collective-permute-start | bytes 737288 | tf_op jit(solution)/shard_map/ppermute | solution.py:33
  11.4 16.0 %collective-permute-start = (bf16[8,120,128]{2,1,0:T(8,128)(2,1)S(1)}, bf16[8,120,128]{2,1,0:T(8,128)(2,1)S(1)}, u32[]{:S(2)}, u32[]{:S(2)}) collective-permute-start(bf16[8,120,128]{2,1,0:T(8,128)(2,1)S(1)} %get-tuple-element.72), channel_id=1, source_target_pairs={{0,8},{8,0},{16,24},{24,16},{1,9},{9,1},{17,25},{25,17},{2,10},{10... | collective-permute-start | bytes 737288 | tf_op jit(solution)/shard_map/ppermute | solution.py:33
  16.6 17.0 %collective-permute-start.26 = (bf16[224,608]{1,0:T(8,128)(2,1)S(1)}, bf16[224,608]{1,0:T(8,128)(2,1)S(1)}, u32[]{:S(2)}, u32[]{:S(2)}) collective-permute-start(bf16[224,608]{1,0:T(8,128)(2,1)S(1)} %get-tuple-element.78), channel_id=1, source_target_pairs={{0,8},{8,0},{16,24},{24,16},{1,9},{9,1},{17,25},{25,17},{2,10},{10... | collective-permute-start | bytes 817160 | tf_op jit(solution)/shard_map/ppermute | solution.py:33
  18.3 16.8 %collective-permute-start.27 = (bf16[224,608]{1,0:T(8,128)(2,1)S(1)}, bf16[224,608]{1,0:T(8,128)(2,1)S(1)}, u32[]{:S(2)}, u32[]{:S(2)}) collective-permute-start(bf16[224,608]{1,0:T(8,128)(2,1)S(1)} %get-tuple-element.79), channel_id=1, source_target_pairs={{0,16},{8,24},{16,0},{24,8},{1,17},{9,25},{17,1},{25,9},{2,18},{10... | collective-permute-start | bytes 817160 | tf_op jit(solution)/shard_map/ppermute | solution.py:33
  21.6 17.3 %collective-permute-start.28 = (bf16[224,608]{1,0:T(8,128)(2,1)S(1)}, bf16[224,608]{1,0:T(8,128)(2,1)S(1)}, u32[]{:S(2)}, u32[]{:S(2)}) collective-permute-start(bf16[224,608]{1,0:T(8,128)(2,1)S(1)} %get-tuple-element.80), channel_id=1, source_target_pairs={{0,24},{8,16},{16,8},{24,0},{1,25},{9,17},{17,9},{25,1},{2,26},{10... | collective-permute-start | bytes 817160 | tf_op jit(solution)/shard_map/ppermute | solution.py:33
  26.6 12.3 %collective-permute-start.8 = (bf16[8,120,128]{2,1,0:T(8,128)(2,1)S(1)}, bf16[8,120,128]{2,1,0:T(8,128)(2,1)S(1)}, u32[]{:S(2)}, u32[]{:S(2)}) collective-permute-start(bf16[8,120,128]{2,1,0:T(8,128)(2,1)S(1)} %collective-permute-done.2.rest_2_), channel_id=1, source_target_pairs={{0,1},{1,0},{2,3},{3,2},{4,5},{5,4},{6,7},{7,6},{8,9},{9,8},{10,11... | collective-permute-start | bytes 737288 | tf_op jit(solution)/shard_map/ppermute | solution.py:28
  27.4 12.0 %collective-permute-start.5 = (bf16[8,120,128]{2,1,0:T(8,128)(2,1)S(1)}, bf16[8,120,128]{2,1,0:T(8,128)(2,1)S(1)}, u32[]{:S(2)}, u32[]{:S(2)}) collective-permute-start(bf16[8,120,128]{2,1,0:T(8,128)(2,1)S(1)} %collective-permute-done.2.rest_2_), channel_id=1, source_target_pairs={{0,2},{1,3},{2,0},{3,1},{4,6},{5,7},{6,4},{7,5},{8,10},{9,11},{10,... | collective-permute-start | bytes 737288 | tf_op jit(solution)/shard_map/ppermute | solution.py:38
  48.4 14.3 %collective-permute-start.30 = (bf16[224,608]{1,0:T(8,128)(2,1)S(1)}, bf16[224,608]{1,0:T(8,128)(2,1)S(1)}, u32[]{:S(2)}, u32[]{:S(2)}) collective-permute-start(bf16[224,608]{1,0:T(8,128)(2,1)S(1)} %collective-permute-done.27.rest_10_), channel_id=1, source_target_pairs={{0,2},{1,3},{2,0},{3,1},{4,6},{5,7},{6,4},{7,5},{8,10},{9,11},{10,... | collective-permute-start | bytes 817160 | tf_op jit(solution)/shard_map/ppermute | solution.py:38
  57.6 13.0 %collective-permute-start.31 = (bf16[224,608]{1,0:T(8,128)(2,1)S(1)}, bf16[224,608]{1,0:T(8,128)(2,1)S(1)}, u32[]{:S(2)}, u32[]{:S(2)}) collective-permute-start(bf16[224,608]{1,0:T(8,128)(2,1)S(1)} %collective-permute-done.28.rest_11_), channel_id=1, source_target_pairs={{0,2},{1,3},{2,0},{3,1},{4,6},{5,7},{6,4},{7,5},{8,10},{9,11},{10,... | collective-permute-start | bytes 817160 | tf_op jit(solution)/shard_map/ppermute | solution.py:38
  81.2 25.9 %collective-permute-start.71 = (bf16[304,896]{1,0:T(8,128)(2,1)S(1)}, bf16[304,896]{1,0:T(8,128)(2,1)S(1)}, u32[]{:S(2)}, u32[]{:S(2)}) collective-permute-start(bf16[304,896]{1,0:T(8,128)(2,1)S(1)} %get-tuple-element.130), channel_id=1, source_target_pairs={{0,2},{1,3},{6,4},{7,5},{8,10},{9,11},{14,12},{15,13},{16,18},{17,... | collective-permute-start | bytes 1634312 | tf_op jit(solution)/shard_map/ppermute | solution.py:51
  87.4 12.1 %collective-permute-start.39 = (bf16[128,896]{1,0:T(8,128)(2,1)S(1)}, bf16[128,896]{1,0:T(8,128)(2,1)S(1)}, u32[]{:S(2)}, u32[]{:S(2)}) collective-permute-start(bf16[128,896]{1,0:T(8,128)(2,1)S(1)} %get-tuple-element.97), channel_id=1, source_target_pairs={{0,24},{8,16},{16,8},{24,0},{1,25},{9,17},{17,9},{25,1},{2,26},{10... | collective-permute-start | bytes 688136 | tf_op jit(solution)/shard_map/ppermute | solution.py:33
  88.6 22.4 %collective-permute-start.74 = (bf16[304,896]{1,0:T(8,128)(2,1)S(1)}, bf16[304,896]{1,0:T(8,128)(2,1)S(1)}, u32[]{:S(2)}, u32[]{:S(2)}) collective-permute-start(bf16[304,896]{1,0:T(8,128)(2,1)S(1)} %get-tuple-element.131), channel_id=1, source_target_pairs={{0,2},{1,3},{6,4},{7,5},{8,10},{9,11},{14,12},{15,13},{16,18},{17,... | collective-permute-start | bytes 1634312 | tf_op jit(solution)/shard_map/ppermute | solution.py:51
  94.8 16.3 %collective-permute-start.55 = (bf16[2128,128]{1,0:T(8,128)(2,1)S(1)}, bf16[2128,128]{1,0:T(8,128)(2,1)S(1)}, u32[]{:S(2)}, u32[]{:S(2)}) collective-permute-start(bf16[2128,128]{1,0:T(8,128)(2,1)S(1)} %get-tuple-element.125), channel_id=1, source_target_pairs={{0,8},{8,0},{16,24},{24,16},{1,9},{9,1},{17,25},{25,17},{2,10},{10... | collective-permute-start | bytes 1634312 | tf_op jit(solution)/shard_map/ppermute | solution.py:33
  106.5 68.5 %collective-permute-start.40 = (bf16[4,1864,128]{2,1,0:T(8,128)(2,1)S(1)}, bf16[4,1864,128]{2,1,0:T(8,128)(2,1)S(1)}, u32[]{:S(2)}, u32[]{:S(2)}) collective-permute-start(bf16[4,1864,128]{2,1,0:T(8,128)(2,1)S(1)} %get-tuple-element.111), channel_id=1, source_target_pairs={{0,1},{1,0},{2,3},{3,2},{4,5},{5,4},{6,7},{7,6},{8,9},{9,8},{10,11... | collective-permute-start | bytes 5726216 | tf_op jit(solution)/shard_map/ppermute | solution.py:28
  106.5 26.4 %collective-permute-start.59 = (bf16[2128,128]{1,0:T(8,128)(2,1)S(1)}, bf16[2128,128]{1,0:T(8,128)(2,1)S(1)}, u32[]{:S(2)}, u32[]{:S(2)}) collective-permute-start(bf16[2128,128]{1,0:T(8,128)(2,1)S(1)} %get-tuple-element.126), channel_id=1, source_target_pairs={{0,16},{8,24},{16,0},{24,8},{1,17},{9,25},{17,1},{25,9},{2,18},{10... | collective-permute-start | bytes 1634312 | tf_op jit(solution)/shard_map/ppermute | solution.py:33
  107.1 26.6 %collective-permute-start.63 = (bf16[2128,128]{1,0:T(8,128)(2,1)S(1)}, bf16[2128,128]{1,0:T(8,128)(2,1)S(1)}, u32[]{:S(2)}, u32[]{:S(2)}) collective-permute-start(bf16[2128,128]{1,0:T(8,128)(2,1)S(1)} %get-tuple-element.127), channel_id=1, source_target_pairs={{0,24},{8,16},{16,8},{24,0},{1,25},{9,17},{17,9},{25,1},{2,26},{10... | collective-permute-start | bytes 1634312 | tf_op jit(solution)/shard_map/ppermute | solution.py:33
  111.0 29.1 %collective-permute-start.32 = (bf16[512,896]{1,0:T(8,128)(2,1)S(1)}, bf16[512,896]{1,0:T(8,128)(2,1)S(1)}, u32[]{:S(2)}, u32[]{:S(2)}) collective-permute-start(bf16[512,896]{1,0:T(8,128)(2,1)S(1)} %get-tuple-element.83), channel_id=1, source_target_pairs={{0,1},{1,0},{2,3},{3,2},{4,5},{5,4},{6,7},{7,6},{8,9},{9,8},{10,11... | collective-permute-start | bytes 2752520 | tf_op jit(solution)/shard_map/ppermute | solution.py:28
  111.1 28.3 %collective-permute-start.52 = (bf16[2128,128]{1,0:T(8,128)(2,1)S(1)}, bf16[2128,128]{1,0:T(8,128)(2,1)S(1)}, u32[]{:S(2)}, u32[]{:S(2)}) collective-permute-start(bf16[2128,128]{1,0:T(8,128)(2,1)S(1)} %get-tuple-element.124), channel_id=1, source_target_pairs={{0,2},{1,3},{6,4},{7,5},{8,10},{9,11},{14,12},{15,13},{16,18},{17,... | collective-permute-start | bytes 1634312 | tf_op jit(solution)/shard_map/ppermute | solution.py:51
  133.6 19.0 %collective-permute-start.56 = (bf16[2128,128]{1,0:T(8,128)(2,1)S(1)}, bf16[2128,128]{1,0:T(8,128)(2,1)S(1)}, u32[]{:S(2)}, u32[]{:S(2)}) collective-permute-start(bf16[2128,128]{1,0:T(8,128)(2,1)S(1)} %collective-permute-done.55), channel_id=1, source_target_pairs={{0,2},{1,3},{6,4},{7,5},{8,10},{9,11},{14,12},{15,13},{16,18},{17,... | collective-permute-start | bytes 1634312 | tf_op jit(solution)/shard_map/ppermute | solution.py:51
  139.4 14.1 %collective-permute-start.75 = (bf16[304,896]{1,0:T(8,128)(2,1)S(1)}, bf16[304,896]{1,0:T(8,128)(2,1)S(1)}, u32[]{:S(2)}, u32[]{:S(2)}) collective-permute-start(bf16[304,896]{1,0:T(8,128)(2,1)S(1)} %add.62), channel_id=1, source_target_pairs={{2,4},{3,5},{4,2},{5,3},{10,12},{11,13},{12,10},{13,11},{18,20},{1... | collective-permute-start | bytes 1634312 | tf_op jit(solution)/shard_map/ppermute | solution.py:51
  140.1 23.5 %collective-permute-start.60 = (bf16[2128,128]{1,0:T(8,128)(2,1)S(1)}, bf16[2128,128]{1,0:T(8,128)(2,1)S(1)}, u32[]{:S(2)}, u32[]{:S(2)}) collective-permute-start(bf16[2128,128]{1,0:T(8,128)(2,1)S(1)} %collective-permute-done.59), channel_id=1, source_target_pairs={{0,2},{1,3},{6,4},{7,5},{8,10},{9,11},{14,12},{15,13},{16,18},{17,... | collective-permute-start | bytes 1634312 | tf_op jit(solution)/shard_map/ppermute | solution.py:51
  142.7 31.0 %collective-permute-start.64 = (bf16[2128,128]{1,0:T(8,128)(2,1)S(1)}, bf16[2128,128]{1,0:T(8,128)(2,1)S(1)}, u32[]{:S(2)}, u32[]{:S(2)}) collective-permute-start(bf16[2128,128]{1,0:T(8,128)(2,1)S(1)} %collective-permute-done.63), channel_id=1, source_target_pairs={{0,2},{1,3},{6,4},{7,5},{8,10},{9,11},{14,12},{15,13},{16,18},{17,... | collective-permute-start | bytes 1634312 | tf_op jit(solution)/shard_map/ppermute | solution.py:51
  152.7 21.7 %collective-permute-start.53 = (bf16[2128,128]{1,0:T(8,128)(2,1)S(1)}, bf16[2128,128]{1,0:T(8,128)(2,1)S(1)}, u32[]{:S(2)}, u32[]{:S(2)}) collective-permute-start(bf16[2128,128]{1,0:T(8,128)(2,1)S(1)} %add.52), channel_id=1, source_target_pairs={{2,4},{3,5},{4,2},{5,3},{10,12},{11,13},{12,10},{13,11},{18,20},{1... | collective-permute-start | bytes 1634312 | tf_op jit(solution)/shard_map/ppermute | solution.py:51
  153.5 34.1 %collective-permute-start.57 = (bf16[2128,128]{1,0:T(8,128)(2,1)S(1)}, bf16[2128,128]{1,0:T(8,128)(2,1)S(1)}, u32[]{:S(2)}, u32[]{:S(2)}) collective-permute-start(bf16[2128,128]{1,0:T(8,128)(2,1)S(1)} %add.54), channel_id=1, source_target_pairs={{2,4},{3,5},{4,2},{5,3},{10,12},{11,13},{12,10},{13,11},{18,20},{1... | collective-permute-start | bytes 1634312 | tf_op jit(solution)/shard_map/ppermute | solution.py:51
  163.6 14.0 %collective-permute-start.33 = (bf16[128,896]{1,0:T(8,128)(2,1)S(1)}, bf16[128,896]{1,0:T(8,128)(2,1)S(1)}, u32[]{:S(2)}, u32[]{:S(2)}) collective-permute-start(bf16[128,896]{1,0:T(8,128)(2,1)S(1)} %get-tuple-element.85), channel_id=1, source_target_pairs={{0,8},{8,0},{16,24},{24,16},{1,9},{9,1},{17,25},{25,17},{2,10},{10... | collective-permute-start | bytes 688136 | tf_op jit(solution)/shard_map/ppermute | solution.py:33
  173.7 14.8 %collective-permute-start.61 = (bf16[2128,128]{1,0:T(8,128)(2,1)S(1)}, bf16[2128,128]{1,0:T(8,128)(2,1)S(1)}, u32[]{:S(2)}, u32[]{:S(2)}) collective-permute-start(bf16[2128,128]{1,0:T(8,128)(2,1)S(1)} %add.56), channel_id=1, source_target_pairs={{2,4},{3,5},{4,2},{5,3},{10,12},{11,13},{12,10},{13,11},{18,20},{1... | collective-permute-start | bytes 1634312 | tf_op jit(solution)/shard_map/ppermute | solution.py:51
  177.7 17.0 %collective-permute-start.41 = (bf16[1864,128]{1,0:T(8,128)(2,1)S(1)}, bf16[1864,128]{1,0:T(8,128)(2,1)S(1)}, u32[]{:S(2)}, u32[]{:S(2)}) collective-permute-start(bf16[1864,128]{1,0:T(8,128)(2,1)S(1)} %get-tuple-element.113), channel_id=1, source_target_pairs={{0,8},{8,0},{16,24},{24,16},{1,9},{9,1},{17,25},{25,17},{2,10},{10... | collective-permute-start | bytes 1431560 | tf_op jit(solution)/shard_map/ppermute | solution.py:33
  185.4 21.7 %collective-permute-start.42 = (bf16[1864,128]{1,0:T(8,128)(2,1)S(1)}, bf16[1864,128]{1,0:T(8,128)(2,1)S(1)}, u32[]{:S(2)}, u32[]{:S(2)}) collective-permute-start(bf16[1864,128]{1,0:T(8,128)(2,1)S(1)} %get-tuple-element.114), channel_id=1, source_target_pairs={{0,16},{8,24},{16,0},{24,8},{1,17},{9,25},{17,1},{25,9},{2,18},{10... | collective-permute-start | bytes 1431560 | tf_op jit(solution)/shard_map/ppermute | solution.py:33
  185.9 22.5 %collective-permute-start.43 = (bf16[1864,128]{1,0:T(8,128)(2,1)S(1)}, bf16[1864,128]{1,0:T(8,128)(2,1)S(1)}, u32[]{:S(2)}, u32[]{:S(2)}) collective-permute-start(bf16[1864,128]{1,0:T(8,128)(2,1)S(1)} %get-tuple-element.115), channel_id=1, source_target_pairs={{0,24},{8,16},{16,8},{24,0},{1,25},{9,17},{17,9},{25,1},{2,26},{10... | collective-permute-start | bytes 1431560 | tf_op jit(solution)/shard_map/ppermute | solution.py:33
  187.7 23.1 %collective-permute-start.65 = (bf16[2128,128]{1,0:T(8,128)(2,1)S(1)}, bf16[2128,128]{1,0:T(8,128)(2,1)S(1)}, u32[]{:S(2)}, u32[]{:S(2)}) collective-permute-start(bf16[2128,128]{1,0:T(8,128)(2,1)S(1)} %add.58), channel_id=1, source_target_pairs={{2,4},{3,5},{4,2},{5,3},{10,12},{11,13},{12,10},{13,11},{18,20},{1... | collective-permute-start | bytes 1634312 | tf_op jit(solution)/shard_map/ppermute | solution.py:51
  188.5 28.3 %collective-permute-start.73 = (bf16[304,896]{1,0:T(8,128)(2,1)S(1)}, bf16[304,896]{1,0:T(8,128)(2,1)S(1)}, u32[]{:S(2)}, u32[]{:S(2)}) collective-permute-start(bf16[304,896]{1,0:T(8,128)(2,1)S(1)} %add.61.total), channel_id=1, source_target_pairs={{2,0},{3,1},{4,6},{5,7},{10,8},{11,9},{12,14},{13,15},{18,16},{19,... | collective-permute-start | bytes 1634312 | tf_op jit(solution)/shard_map/ppermute | solution.py:51
  194.6 28.8 %collective-permute-start.76 = (bf16[304,896]{1,0:T(8,128)(2,1)S(1)}, bf16[304,896]{1,0:T(8,128)(2,1)S(1)}, u32[]{:S(2)}, u32[]{:S(2)}) collective-permute-start(bf16[304,896]{1,0:T(8,128)(2,1)S(1)} %add.63.total), channel_id=1, source_target_pairs={{2,0},{3,1},{4,6},{5,7},{10,8},{11,9},{12,14},{13,15},{18,16},{19,... | collective-permute-start | bytes 1634312 | tf_op jit(solution)/shard_map/ppermute | solution.py:51
  207.1 28.0 %collective-permute-start.54 = (bf16[2128,128]{1,0:T(8,128)(2,1)S(1)}, bf16[2128,128]{1,0:T(8,128)(2,1)S(1)}, u32[]{:S(2)}, u32[]{:S(2)}) collective-permute-start(bf16[2128,128]{1,0:T(8,128)(2,1)S(1)} %add.53.total), channel_id=1, source_target_pairs={{2,0},{3,1},{4,6},{5,7},{10,8},{11,9},{12,14},{13,15},{18,16},{19,... | collective-permute-start | bytes 1634312 | tf_op jit(solution)/shard_map/ppermute | solution.py:51
  208.4 38.3 %collective-permute-start.58 = (bf16[2128,128]{1,0:T(8,128)(2,1)S(1)}, bf16[2128,128]{1,0:T(8,128)(2,1)S(1)}, u32[]{:S(2)}, u32[]{:S(2)}) collective-permute-start(bf16[2128,128]{1,0:T(8,128)(2,1)S(1)} %add.55.total), channel_id=1, source_target_pairs={{2,0},{3,1},{4,6},{5,7},{10,8},{11,9},{12,14},{13,15},{18,16},{19,... | collective-permute-start | bytes 1634312 | tf_op jit(solution)/shard_map/ppermute | solution.py:51
  216.8 41.6 %collective-permute-start.62 = (bf16[2128,128]{1,0:T(8,128)(2,1)S(1)}, bf16[2128,128]{1,0:T(8,128)(2,1)S(1)}, u32[]{:S(2)}, u32[]{:S(2)}) collective-permute-start(bf16[2128,128]{1,0:T(8,128)(2,1)S(1)} %add.57.total), channel_id=1, source_target_pairs={{2,0},{3,1},{4,6},{5,7},{10,8},{11,9},{12,14},{13,15},{18,16},{19,... | collective-permute-start | bytes 1634312 | tf_op jit(solution)/shard_map/ppermute | solution.py:51
  220.5 49.6 %collective-permute-start.66 = (bf16[2128,128]{1,0:T(8,128)(2,1)S(1)}, bf16[2128,128]{1,0:T(8,128)(2,1)S(1)}, u32[]{:S(2)}, u32[]{:S(2)}) collective-permute-start(bf16[2128,128]{1,0:T(8,128)(2,1)S(1)} %add.59.total), channel_id=1, source_target_pairs={{2,0},{3,1},{4,6},{5,7},{10,8},{11,9},{12,14},{13,15},{18,16},{19,... | collective-permute-start | bytes 1634312 | tf_op jit(solution)/shard_map/ppermute | solution.py:51
  223.4 23.4 %collective-permute-start.45 = (bf16[1080,128]{1,0:T(8,128)(2,1)S(1)}, bf16[1080,128]{1,0:T(8,128)(2,1)S(1)}, u32[]{:S(2)}, u32[]{:S(2)}) collective-permute-start(bf16[1080,128]{1,0:T(8,128)(2,1)S(1)} %add.48), channel_id=1, source_target_pairs={{2,4},{3,5},{4,2},{5,3},{10,12},{11,13},{12,10},{13,11},{18,20},{1... | collective-permute-start | bytes 829448 | tf_op jit(solution)/shard_map/ppermute | solution.py:51
  235.1 36.8 %collective-permute-start.77 = (bf16[304,896]{1,0:T(8,128)(2,1)S(1)}, bf16[304,896]{1,0:T(8,128)(2,1)S(1)}, u32[]{:S(2)}, u32[]{:S(2)}) collective-permute-start(bf16[304,896]{1,0:T(8,128)(2,1)S(1)} %shard_map.208.rest_0_), channel_id=1, source_target_pairs={{0,1},{1,0},{2,3},{3,2},{4,5},{5,4},{6,7},{7,6},{8,9},{9,8},{10,11... | collective-permute-start | bytes 1634312 | tf_op jit(solution)/shard_map/ppermute | solution.py:28
  246.8 25.7 %collective-permute-start.78 = (bf16[304,896]{1,0:T(8,128)(2,1)S(1)}, bf16[304,896]{1,0:T(8,128)(2,1)S(1)}, u32[]{:S(2)}, u32[]{:S(2)}) collective-permute-start(bf16[304,896]{1,0:T(8,128)(2,1)S(1)} %shard_map.209.rest_1_), channel_id=1, source_target_pairs={{0,1},{1,0},{2,3},{3,2},{4,5},{5,4},{6,7},{7,6},{8,9},{9,8},{10,11... | collective-permute-start | bytes 1634312 | tf_op jit(solution)/shard_map/ppermute | solution.py:28
  253.2 20.0 %collective-permute-start.46 = (bf16[1080,128]{1,0:T(8,128)(2,1)S(1)}, bf16[1080,128]{1,0:T(8,128)(2,1)S(1)}, u32[]{:S(2)}, u32[]{:S(2)}) collective-permute-start(bf16[1080,128]{1,0:T(8,128)(2,1)S(1)} %add.49.total), channel_id=1, source_target_pairs={{2,0},{3,1},{4,6},{5,7},{10,8},{11,9},{12,14},{13,15},{18,16},{19,... | collective-permute-start | bytes 829448 | tf_op jit(solution)/shard_map/ppermute | solution.py:51
  258.4 14.1 %collective-permute-start.48 = (bf16[784,128]{1,0:T(8,128)(2,1)S(1)}, bf16[784,128]{1,0:T(8,128)(2,1)S(1)}, u32[]{:S(2)}, u32[]{:S(2)}) collective-permute-start(bf16[784,128]{1,0:T(8,128)(2,1)S(1)} %add.50), channel_id=1, source_target_pairs={{2,4},{3,5},{4,2},{5,3},{10,12},{11,13},{12,10},{13,11},{18,20},{1... | collective-permute-start | bytes 602120 | tf_op jit(solution)/shard_map/ppermute | solution.py:51
  270.1 12.4 %collective-permute-start.67 = (bf16[2128,128]{1,0:T(8,128)(2,1)S(1)}, bf16[2128,128]{1,0:T(8,128)(2,1)S(1)}, u32[]{:S(2)}, u32[]{:S(2)}) collective-permute-start(bf16[2128,128]{1,0:T(8,128)(2,1)S(1)} %shard_map.203.rest_0_), channel_id=1, source_target_pairs={{0,1},{1,0},{2,3},{3,2},{4,5},{5,4},{6,7},{7,6},{8,9},{9,8},{10,11... | collective-permute-start | bytes 1634312 | tf_op jit(solution)/shard_map/ppermute | solution.py:28
  271.9 15.5 %collective-permute-start.68 = (bf16[2128,128]{1,0:T(8,128)(2,1)S(1)}, bf16[2128,128]{1,0:T(8,128)(2,1)S(1)}, u32[]{:S(2)}, u32[]{:S(2)}) collective-permute-start(bf16[2128,128]{1,0:T(8,128)(2,1)S(1)} %shard_map.204.rest_1_), channel_id=1, source_target_pairs={{0,1},{1,0},{2,3},{3,2},{4,5},{5,4},{6,7},{7,6},{8,9},{9,8},{10,11... | collective-permute-start | bytes 1634312 | tf_op jit(solution)/shard_map/ppermute | solution.py:28
  272.5 14.9 %collective-permute-start.69 = (bf16[2128,128]{1,0:T(8,128)(2,1)S(1)}, bf16[2128,128]{1,0:T(8,128)(2,1)S(1)}, u32[]{:S(2)}, u32[]{:S(2)}) collective-permute-start(bf16[2128,128]{1,0:T(8,128)(2,1)S(1)} %shard_map.205.rest_2_), channel_id=1, source_target_pairs={{0,1},{1,0},{2,3},{3,2},{4,5},{5,4},{6,7},{7,6},{8,9},{9,8},{10,11... | collective-permute-start | bytes 1634312 | tf_op jit(solution)/shard_map/ppermute | solution.py:28
  272.6 14.8 %collective-permute-start.70 = (bf16[2128,128]{1,0:T(8,128)(2,1)S(1)}, bf16[2128,128]{1,0:T(8,128)(2,1)S(1)}, u32[]{:S(2)}, u32[]{:S(2)}) collective-permute-start(bf16[2128,128]{1,0:T(8,128)(2,1)S(1)} %shard_map.206.rest_3_), channel_id=1, source_target_pairs={{0,1},{1,0},{2,3},{3,2},{4,5},{5,4},{6,7},{7,6},{8,9},{9,8},{10,11... | collective-permute-start | bytes 1634312 | tf_op jit(solution)/shard_map/ppermute | solution.py:28
  281.9 12.3 %collective-permute-start.50 = (bf16[1080,128]{1,0:T(8,128)(2,1)S(1)}, bf16[1080,128]{1,0:T(8,128)(2,1)S(1)}, u32[]{:S(2)}, u32[]{:S(2)}) collective-permute-start(bf16[1080,128]{1,0:T(8,128)(2,1)S(1)} %shard_map.199.mine), channel_id=1, source_target_pairs={{0,1},{1,0},{2,3},{3,2},{4,5},{5,4},{6,7},{7,6},{8,9},{9,8},{10,11... | collective-permute-start | bytes 829448 | tf_op jit(solution)/shard_map/ppermute | solution.py:28
  (37 other events, 469.6 us)

commit v4 on v3

--- a/solution.py
+++ b/solution.py
@@ -77,7 +77,7 @@
 GRANTS = {'pack': 12, 'attend': 5, 'down_back': 5, 'feed': 9, 'narrow': 4, 'back': 18, 'wide': 8, 'merge': 5, 'finish': 4, 'lay': 24, 'close': 6, 'ydown': 4, 'open': 3, 'yout': 4, 'pick': 4, 'stack': 8}
 
 
-def call(kernel, name, outs, where, args, scratch=(), flops=0, space=pltpu.VMEM):
+def call(kernel, name, outs, where, args, scratch=(), flops=0, space=pltpu.VMEM, steps=1):
     grant = GRANTS[name]
     total = sum(a.size * a.dtype.itemsize for a in args)
     total += sum(o.size * jnp.dtype(o.dtype).itemsize for o in outs)
@@ -86,7 +86,10 @@
         kernel,
         out_shape=outs,
         in_specs=[pl.BlockSpec(memory_space=pltpu.SMEM)] + [pl.BlockSpec(memory_space=space)] * len(args),
-        out_specs=[vmem] * len(outs),
+        out_specs=[vmem] * len(outs) if steps == 1 else [
+            pl.BlockSpec((o.shape[0] // steps, o.shape[1]), lambda i: (i, 0)) for o in outs
+        ],
+        grid=() if steps == 1 else (steps,),
         scratch_shapes=list(scratch),
         cost_estimate=pl.CostEstimate(flops=flops, bytes_accessed=total, transcendentals=0),
         compiler_params=pltpu.CompilerParams(vmem_limit_bytes=grant << 20),
@@ -482,32 +485,34 @@
     rows, slab = stage.shape[1] // 2, stage.shape[2]
     whole, rest, fold, part, blocks, tall = dense_plan(rows, slab)
     s, c = where[0], where[1]
-    for k, source in enumerate((*mine, *other)):
-        for m in range(2):
-            base = m * tall
-            for b in range(whole):
-                lanes = slice(b * LANES, (b + 1) * LANES)
-                stage[k, m * rows : (m + 1) * rows, lanes] = source[base : base + rows].astype(F32)
-                base += rows
-            if rest:
-                folded = [
-                    source[base + b * part : base + (b + 1) * part].astype(F32)
-                    for b in range(blocks)
-                ]
-                folded = jnp.concatenate(folded, axis=1) if blocks > 1 else folded[0]
-                for i in range(fold):
-                    at = slice(m * rows + i * part, m * rows + (i + 1) * part)
-                    stage[k, at, whole * LANES :] = folded[:, i * rest : (i + 1) * rest]
-    step = rows // 4 if rows % 32 == 0 else rows
-
-    @pl.loop(0, rows // step)
-    def _(i):
-        top = pl.multiple_of(i * step, 8)
-        for j in range(2 * shards):
-            at = ((j // 2) ^ s) + jnp.where(c == j % 2, 0, shards)
-            lanes = slice(j * slab, (j + 1) * slab)
-            gate_ref[pl.ds(top, step), lanes] = stage[at, pl.ds(top, step)]
-            up_ref[pl.ds(top, step), lanes] = stage[at, pl.ds(pl.multiple_of(top + rows, 8), step)]
+
+    @pl.when(pl.program_id(0) == 0)
+    def _():
+        for k, source in enumerate((*mine, *other)):
+            for m in range(2):
+                base = m * tall
+                for b in range(whole):
+                    here = slice(m * rows, (m + 1) * rows)
+                    lanes = slice(b * LANES, (b + 1) * LANES)
+                    stage[k, here, lanes] = source[base : base + rows].astype(F32)
+                    base += rows
+                if rest:
+                    folded = [
+                        source[base + b * part : base + (b + 1) * part].astype(F32)
+                        for b in range(blocks)
+                    ]
+                    folded = jnp.concatenate(folded, axis=1) if blocks > 1 else folded[0]
+                    for i in range(fold):
+                        at = slice(m * rows + i * part, m * rows + (i + 1) * part)
+                        stage[k, at, whole * LANES :] = folded[:, i * rest : (i + 1) * rest]
+
+    step = gate_ref.shape[0]
+    top = pl.multiple_of(pl.program_id(0) * step, 8)
+    for j in range(2 * shards):
+        at = ((j // 2) ^ s) + jnp.where(c == j % 2, 0, shards)
+        lanes = slice(j * slab, (j + 1) * slab)
+        gate_ref[:, lanes] = stage[at, pl.ds(top, step)]
+        up_ref[:, lanes] = stage[at, pl.ds(pl.multiple_of(top + rows, 8), step)]
 
 
 def lay(where, mine, other, rows, slab):
@@ -516,6 +521,7 @@
     return call(
         functools.partial(lay_kernel, shards), "lay", outs, where, [*mine, *other],
         [pltpu.VMEM((2 * shards, 2 * rows, slab), F32)],
+        steps=4 if rows % 32 == 0 else 2,
     )
 
 

time: 297 us -> 296 us (level)
  no operation moved by 1% of the time
where the time goes in v4:
time: 296 us; the launch traced here: 295 us
  waiting for transfers between devices  142 us (48%)
  starting transfers between devices  93.4 us (32%)
  Pallas kernels  55.8 us (19%)
    ppermute x24, waiting for transfers between devices, hop(): return lax.ppermute(value, 'replica', links)  69.4 us
    ppermute x24, waiting for transfers between devices, shard_swap(): return lax.ppermute(x, 'shard', [(i, i ^ k) for i in range(n)])  63.1 us
    pallas_call x25, Pallas kernels, call(): pl.pallas_call(kernel, out_shape=outs, in_specs=[pl.BlockSpec(memory_spac...  55.8 us
    ppermute x24, starting transfers between devices, hop(): return lax.ppermute(value, 'replica', links)  49.1 us
    ppermute x24, starting transfers between devices, shard_swap(): return lax.ppermute(x, 'shard', [(i, i ^ k) for i in range(n)])  32.6 us
    ppermute x6, waiting for transfers between devices, pair_swap(): return lax.ppermute(x, 'replica', [(i, i ^ 2) for i in range(n)])  9.67 us
    ppermute x6, starting transfers between devices, pair_swap(): return lax.ppermute(x, 'replica', [(i, i ^ 2) for i in range(n)])  7.2 us
  transfers between devices with their start and end apart: 79, of which 29 were waited for; matrix products, arithmetic and copies ran while one was open for 1% of the time, Pallas kernels for 15%

profile of v4, /device:TPU:0, one launch (start us, length us, event | category | flops | bytes accessed | tf_op | source)
XLA Modules:
  0.0 294.9 jit_solution(10996201676988191544)
XLA Ops:
  1.2 3.5 %collective-permute-start.14 = (bf16[128,896]{1,0:T(8,128)(2,1)}, bf16[128,896]{1,0:T(8,128)(2,1)S(1)}, u32[]{:S(2)}, u32[]{:S(2)}) collective-permute-start(bf16[128,896]{1,0:T(8,128)(2,1)} %rest_5_.1), channel_id=1, source_target_pairs={{0,24},{8,16},{16,8},{24,0},{1,25},{9,17},{17,9},{25,1},{2,26},{10... | collective-permute-start | bytes 688136 | tf_op jit(solution)/shard_map/ppermute | solution.py:33
  7.1 2.9 collective-permute-start.2
  11.4 2.0 collective-permute-start
  13.4 3.2 %shard_map.189 = (bf16[448,608]{1,0:T(8,128)(2,1)S(1)}, bf16[224,608]{1,0:T(8,128)(2,1)S(1)}, bf16[224,608]{1,0:T(8,128)(2,1)S(1)}, bf16[224,608]{1,0:T(8,128)(2,1)S(1)}) custom-call(s32[3]{0:T(128)S(1)} %pad_add_fusion.where, bf16[224,4864]{1,0:T(8,128)(2,1)} %gate.1, bf16[224,4864]{1,0:T(8,128)(2,1)} %up.1), custom_call_target="tpu_custom_call" | custom-call | bytes 5720064 | tf_op jit(solution)/shard_map/pallas_call | solution.py:85
  16.6 1.8 collective-permute-start.26
  19.2 2.5 collective-permute-done.2.rest_2_
  21.6 2.9 collective-permute-start.28
  24.6 2.1 collective-permute-done.1.rest_1_
  29.0 4.6 %collective-permute-done.26.rest_9_ = bf16[224,608]{1,0:T(8,128)(2,1)S(1)} collective-permute-done((bf16[224,608]{1,0:T(8,128)(2,1)S(1)}, bf16[224,608]{1,0:T(8,128)(2,1)S(1)}, u32[]{:S(2)}, u32[]{:S(2)}) %collective-permute-start.26) | collective-permute-done | bytes 272416 | tf_op jit(solution)/shard_map/ppermute | solution.py:33
  35.6 3.3 %collective-permute-done.28.rest_11_ = bf16[224,608]{1,0:T(8,128)(2,1)S(1)} collective-permute-done((bf16[224,608]{1,0:T(8,128)(2,1)S(1)}, bf16[224,608]{1,0:T(8,128)(2,1)S(1)}, u32[]{:S(2)}, u32[]{:S(2)}) %collective-permute-start.28) | collective-permute-done | bytes 272416 | tf_op jit(solution)/shard_map/ppermute | solution.py:33
  39.5 2.9 collective-permute-done.4.rest_4_
  42.4 3.3 %collective-permute-done.3.rest_3_ = bf16[8,120,128]{2,1,0:T(8,128)(2,1)S(1)} collective-permute-done((bf16[8,120,128]{2,1,0:T(8,128)(2,1)S(1)}, bf16[8,120,128]{2,1,0:T(8,128)(2,1)S(1)}, u32[]{:S(2)}, u32[]{:S(2)}) %collective-permute-start.3) | collective-permute-done | bytes 245792 | tf_op jit(solution)/shard_map/ppermute | solution.py:38
  48.9 5.2 %shard_map.187 = (bf16[128,896]{1,0:T(8,128)(2,1)S(1)}, bf16[128,896]{1,0:T(8,128)(2,1)S(1)}, bf16[128,128]{1,0:T(8,128)(2,1)S(1)}, bf16[128,128]{1,0:T(8,128)(2...) custom-call(s32[3]{0:T(128)S(1)} %pad_add_fusion.where, ...), custom_call_target="tpu_custom_call" | custom-call | flops 704643072 | bytes 10308096 | tf_op jit(solution)/shard_map/pallas_call | solution.py:85
  54.1 2.5 collective-permute-start.21
  59.2 3.4 %collective-permute-done.30.rest_13_ = bf16[224,608]{1,0:T(8,128)(2,1)S(1)} collective-permute-done((bf16[224,608]{1,0:T(8,128)(2,1)S(1)}, bf16[224,608]{1,0:T(8,128)(2,1)S(1)}, u32[]{:S(2)}, u32[]{:S(2)}) %collective-permute-start.30) | collective-permute-done | bytes 272416 | tf_op jit(solution)/shard_map/ppermute | solution.py:38
  63.6 3.8 %collective-permute-done.20.rest_2_ = bf16[128,896]{1,0:T(8,128)(2,1)S(1)} collective-permute-done((bf16[128,896]{1,0:T(8,128)(2,1)S(1)}, bf16[128,896]{1,0:T(8,128)(2,1)S(1)}, u32[]{:S(2)}, u32[]{:S(2)}) %collective-permute-start.20) | collective-permute-done | bytes 229408 | tf_op jit(solution)/shard_map/ppermute | solution.py:33
  67.8 2.8 shard_map.188
  70.7 6.5 %shard_map.190 = (bf16[304,896]{1,0:T(8,128)(2,1)S(1)}, bf16[304,896]{1,0:T(8,128)(2,1)S(1)}, bf16[1024,608]{1,0:T(8,128)(2,1)S(1)}, bf16[1024,608]{1,0:T(8,128)...) custom-call(s32[3]{0:T(128)S(1)} %pad_add_fusion.where, ...), custom_call_target="tpu_custom_call" | custom-call | flops 3347054592 | bytes 17178624 | tf_op jit(solution)/shard_map/pallas_call | solution.py:85
  77.1 3.9 %shard_map.194 = (f32[512,896]{1,0:T(8,128)S(1)}, bf16[512,896]{1,0:T(8,128)(2,1)S(1)}) custom-call(s32[3]{0:T(128)S(1)} %pad_add_fusion.where, bf16[1024,608]{1,0:T(8,128)(2,1)S(1)} %get-tuple-element.88.dgate, bf16[1024,608]{1,0:T(8,128)(2,1)S(1)} %get-tuple-element.89.dup, bf16[896,608]{1,0:T(8,128)(2,1)S(1)} %get-tuple-element.90.wg, ...), custom_call_target="tpu_custom_call" | custom-call | flops 2231369728 | bytes 7421952 | tf_op jit(solution)/shard_map/pallas_call | solution.py:85
  81.2 3.1 %collective-permute-start.71 = (bf16[304,896]{1,0:T(8,128)(2,1)S(1)}, bf16[304,896]{1,0:T(8,128)(2,1)S(1)}, u32[]{:S(2)}, u32[]{:S(2)}) collective-permute-start(bf16[304,896]{1,0:T(8,128)(2,1)S(1)} %get-tuple-element.130), channel_id=1, source_target_pairs={{0,2},{1,3},{6,4},{7,5},{8,10},{9,11},{14,12},{15,13},{16,18},{17,... | collective-permute-start | bytes 1634312 | tf_op jit(solution)/shard_map/ppermute | solution.py:51
  88.6 2.4 collective-permute-start.74
  91.0 3.8 %shard_map.202 = (bf16[2128,128]{1,0:T(8,128)(2,1)S(1)}, bf16[2128,128]{1,0:T(8,128)(2,1)S(1)}, bf16[2128,128]{1,0:T(8,128)(2,1)S(1)}, bf16[2128,128]{1,0:T(8,128)(2,1)S(1)}) custom-call(s32[3]{0:T(128)S(1)} %pad_add_fusion.where, bf16[1024,896]{1,0:T(8,128)(2,1)S(1)} %get-tuple-element.123.n, bf16[1024,608]{1,0:T(8,128)(2,1)S(1)} %get-tuple-element.88.dgate, ...), custom_call_target="tpu_custom_call" | custom-call | flops 2231369728 | bytes 6504448 | tf_op jit(solution)/shard_map/pallas_call | solution.py:85
  96.4 1.9 collective-permute-done.38.rest_2_
  99.4 7.1 %shard_map.196 = (f32[128,896]{1,0:T(8,128)}, f32[4,1864,128]{2,1,0:T(8,128)S(1)}, bf16[4,1864,128]{2,1,0:T(8,128)(2,1)S(1)}) custom-call(s32[3]{0:T(128)S(1)} %pad_add_fusion.where, f32[128,896]{1,0:T(8,128)S(1)} %get-tuple-element.94.rest_0_, bf16[128,896]{1,0:T(8,128)(2,1)S(1)} %collective-permute-done.37.rest_1_, ...), custom_call_target="tpu_custom_call" | custom-call | flops 939524096 | bytes 13758464 | tf_op jit(solution)/shard_map/pallas_call | solution.py:85
  108.7 2.3 shard_map.191
  111.1 2.4 collective-permute-start.52
  113.7 19.3 %collective-permute-done.59 = bf16[2128,128]{1,0:T(8,128)(2,1)S(1)} collective-permute-done((bf16[2128,128]{1,0:T(8,128)(2,1)S(1)}, bf16[2128,128]{1,0:T(8,128)(2,1)S(1)}, u32[]{:S(2)}, u32[]{:S(2)}) %collective-permute-start.59) | collective-permute-done | bytes 544800 | tf_op jit(solution)/shard_map/ppermute | solution.py:33
  133.6 5.6 %collective-permute-start.56 = (bf16[2128,128]{1,0:T(8,128)(2,1)S(1)}, bf16[2128,128]{1,0:T(8,128)(2,1)S(1)}, u32[]{:S(2)}, u32[]{:S(2)}) collective-permute-start(bf16[2128,128]{1,0:T(8,128)(2,1)S(1)} %collective-permute-done.55), channel_id=1, source_target_pairs={{0,2},{1,3},{6,4},{7,5},{8,10},{9,11},{14,12},{15,13},{16,18},{17,... | collective-permute-start | bytes 1634312 | tf_op jit(solution)/shard_map/ppermute | solution.py:51
  140.1 2.6 collective-permute-start.60
  142.7 9.8 %collective-permute-start.64 = (bf16[2128,128]{1,0:T(8,128)(2,1)S(1)}, bf16[2128,128]{1,0:T(8,128)(2,1)S(1)}, u32[]{:S(2)}, u32[]{:S(2)}) collective-permute-start(bf16[2128,128]{1,0:T(8,128)(2,1)S(1)} %collective-permute-done.63), channel_id=1, source_target_pairs={{0,2},{1,3},{6,4},{7,5},{8,10},{9,11},{14,12},{15,13},{16,18},{17,... | collective-permute-start | bytes 1634312 | tf_op jit(solution)/shard_map/ppermute | solution.py:51
  154.9 8.7 %collective-permute-done.60 = bf16[2128,128]{1,0:T(8,128)(2,1)S(1)} collective-permute-done((bf16[2128,128]{1,0:T(8,128)(2,1)S(1)}, bf16[2128,128]{1,0:T(8,128)(2,1)S(1)}, u32[]{:S(2)}, u32[]{:S(2)}) %collective-permute-start.60) | collective-permute-done | bytes 544800 | tf_op jit(solution)/shard_map/ppermute | solution.py:51
  164.5 9.2 %collective-permute-done.64 = bf16[2128,128]{1,0:T(8,128)(2,1)S(1)} collective-permute-done((bf16[2128,128]{1,0:T(8,128)(2,1)S(1)}, bf16[2128,128]{1,0:T(8,128)(2,1)S(1)}, u32[]{:S(2)}, u32[]{:S(2)}) %collective-permute-start.64) | collective-permute-done | bytes 544800 | tf_op jit(solution)/shard_map/ppermute | solution.py:51
  175.0 1.7 collective-permute-start.35
  179.1 6.3 %collective-permute-done.34.rest_2_ = bf16[128,896]{1,0:T(8,128)(2,1)S(1)} collective-permute-done((bf16[128,896]{1,0:T(8,128)(2,1)S(1)}, bf16[128,896]{1,0:T(8,128)(2,1)S(1)}, u32[]{:S(2)}, u32[]{:S(2)}) %collective-permute-start.34) | collective-permute-done | bytes 229408 | tf_op jit(solution)/shard_map/ppermute | solution.py:33
  185.9 1.7 collective-permute-start.43
  190.0 4.7 %collective-permute-done.41.rest_0_ = bf16[1864,128]{1,0:T(8,128)(2,1)S(1)} collective-permute-done((bf16[1864,128]{1,0:T(8,128)(2,1)S(1)}, bf16[1864,128]{1,0:T(8,128)(2,1)S(1)}, u32[]{:S(2)}, u32[]{:S(2)}) %collective-permute-start.41) | collective-permute-done | bytes 477216 | tf_op jit(solution)/shard_map/ppermute | solution.py:33
  196.2 10.9 %collective-permute-done.42.rest_1_ = bf16[1864,128]{1,0:T(8,128)(2,1)S(1)} collective-permute-done((bf16[1864,128]{1,0:T(8,128)(2,1)S(1)}, bf16[1864,128]{1,0:T(8,128)(2,1)S(1)}, u32[]{:S(2)}, u32[]{:S(2)}) %collective-permute-start.42) | collective-permute-done | bytes 477216 | tf_op jit(solution)/shard_map/ppermute | solution.py:33
  210.7 5.8 %collective-permute-start.44 = (bf16[1080,128]{1,0:T(8,128)(2,1)S(1)}, bf16[1080,128]{1,0:T(8,128)(2,1)S(1)}, u32[]{:S(2)}, u32[]{:S(2)}) collective-permute-start(bf16[1080,128]{1,0:T(8,128)(2,1)S(1)} %get-tuple-element.116), channel_id=1, source_target_pairs={{0,2},{1,3},{6,4},{7,5},{8,10},{9,11},{14,12},{15,13},{16,18},{17,... | collective-permute-start | bytes 829448 | tf_op jit(solution)/shard_map/ppermute | solution.py:51
  218.1 2.4 collective-permute-done.44
  225.3 9.8 %collective-permute-done.54.arrived = bf16[2128,128]{1,0:T(8,128)(2,1)S(1)} collective-permute-done((bf16[2128,128]{1,0:T(8,128)(2,1)S(1)}, bf16[2128,128]{1,0:T(8,128)(2,1)S(1)}, u32[]{:S(2)}, u32[]{:S(2)}) %collective-permute-start.54) | collective-permute-done | bytes 544800 | tf_op jit(solution)/shard_map/ppermute | solution.py:51
  235.1 11.7 %collective-permute-done.58.arrived = bf16[2128,128]{1,0:T(8,128)(2,1)S(1)} collective-permute-done((bf16[2128,128]{1,0:T(8,128)(2,1)S(1)}, bf16[2128,128]{1,0:T(8,128)(2,1)S(1)}, u32[]{:S(2)}, u32[]{:S(2)}) %collective-permute-start.58) | collective-permute-done | bytes 544800 | tf_op jit(solution)/shard_map/ppermute | solution.py:51
  248.3 4.9 %collective-permute-done.47 = bf16[784,128]{1,0:T(8,128)(2,1)S(1)} collective-permute-done((bf16[784,128]{1,0:T(8,128)(2,1)S(1)}, bf16[784,128]{1,0:T(8,128)(2,1)S(1)}, u32[]{:S(2)}, u32[]{:S(2)}) %collective-permute-start.47) | collective-permute-done | bytes 200736 | tf_op jit(solution)/shard_map/ppermute | solution.py:51
  255.2 3.3 %collective-permute-done.62.arrived = bf16[2128,128]{1,0:T(8,128)(2,1)S(1)} collective-permute-done((bf16[2128,128]{1,0:T(8,128)(2,1)S(1)}, bf16[2128,128]{1,0:T(8,128)(2,1)S(1)}, u32[]{:S(2)}, u32[]{:S(2)}) %collective-permute-start.62) | collective-permute-done | bytes 544800 | tf_op jit(solution)/shard_map/ppermute | solution.py:51
  259.1 11.0 %collective-permute-done.66.arrived = bf16[2128,128]{1,0:T(8,128)(2,1)S(1)} collective-permute-done((bf16[2128,128]{1,0:T(8,128)(2,1)S(1)}, bf16[2128,128]{1,0:T(8,128)(2,1)S(1)}, u32[]{:S(2)}, u32[]{:S(2)}) %collective-permute-start.66) | collective-permute-done | bytes 544800 | tf_op jit(solution)/shard_map/ppermute | solution.py:51
  275.1 6.8 %collective-permute-done.49.arrived = bf16[784,128]{1,0:T(8,128)(2,1)S(1)} collective-permute-done((bf16[784,128]{1,0:T(8,128)(2,1)S(1)}, bf16[784,128]{1,0:T(8,128)(2,1)S(1)}, u32[]{:S(2)}, u32[]{:S(2)}) %collective-permute-start.49) | collective-permute-done | bytes 200736 | tf_op jit(solution)/shard_map/ppermute | solution.py:51
  284.5 2.9 shard_map.210
  287.4 5.7 %shard_map.207 = (f32[224,4864]{1,0:T(8,128)}, f32[224,4864]{1,0:T(8,128)}) custom-call(s32[3]{0:T(128)S(1)} %pad_add_fusion.where, bf16[2128,128]{1,0:T(8,128)(2,1)S(1)} %shard_map.203.rest_0_, bf16[2128,128]{1,0:T(8,128)(2,1)S(1)} %shard_map.204.rest_1_, bf16[2128,128]{1,0:T(8,128)(2,1)S(1)} %shard_map.205.rest_2_, ...), custom_call_target="tpu_custom_call" | custom-call | bytes 13074432 | tf_op jit(solution)/shard_map/pallas_call | solution.py:85
  293.1 1.8 shard_map.201
  (164 shorter events, 61.1 us)
Async XLA Ops:
  4.7 11.8 %collective-permute-start.13 = (bf16[128,896]{1,0:T(8,128)(2,1)}, bf16[128,896]{1,0:T(8,128)(2,1)S(1)}, u32[]{:S(2)}, u32[]{:S(2)}) collective-permute-start(bf16[128,896]{1,0:T(8,128)(2,1)} %rest_5_.1), channel_id=1, source_target_pairs={{0,16},{8,24},{16,0},{24,8},{1,17},{9,25},{17,1},{25,9},{2,18},{10... | collective-permute-start | bytes 688136 | tf_op jit(solution)/shard_map/ppermute | solution.py:33
  5.2 13.1 %collective-permute-start.12 = (bf16[128,896]{1,0:T(8,128)(2,1)}, bf16[128,896]{1,0:T(8,128)(2,1)S(1)}, u32[]{:S(2)}, u32[]{:S(2)}) collective-permute-start(bf16[128,896]{1,0:T(8,128)(2,1)} %rest_5_.1), channel_id=1, source_target_pairs={{0,8},{8,0},{16,24},{24,16},{1,9},{9,1},{17,25},{25,17},{2,10},{10... | collective-permute-start | bytes 688136 | tf_op jit(solution)/shard_map/ppermute | solution.py:33
  7.1 14.6 %collective-permute-start.2 = (bf16[8,120,128]{2,1,0:T(8,128)(2,1)S(1)}, bf16[8,120,128]{2,1,0:T(8,128)(2,1)S(1)}, u32[]{:S(2)}, u32[]{:S(2)}) collective-permute-start(bf16[8,120,128]{2,1,0:T(8,128)(2,1)S(1)} %get-tuple-element.72), channel_id=1, source_target_pairs={{0,24},{8,16},{16,8},{24,0},{1,25},{9,17},{17,9},{25,1},{2,26},{10... | collective-permute-start | bytes 737288 | tf_op jit(solution)/shard_map/ppermute | solution.py:33
  10.0 16.7 %collective-permute-start.1 = (bf16[8,120,128]{2,1,0:T(8,128)(2,1)S(1)}, bf16[8,120,128]{2,1,0:T(8,128)(2,1)S(1)}, u32[]{:S(2)}, u32[]{:S(2)}) collective-permute-start(bf16[8,120,128]{2,1,0:T(8,128)(2,1)S(1)} %get-tuple-element.72), channel_id=1, source_target_pairs={{0,16},{8,24},{16,0},{24,8},{1,17},{9,25},{17,1},{25,9},{2,18},{10... | collective-permute-start | bytes 737288 | tf_op jit(solution)/shard_map/ppermute | solution.py:33
  11.4 16.0 %collective-permute-start = (bf16[8,120,128]{2,1,0:T(8,128)(2,1)S(1)}, bf16[8,120,128]{2,1,0:T(8,128)(2,1)S(1)}, u32[]{:S(2)}, u32[]{:S(2)}) collective-permute-start(bf16[8,120,128]{2,1,0:T(8,128)(2,1)S(1)} %get-tuple-element.72), channel_id=1, source_target_pairs={{0,8},{8,0},{16,24},{24,16},{1,9},{9,1},{17,25},{25,17},{2,10},{10... | collective-permute-start | bytes 737288 | tf_op jit(solution)/shard_map/ppermute | solution.py:33
  16.6 17.0 %collective-permute-start.26 = (bf16[224,608]{1,0:T(8,128)(2,1)S(1)}, bf16[224,608]{1,0:T(8,128)(2,1)S(1)}, u32[]{:S(2)}, u32[]{:S(2)}) collective-permute-start(bf16[224,608]{1,0:T(8,128)(2,1)S(1)} %get-tuple-element.78), channel_id=1, source_target_pairs={{0,8},{8,0},{16,24},{24,16},{1,9},{9,1},{17,25},{25,17},{2,10},{10... | collective-permute-start | bytes 817160 | tf_op jit(solution)/shard_map/ppermute | solution.py:33
  18.3 16.8 %collective-permute-start.27 = (bf16[224,608]{1,0:T(8,128)(2,1)S(1)}, bf16[224,608]{1,0:T(8,128)(2,1)S(1)}, u32[]{:S(2)}, u32[]{:S(2)}) collective-permute-start(bf16[224,608]{1,0:T(8,128)(2,1)S(1)} %get-tuple-element.79), channel_id=1, source_target_pairs={{0,16},{8,24},{16,0},{24,8},{1,17},{9,25},{17,1},{25,9},{2,18},{10... | collective-permute-start | bytes 817160 | tf_op jit(solution)/shard_map/ppermute | solution.py:33
  21.6 17.3 %collective-permute-start.28 = (bf16[224,608]{1,0:T(8,128)(2,1)S(1)}, bf16[224,608]{1,0:T(8,128)(2,1)S(1)}, u32[]{:S(2)}, u32[]{:S(2)}) collective-permute-start(bf16[224,608]{1,0:T(8,128)(2,1)S(1)} %get-tuple-element.80), channel_id=1, source_target_pairs={{0,24},{8,16},{16,8},{24,0},{1,25},{9,17},{17,9},{25,1},{2,26},{10... | collective-permute-start | bytes 817160 | tf_op jit(solution)/shard_map/ppermute | solution.py:33
  26.6 12.3 %collective-permute-start.8 = (bf16[8,120,128]{2,1,0:T(8,128)(2,1)S(1)}, bf16[8,120,128]{2,1,0:T(8,128)(2,1)S(1)}, u32[]{:S(2)}, u32[]{:S(2)}) collective-permute-start(bf16[8,120,128]{2,1,0:T(8,128)(2,1)S(1)} %collective-permute-done.2.rest_2_), channel_id=1, source_target_pairs={{0,1},{1,0},{2,3},{3,2},{4,5},{5,4},{6,7},{7,6},{8,9},{9,8},{10,11... | collective-permute-start | bytes 737288 | tf_op jit(solution)/shard_map/ppermute | solution.py:28
  27.4 12.0 %collective-permute-start.5 = (bf16[8,120,128]{2,1,0:T(8,128)(2,1)S(1)}, bf16[8,120,128]{2,1,0:T(8,128)(2,1)S(1)}, u32[]{:S(2)}, u32[]{:S(2)}) collective-permute-start(bf16[8,120,128]{2,1,0:T(8,128)(2,1)S(1)} %collective-permute-done.2.rest_2_), channel_id=1, source_target_pairs={{0,2},{1,3},{2,0},{3,1},{4,6},{5,7},{6,4},{7,5},{8,10},{9,11},{10,... | collective-permute-start | bytes 737288 | tf_op jit(solution)/shard_map/ppermute | solution.py:38
  48.4 14.3 %collective-permute-start.30 = (bf16[224,608]{1,0:T(8,128)(2,1)S(1)}, bf16[224,608]{1,0:T(8,128)(2,1)S(1)}, u32[]{:S(2)}, u32[]{:S(2)}) collective-permute-start(bf16[224,608]{1,0:T(8,128)(2,1)S(1)} %collective-permute-done.27.rest_10_), channel_id=1, source_target_pairs={{0,2},{1,3},{2,0},{3,1},{4,6},{5,7},{6,4},{7,5},{8,10},{9,11},{10,... | collective-permute-start | bytes 817160 | tf_op jit(solution)/shard_map/ppermute | solution.py:38
  57.6 13.0 %collective-permute-start.31 = (bf16[224,608]{1,0:T(8,128)(2,1)S(1)}, bf16[224,608]{1,0:T(8,128)(2,1)S(1)}, u32[]{:S(2)}, u32[]{:S(2)}) collective-permute-start(bf16[224,608]{1,0:T(8,128)(2,1)S(1)} %collective-permute-done.28.rest_11_), channel_id=1, source_target_pairs={{0,2},{1,3},{2,0},{3,1},{4,6},{5,7},{6,4},{7,5},{8,10},{9,11},{10,... | collective-permute-start | bytes 817160 | tf_op jit(solution)/shard_map/ppermute | solution.py:38
  81.2 25.9 %collective-permute-start.71 = (bf16[304,896]{1,0:T(8,128)(2,1)S(1)}, bf16[304,896]{1,0:T(8,128)(2,1)S(1)}, u32[]{:S(2)}, u32[]{:S(2)}) collective-permute-start(bf16[304,896]{1,0:T(8,128)(2,1)S(1)} %get-tuple-element.130), channel_id=1, source_target_pairs={{0,2},{1,3},{6,4},{7,5},{8,10},{9,11},{14,12},{15,13},{16,18},{17,... | collective-permute-start | bytes 1634312 | tf_op jit(solution)/shard_map/ppermute | solution.py:51
  87.4 12.1 %collective-permute-start.39 = (bf16[128,896]{1,0:T(8,128)(2,1)S(1)}, bf16[128,896]{1,0:T(8,128)(2,1)S(1)}, u32[]{:S(2)}, u32[]{:S(2)}) collective-permute-start(bf16[128,896]{1,0:T(8,128)(2,1)S(1)} %get-tuple-element.97), channel_id=1, source_target_pairs={{0,24},{8,16},{16,8},{24,0},{1,25},{9,17},{17,9},{25,1},{2,26},{10... | collective-permute-start | bytes 688136 | tf_op jit(solution)/shard_map/ppermute | solution.py:33
  88.6 22.4 %collective-permute-start.74 = (bf16[304,896]{1,0:T(8,128)(2,1)S(1)}, bf16[304,896]{1,0:T(8,128)(2,1)S(1)}, u32[]{:S(2)}, u32[]{:S(2)}) collective-permute-start(bf16[304,896]{1,0:T(8,128)(2,1)S(1)} %get-tuple-element.131), channel_id=1, source_target_pairs={{0,2},{1,3},{6,4},{7,5},{8,10},{9,11},{14,12},{15,13},{16,18},{17,... | collective-permute-start | bytes 1634312 | tf_op jit(solution)/shard_map/ppermute | solution.py:51
  94.8 16.3 %collective-permute-start.55 = (bf16[2128,128]{1,0:T(8,128)(2,1)S(1)}, bf16[2128,128]{1,0:T(8,128)(2,1)S(1)}, u32[]{:S(2)}, u32[]{:S(2)}) collective-permute-start(bf16[2128,128]{1,0:T(8,128)(2,1)S(1)} %get-tuple-element.125), channel_id=1, source_target_pairs={{0,8},{8,0},{16,24},{24,16},{1,9},{9,1},{17,25},{25,17},{2,10},{10... | collective-permute-start | bytes 1634312 | tf_op jit(solution)/shard_map/ppermute | solution.py:33
  106.5 68.5 %collective-permute-start.40 = (bf16[4,1864,128]{2,1,0:T(8,128)(2,1)S(1)}, bf16[4,1864,128]{2,1,0:T(8,128)(2,1)S(1)}, u32[]{:S(2)}, u32[]{:S(2)}) collective-permute-start(bf16[4,1864,128]{2,1,0:T(8,128)(2,1)S(1)} %get-tuple-element.111), channel_id=1, source_target_pairs={{0,1},{1,0},{2,3},{3,2},{4,5},{5,4},{6,7},{7,6},{8,9},{9,8},{10,11... | collective-permute-start | bytes 5726216 | tf_op jit(solution)/shard_map/ppermute | solution.py:28
  106.5 26.4 %collective-permute-start.59 = (bf16[2128,128]{1,0:T(8,128)(2,1)S(1)}, bf16[2128,128]{1,0:T(8,128)(2,1)S(1)}, u32[]{:S(2)}, u32[]{:S(2)}) collective-permute-start(bf16[2128,128]{1,0:T(8,128)(2,1)S(1)} %get-tuple-element.126), channel_id=1, source_target_pairs={{0,16},{8,24},{16,0},{24,8},{1,17},{9,25},{17,1},{25,9},{2,18},{10... | collective-permute-start | bytes 1634312 | tf_op jit(solution)/shard_map/ppermute | solution.py:33
  107.1 26.6 %collective-permute-start.63 = (bf16[2128,128]{1,0:T(8,128)(2,1)S(1)}, bf16[2128,128]{1,0:T(8,128)(2,1)S(1)}, u32[]{:S(2)}, u32[]{:S(2)}) collective-permute-start(bf16[2128,128]{1,0:T(8,128)(2,1)S(1)} %get-tuple-element.127), channel_id=1, source_target_pairs={{0,24},{8,16},{16,8},{24,0},{1,25},{9,17},{17,9},{25,1},{2,26},{10... | collective-permute-start | bytes 1634312 | tf_op jit(solution)/shard_map/ppermute | solution.py:33
  111.0 29.1 %collective-permute-start.32 = (bf16[512,896]{1,0:T(8,128)(2,1)S(1)}, bf16[512,896]{1,0:T(8,128)(2,1)S(1)}, u32[]{:S(2)}, u32[]{:S(2)}) collective-permute-start(bf16[512,896]{1,0:T(8,128)(2,1)S(1)} %get-tuple-element.83), channel_id=1, source_target_pairs={{0,1},{1,0},{2,3},{3,2},{4,5},{5,4},{6,7},{7,6},{8,9},{9,8},{10,11... | collective-permute-start | bytes 2752520 | tf_op jit(solution)/shard_map/ppermute | solution.py:28
  111.1 28.3 %collective-permute-start.52 = (bf16[2128,128]{1,0:T(8,128)(2,1)S(1)}, bf16[2128,128]{1,0:T(8,128)(2,1)S(1)}, u32[]{:S(2)}, u32[]{:S(2)}) collective-permute-start(bf16[2128,128]{1,0:T(8,128)(2,1)S(1)} %get-tuple-element.124), channel_id=1, source_target_pairs={{0,2},{1,3},{6,4},{7,5},{8,10},{9,11},{14,12},{15,13},{16,18},{17,... | collective-permute-start | bytes 1634312 | tf_op jit(solution)/shard_map/ppermute | solution.py:51
  133.6 19.0 %collective-permute-start.56 = (bf16[2128,128]{1,0:T(8,128)(2,1)S(1)}, bf16[2128,128]{1,0:T(8,128)(2,1)S(1)}, u32[]{:S(2)}, u32[]{:S(2)}) collective-permute-start(bf16[2128,128]{1,0:T(8,128)(2,1)S(1)} %collective-permute-done.55), channel_id=1, source_target_pairs={{0,2},{1,3},{6,4},{7,5},{8,10},{9,11},{14,12},{15,13},{16,18},{17,... | collective-permute-start | bytes 1634312 | tf_op jit(solution)/shard_map/ppermute | solution.py:51
  139.4 14.1 %collective-permute-start.75 = (bf16[304,896]{1,0:T(8,128)(2,1)S(1)}, bf16[304,896]{1,0:T(8,128)(2,1)S(1)}, u32[]{:S(2)}, u32[]{:S(2)}) collective-permute-start(bf16[304,896]{1,0:T(8,128)(2,1)S(1)} %add.62), channel_id=1, source_target_pairs={{2,4},{3,5},{4,2},{5,3},{10,12},{11,13},{12,10},{13,11},{18,20},{1... | collective-permute-start | bytes 1634312 | tf_op jit(solution)/shard_map/ppermute | solution.py:51
  140.1 23.5 %collective-permute-start.60 = (bf16[2128,128]{1,0:T(8,128)(2,1)S(1)}, bf16[2128,128]{1,0:T(8,128)(2,1)S(1)}, u32[]{:S(2)}, u32[]{:S(2)}) collective-permute-start(bf16[2128,128]{1,0:T(8,128)(2,1)S(1)} %collective-permute-done.59), channel_id=1, source_target_pairs={{0,2},{1,3},{6,4},{7,5},{8,10},{9,11},{14,12},{15,13},{16,18},{17,... | collective-permute-start | bytes 1634312 | tf_op jit(solution)/shard_map/ppermute | solution.py:51
  142.7 31.0 %collective-permute-start.64 = (bf16[2128,128]{1,0:T(8,128)(2,1)S(1)}, bf16[2128,128]{1,0:T(8,128)(2,1)S(1)}, u32[]{:S(2)}, u32[]{:S(2)}) collective-permute-start(bf16[2128,128]{1,0:T(8,128)(2,1)S(1)} %collective-permute-done.63), channel_id=1, source_target_pairs={{0,2},{1,3},{6,4},{7,5},{8,10},{9,11},{14,12},{15,13},{16,18},{17,... | collective-permute-start | bytes 1634312 | tf_op jit(solution)/shard_map/ppermute | solution.py:51
  152.7 21.7 %collective-permute-start.53 = (bf16[2128,128]{1,0:T(8,128)(2,1)S(1)}, bf16[2128,128]{1,0:T(8,128)(2,1)S(1)}, u32[]{:S(2)}, u32[]{:S(2)}) collective-permute-start(bf16[2128,128]{1,0:T(8,128)(2,1)S(1)} %add.52), channel_id=1, source_target_pairs={{2,4},{3,5},{4,2},{5,3},{10,12},{11,13},{12,10},{13,11},{18,20},{1... | collective-permute-start | bytes 1634312 | tf_op jit(solution)/shard_map/ppermute | solution.py:51
  153.5 34.1 %collective-permute-start.57 = (bf16[2128,128]{1,0:T(8,128)(2,1)S(1)}, bf16[2128,128]{1,0:T(8,128)(2,1)S(1)}, u32[]{:S(2)}, u32[]{:S(2)}) collective-permute-start(bf16[2128,128]{1,0:T(8,128)(2,1)S(1)} %add.54), channel_id=1, source_target_pairs={{2,4},{3,5},{4,2},{5,3},{10,12},{11,13},{12,10},{13,11},{18,20},{1... | collective-permute-start | bytes 1634312 | tf_op jit(solution)/shard_map/ppermute | solution.py:51
  163.6 14.0 %collective-permute-start.33 = (bf16[128,896]{1,0:T(8,128)(2,1)S(1)}, bf16[128,896]{1,0:T(8,128)(2,1)S(1)}, u32[]{:S(2)}, u32[]{:S(2)}) collective-permute-start(bf16[128,896]{1,0:T(8,128)(2,1)S(1)} %get-tuple-element.85), channel_id=1, source_target_pairs={{0,8},{8,0},{16,24},{24,16},{1,9},{9,1},{17,25},{25,17},{2,10},{10... | collective-permute-start | bytes 688136 | tf_op jit(solution)/shard_map/ppermute | solution.py:33
  173.7 14.8 %collective-permute-start.61 = (bf16[2128,128]{1,0:T(8,128)(2,1)S(1)}, bf16[2128,128]{1,0:T(8,128)(2,1)S(1)}, u32[]{:S(2)}, u32[]{:S(2)}) collective-permute-start(bf16[2128,128]{1,0:T(8,128)(2,1)S(1)} %add.56), channel_id=1, source_target_pairs={{2,4},{3,5},{4,2},{5,3},{10,12},{11,13},{12,10},{13,11},{18,20},{1... | collective-permute-start | bytes 1634312 | tf_op jit(solution)/shard_map/ppermute | solution.py:51
  177.7 17.0 %collective-permute-start.41 = (bf16[1864,128]{1,0:T(8,128)(2,1)S(1)}, bf16[1864,128]{1,0:T(8,128)(2,1)S(1)}, u32[]{:S(2)}, u32[]{:S(2)}) collective-permute-start(bf16[1864,128]{1,0:T(8,128)(2,1)S(1)} %get-tuple-element.113), channel_id=1, source_target_pairs={{0,8},{8,0},{16,24},{24,16},{1,9},{9,1},{17,25},{25,17},{2,10},{10... | collective-permute-start | bytes 1431560 | tf_op jit(solution)/shard_map/ppermute | solution.py:33
  185.4 21.7 %collective-permute-start.42 = (bf16[1864,128]{1,0:T(8,128)(2,1)S(1)}, bf16[1864,128]{1,0:T(8,128)(2,1)S(1)}, u32[]{:S(2)}, u32[]{:S(2)}) collective-permute-start(bf16[1864,128]{1,0:T(8,128)(2,1)S(1)} %get-tuple-element.114), channel_id=1, source_target_pairs={{0,16},{8,24},{16,0},{24,8},{1,17},{9,25},{17,1},{25,9},{2,18},{10... | collective-permute-start | bytes 1431560 | tf_op jit(solution)/shard_map/ppermute | solution.py:33
  185.9 22.5 %collective-permute-start.43 = (bf16[1864,128]{1,0:T(8,128)(2,1)S(1)}, bf16[1864,128]{1,0:T(8,128)(2,1)S(1)}, u32[]{:S(2)}, u32[]{:S(2)}) collective-permute-start(bf16[1864,128]{1,0:T(8,128)(2,1)S(1)} %get-tuple-element.115), channel_id=1, source_target_pairs={{0,24},{8,16},{16,8},{24,0},{1,25},{9,17},{17,9},{25,1},{2,26},{10... | collective-permute-start | bytes 1431560 | tf_op jit(solution)/shard_map/ppermute | solution.py:33
  187.7 23.1 %collective-permute-start.65 = (bf16[2128,128]{1,0:T(8,128)(2,1)S(1)}, bf16[2128,128]{1,0:T(8,128)(2,1)S(1)}, u32[]{:S(2)}, u32[]{:S(2)}) collective-permute-start(bf16[2128,128]{1,0:T(8,128)(2,1)S(1)} %add.58), channel_id=1, source_target_pairs={{2,4},{3,5},{4,2},{5,3},{10,12},{11,13},{12,10},{13,11},{18,20},{1... | collective-permute-start | bytes 1634312 | tf_op jit(solution)/shard_map/ppermute | solution.py:51
  188.5 28.3 %collective-permute-start.73 = (bf16[304,896]{1,0:T(8,128)(2,1)S(1)}, bf16[304,896]{1,0:T(8,128)(2,1)S(1)}, u32[]{:S(2)}, u32[]{:S(2)}) collective-permute-start(bf16[304,896]{1,0:T(8,128)(2,1)S(1)} %add.61.total), channel_id=1, source_target_pairs={{2,0},{3,1},{4,6},{5,7},{10,8},{11,9},{12,14},{13,15},{18,16},{19,... | collective-permute-start | bytes 1634312 | tf_op jit(solution)/shard_map/ppermute | solution.py:51
  194.6 28.8 %collective-permute-start.76 = (bf16[304,896]{1,0:T(8,128)(2,1)S(1)}, bf16[304,896]{1,0:T(8,128)(2,1)S(1)}, u32[]{:S(2)}, u32[]{:S(2)}) collective-permute-start(bf16[304,896]{1,0:T(8,128)(2,1)S(1)} %add.63.total), channel_id=1, source_target_pairs={{2,0},{3,1},{4,6},{5,7},{10,8},{11,9},{12,14},{13,15},{18,16},{19,... | collective-permute-start | bytes 1634312 | tf_op jit(solution)/shard_map/ppermute | solution.py:51
  207.1 28.0 %collective-permute-start.54 = (bf16[2128,128]{1,0:T(8,128)(2,1)S(1)}, bf16[2128,128]{1,0:T(8,128)(2,1)S(1)}, u32[]{:S(2)}, u32[]{:S(2)}) collective-permute-start(bf16[2128,128]{1,0:T(8,128)(2,1)S(1)} %add.53.total), channel_id=1, source_target_pairs={{2,0},{3,1},{4,6},{5,7},{10,8},{11,9},{12,14},{13,15},{18,16},{19,... | collective-permute-start | bytes 1634312 | tf_op jit(solution)/shard_map/ppermute | solution.py:51
  208.4 38.3 %collective-permute-start.58 = (bf16[2128,128]{1,0:T(8,128)(2,1)S(1)}, bf16[2128,128]{1,0:T(8,128)(2,1)S(1)}, u32[]{:S(2)}, u32[]{:S(2)}) collective-permute-start(bf16[2128,128]{1,0:T(8,128)(2,1)S(1)} %add.55.total), channel_id=1, source_target_pairs={{2,0},{3,1},{4,6},{5,7},{10,8},{11,9},{12,14},{13,15},{18,16},{19,... | collective-permute-start | bytes 1634312 | tf_op jit(solution)/shard_map/ppermute | solution.py:51
  216.8 41.6 %collective-permute-start.62 = (bf16[2128,128]{1,0:T(8,128)(2,1)S(1)}, bf16[2128,128]{1,0:T(8,128)(2,1)S(1)}, u32[]{:S(2)}, u32[]{:S(2)}) collective-permute-start(bf16[2128,128]{1,0:T(8,128)(2,1)S(1)} %add.57.total), channel_id=1, source_target_pairs={{2,0},{3,1},{4,6},{5,7},{10,8},{11,9},{12,14},{13,15},{18,16},{19,... | collective-permute-start | bytes 1634312 | tf_op jit(solution)/shard_map/ppermute | solution.py:51
  220.5 49.6 %collective-permute-start.66 = (bf16[2128,128]{1,0:T(8,128)(2,1)S(1)}, bf16[2128,128]{1,0:T(8,128)(2,1)S(1)}, u32[]{:S(2)}, u32[]{:S(2)}) collective-permute-start(bf16[2128,128]{1,0:T(8,128)(2,1)S(1)} %add.59.total), channel_id=1, source_target_pairs={{2,0},{3,1},{4,6},{5,7},{10,8},{11,9},{12,14},{13,15},{18,16},{19,... | collective-permute-start | bytes 1634312 | tf_op jit(solution)/shard_map/ppermute | solution.py:51
  223.4 23.4 %collective-permute-start.45 = (bf16[1080,128]{1,0:T(8,128)(2,1)S(1)}, bf16[1080,128]{1,0:T(8,128)(2,1)S(1)}, u32[]{:S(2)}, u32[]{:S(2)}) collective-permute-start(bf16[1080,128]{1,0:T(8,128)(2,1)S(1)} %add.48), channel_id=1, source_target_pairs={{2,4},{3,5},{4,2},{5,3},{10,12},{11,13},{12,10},{13,11},{18,20},{1... | collective-permute-start | bytes 829448 | tf_op jit(solution)/shard_map/ppermute | solution.py:51
  235.1 36.8 %collective-permute-start.77 = (bf16[304,896]{1,0:T(8,128)(2,1)S(1)}, bf16[304,896]{1,0:T(8,128)(2,1)S(1)}, u32[]{:S(2)}, u32[]{:S(2)}) collective-permute-start(bf16[304,896]{1,0:T(8,128)(2,1)S(1)} %shard_map.208.rest_0_), channel_id=1, source_target_pairs={{0,1},{1,0},{2,3},{3,2},{4,5},{5,4},{6,7},{7,6},{8,9},{9,8},{10,11... | collective-permute-start | bytes 1634312 | tf_op jit(solution)/shard_map/ppermute | solution.py:28
  246.8 25.7 %collective-permute-start.78 = (bf16[304,896]{1,0:T(8,128)(2,1)S(1)}, bf16[304,896]{1,0:T(8,128)(2,1)S(1)}, u32[]{:S(2)}, u32[]{:S(2)}) collective-permute-start(bf16[304,896]{1,0:T(8,128)(2,1)S(1)} %shard_map.209.rest_1_), channel_id=1, source_target_pairs={{0,1},{1,0},{2,3},{3,2},{4,5},{5,4},{6,7},{7,6},{8,9},{9,8},{10,11... | collective-permute-start | bytes 1634312 | tf_op jit(solution)/shard_map/ppermute | solution.py:28
  253.2 20.0 %collective-permute-start.46 = (bf16[1080,128]{1,0:T(8,128)(2,1)S(1)}, bf16[1080,128]{1,0:T(8,128)(2,1)S(1)}, u32[]{:S(2)}, u32[]{:S(2)}) collective-permute-start(bf16[1080,128]{1,0:T(8,128)(2,1)S(1)} %add.49.total), channel_id=1, source_target_pairs={{2,0},{3,1},{4,6},{5,7},{10,8},{11,9},{12,14},{13,15},{18,16},{19,... | collective-permute-start | bytes 829448 | tf_op jit(solution)/shard_map/ppermute | solution.py:51
  258.4 14.1 %collective-permute-start.48 = (bf16[784,128]{1,0:T(8,128)(2,1)S(1)}, bf16[784,128]{1,0:T(8,128)(2,1)S(1)}, u32[]{:S(2)}, u32[]{:S(2)}) collective-permute-start(bf16[784,128]{1,0:T(8,128)(2,1)S(1)} %add.50), channel_id=1, source_target_pairs={{2,4},{3,5},{4,2},{5,3},{10,12},{11,13},{12,10},{13,11},{18,20},{1... | collective-permute-start | bytes 602120 | tf_op jit(solution)/shard_map/ppermute | solution.py:51
  270.1 12.4 %collective-permute-start.67 = (bf16[2128,128]{1,0:T(8,128)(2,1)S(1)}, bf16[2128,128]{1,0:T(8,128)(2,1)S(1)}, u32[]{:S(2)}, u32[]{:S(2)}) collective-permute-start(bf16[2128,128]{1,0:T(8,128)(2,1)S(1)} %shard_map.203.rest_0_), channel_id=1, source_target_pairs={{0,1},{1,0},{2,3},{3,2},{4,5},{5,4},{6,7},{7,6},{8,9},{9,8},{10,11... | collective-permute-start | bytes 1634312 | tf_op jit(solution)/shard_map/ppermute | solution.py:28
  271.9 15.5 %collective-permute-start.68 = (bf16[2128,128]{1,0:T(8,128)(2,1)S(1)}, bf16[2128,128]{1,0:T(8,128)(2,1)S(1)}, u32[]{:S(2)}, u32[]{:S(2)}) collective-permute-start(bf16[2128,128]{1,0:T(8,128)(2,1)S(1)} %shard_map.204.rest_1_), channel_id=1, source_target_pairs={{0,1},{1,0},{2,3},{3,2},{4,5},{5,4},{6,7},{7,6},{8,9},{9,8},{10,11... | collective-permute-start | bytes 1634312 | tf_op jit(solution)/shard_map/ppermute | solution.py:28
  272.5 14.9 %collective-permute-start.69 = (bf16[2128,128]{1,0:T(8,128)(2,1)S(1)}, bf16[2128,128]{1,0:T(8,128)(2,1)S(1)}, u32[]{:S(2)}, u32[]{:S(2)}) collective-permute-start(bf16[2128,128]{1,0:T(8,128)(2,1)S(1)} %shard_map.205.rest_2_), channel_id=1, source_target_pairs={{0,1},{1,0},{2,3},{3,2},{4,5},{5,4},{6,7},{7,6},{8,9},{9,8},{10,11... | collective-permute-start | bytes 1634312 | tf_op jit(solution)/shard_map/ppermute | solution.py:28
  272.6 14.8 %collective-permute-start.70 = (bf16[2128,128]{1,0:T(8,128)(2,1)S(1)}, bf16[2128,128]{1,0:T(8,128)(2,1)S(1)}, u32[]{:S(2)}, u32[]{:S(2)}) collective-permute-start(bf16[2128,128]{1,0:T(8,128)(2,1)S(1)} %shard_map.206.rest_3_), channel_id=1, source_target_pairs={{0,1},{1,0},{2,3},{3,2},{4,5},{5,4},{6,7},{7,6},{8,9},{9,8},{10,11... | collective-permute-start | bytes 1634312 | tf_op jit(solution)/shard_map/ppermute | solution.py:28
  (37 other events, 467.7 us)
